TPU v7x, 512 devices: a whole 4x8x8 slice. The times are simulated.
512 devices in a mesh: ctx: 32 (over z, x_hi, core), head: 16 (over y, x_lo).
Axes of the slice: x: 4 (x_hi: 2, x_lo: 2; x = x_hi * 2 + x_lo), y: 8, z: 8, core: 2. Of those that a mesh axis runs over, the one named last changes fastest.
Arguments:
- tokens: bfloat16 [131072, 1024], P(('ctx', 'head')), may hold values from -11 to 11
- ln_gain: float32 [1024], replicated, may hold values from 0.1 to 1.9
- ln_bias: float32 [1024], replicated, may hold values from -3 to 3
- qkv_weight: bfloat16 [1024, 16, 192], P(None, 'head'), may hold values from -7 to 7
- out_weight: bfloat16 [1024, 1024], P('head'), may hold values from -0.75 to 0.75
- output_bias_vector: float32 [1024], replicated, may hold values from -3 to 3
- lengths: int32 [1024], replicated, may hold values from 1 to 512, 131072 in all
- pairs_dev: int32 [1024, 3], replicated, may hold values from 0 to 31, all different within a row; in each aligned block of 32 rows (0 to 31, 32 to 63, ...) at most 4 rows name the same one
- pairs_off: int32 [1024, 3], replicated, may hold values from 0 to 31
Outputs:
- attended_out: bfloat16 [131072, 1024], P(('ctx', 'head'))
Inputs may be any that keep to these rules, and one draw needn't show every extreme that they name: The lengths sum to 131072. `pairs_dev`: each row names 3 different ctx indices; within the rows of one ctx index's 32 query blocks no ctx index is named more than 4 times.
All inputs are finite; a program needn't handle non-finite values.
Results may differ from a plain program's by a relative error of at most 0.0065.
The roundings to bfloat16 on the way count: a program that leaves them out, or rounds other values in their place, can miss the bound.
Values may be sent and summed in bfloat16 or wider, within the bound.
No kernel may reach another device: no remote copies, remote signals or barrier semaphores. Data moves between devices by JAX's collectives and lax.ppermute only.
A program may use at most 64 MiB of HBM per device.

v0:
```python
import math

import jax
import jax.numpy as jnp
from jax import lax
from jax.sharding import PartitionSpec as P

BLK = 128
RAND = 3


epsilon = 1e-05


def with_halo(cells, sides, width):
    for axis, dim in sides:
        count = lax.axis_size(axis)
        ends = count - 1
        head = lax.slice_in_dim(cells, 0, width, axis=dim)
        tail = lax.slice_in_dim(cells, cells.shape[dim] - width, cells.shape[dim], axis=dim)
        cells = jnp.concatenate(
            [
                lax.ppermute(tail, axis, [(i, (i + 1) % count) for i in range(ends)]),
                cells,
                lax.ppermute(head, axis, [((i + 1) % count, i) for i in range(ends)]),
            ],
            axis=dim,
        )
    return cells


def from_root(value, axis, source):
    kept = jnp.where(lax.axis_index(axis) == source, value, 0).astype(value.dtype)
    return lax.psum(kept, axis)


def normalize(tokens, ln_gain, ln_bias):
    values = tokens.astype(jnp.float32)
    center = values - jnp.mean(values, axis=-1, keepdims=True)
    spread = jnp.mean(center * center, axis=-1, keepdims=True)
    return (center * lax.rsqrt(spread + epsilon) * ln_gain + ln_bias).astype(jnp.bfloat16)


def owning_line(line_end, positions):
    span_rows = positions.shape[0]
    step_rows = math.gcd(span_rows, 512)
    blocked = positions.reshape(span_rows // step_rows, step_rows)

    def count_ends(block_pos):
        return jnp.sum((line_end[None, :] <= block_pos[:, None]).astype(jnp.int32), axis=1)

    return lax.map(count_ends, blocked).reshape(span_rows)


def attend(queries, window_rows, window_line, query_line, global_kv, random_kv, head_dim):
    group_size = queries.shape[0]
    block_rows = queries.shape[1]
    windows = jnp.stack(
        [
            window_rows[member * block_rows : (member + 3) * block_rows]
            for member in range(group_size)
        ]
    )
    window_ids = jnp.stack(
        [
            window_line[member * block_rows : (member + 3) * block_rows]
            for member in range(group_size)
        ]
    )
    global_rows = jnp.broadcast_to(global_kv[None], (group_size,) + global_kv.shape)
    key_rows = jnp.concatenate([windows, global_rows, random_kv], axis=1)
    key_part = key_rows[..., :head_dim]
    value_part = key_rows[..., head_dim:]
    scores = jnp.einsum(
        "gqhd,gkhd->ghqk", queries, key_part, preferred_element_type=jnp.float32
    ) * head_dim ** (-0.5)
    allowed_window = window_ids[:, None, :] == query_line[:, :, None]
    extra_keys = key_rows.shape[1] - 3 * block_rows
    allowed = jnp.concatenate(
        [allowed_window, jnp.ones((group_size, block_rows, extra_keys), dtype=bool)], axis=2
    )
    scores = jnp.where(allowed[:, None], scores, -jnp.inf)
    row_max = jnp.max(scores, axis=-1, keepdims=True)
    exp_scores = jnp.exp(scores - row_max)
    denominator = jnp.sum(exp_scores, axis=-1)
    rounded = exp_scores.astype(jnp.bfloat16)
    summed = jnp.einsum("ghqk,gkhd->gqhd", rounded, value_part, preferred_element_type=jnp.float32)
    return (summed / jnp.transpose(denominator, (0, 2, 1))[..., None]).astype(jnp.bfloat16)


def per_device(
    tokens,
    ln_gain,
    ln_bias,
    qkv_weight,
    out_weight,
    output_bias_vector,
    lengths,
    pairs_dev,
    pairs_off,
):
    ctx_count = lax.axis_size("ctx")
    ctx_index = lax.axis_index("ctx")
    normed = normalize(tokens, ln_gain, ln_bias)
    local_heads = qkv_weight.shape[1]
    head_dim = qkv_weight.shape[2] // 3
    every_head = jnp.einsum(
        "td,dhc->thc",
        normed,
        lax.all_gather(qkv_weight, "head", axis=1, tiled=True),
        preferred_element_type=jnp.float32,
    ).astype(jnp.bfloat16)
    projected_qkv = lax.all_to_all(every_head, "head", split_axis=1, concat_axis=0, tiled=True)
    ctx_rows = projected_qkv.shape[0]
    blocks_dev = ctx_rows // BLK
    q_blocks = projected_qkv[..., :head_dim].reshape(blocks_dev, BLK, local_heads, head_dim)
    kv_width = local_heads * 2 * head_dim
    flat_kv = projected_qkv[..., head_dim:].reshape(ctx_rows, kv_width)
    padded = with_halo(flat_kv, (("ctx", 0),), BLK)
    padded = padded.reshape(ctx_rows + 2 * BLK, local_heads, 2 * head_dim)
    global_kv = from_root(flat_kv[:BLK], "ctx", 0).reshape(BLK, local_heads, 2 * head_dim)
    pair_count = blocks_dev * RAND
    capacity = max(2, (pair_count * 4 + 3 * ctx_count - 1) // (3 * ctx_count))
    all_dev = pairs_dev.reshape(ctx_count, pair_count)
    all_off = pairs_off.reshape(ctx_count, pair_count)
    own_pairs = all_dev == ctx_index
    pair_order = jnp.arange(pair_count, dtype=jnp.int32)
    lower_tri = pair_order[None, :] < pair_order[:, None]
    slot_rank = jnp.sum((own_pairs[:, None, :] & lower_tri[None]).astype(jnp.int32), axis=2)
    slot_ids = jnp.arange(capacity, dtype=jnp.int32)
    selected_items = own_pairs[:, None, :] & (slot_rank[:, None, :] == slot_ids[None, :, None])
    block_ids = jnp.arange(blocks_dev, dtype=jnp.int32)
    shifted_popular = (all_off[:, :, None] == block_ids[None, None, :]).astype(jnp.bfloat16)
    send_hot = jnp.einsum(
        "utk,ukv->utv",
        selected_items.astype(jnp.bfloat16),
        shifted_popular,
        preferred_element_type=jnp.float32,
    )
    send_hot = send_hot.astype(jnp.bfloat16).reshape(ctx_count * capacity, blocks_dev)
    kv_blocks = flat_kv.reshape(blocks_dev, BLK * kv_width)
    outgoing = jnp.dot(send_hot, kv_blocks, preferred_element_type=jnp.float32).astype(jnp.bfloat16)
    outgoing = outgoing.reshape(ctx_count, capacity, BLK, kv_width)
    incoming = lax.all_to_all(outgoing, "ctx", split_axis=0, concat_axis=0, tiled=True).reshape(
        ctx_count * capacity, BLK * kv_width
    )
    own_dev = all_dev[ctx_index]
    earlier = (own_dev[:, None] == own_dev[None, :]) & lower_tri
    position = own_dev * capacity + jnp.sum(earlier.astype(jnp.int32), axis=1)
    slot_every_block = jnp.arange(ctx_count * capacity, dtype=jnp.int32)
    take_hot = (position[:, None] == slot_every_block[None, :]).astype(jnp.bfloat16)
    random_every_block = jnp.dot(take_hot, incoming, preferred_element_type=jnp.float32).astype(
        jnp.bfloat16
    )
    random_every_block = random_every_block.reshape(
        blocks_dev, RAND * BLK, local_heads, 2 * head_dim
    )
    line_end = jnp.cumsum(lengths)
    doc_tokens = ctx_count * ctx_rows
    positions = ctx_index * ctx_rows - BLK + jnp.arange(ctx_rows + 2 * BLK, dtype=jnp.int32)
    inside = (positions >= 0) & (positions < doc_tokens)
    ext_line = jnp.where(inside, owning_line(line_end, jnp.clip(positions, 0, doc_tokens - 1)), -1)
    group_size = math.gcd(blocks_dev, 4)

    def group_step(group_index):
        first_block = group_index * group_size
        window_rows = lax.dynamic_slice_in_dim(padded, first_block * BLK, (group_size + 2) * BLK, 0)
        window_line = lax.dynamic_slice_in_dim(
            ext_line, first_block * BLK, (group_size + 2) * BLK, 0
        )
        query_line = lax.dynamic_slice_in_dim(
            ext_line, (first_block + 1) * BLK, group_size * BLK, 0
        ).reshape(group_size, BLK)
        queries = lax.dynamic_slice_in_dim(q_blocks, first_block, group_size, 0)
        random_kv = lax.dynamic_slice_in_dim(random_every_block, first_block, group_size, 0)
        return attend(queries, window_rows, window_line, query_line, global_kv, random_kv, head_dim)

    attended = lax.map(group_step, jnp.arange(blocks_dev // group_size, dtype=jnp.int32))
    attended = attended.reshape(ctx_rows, local_heads * head_dim)
    rows_back = lax.all_to_all(attended, "head", split_axis=0, concat_axis=1, tiled=True)
    projected = jnp.dot(
        rows_back,
        lax.all_gather(out_weight, "head", axis=0, tiled=True),
        preferred_element_type=jnp.float32,
    )
    return (projected + output_bias_vector).astype(jnp.bfloat16)


def solution(mesh):
    in_specs = (
        P(("ctx", "head"), None),
        P(),
        P(),
        P(None, "head", None),
        P("head", None),
        P(),
        P(),
        P(),
        P(),
    )
    out_specs = P(("ctx", "head"), None)
    return jax.shard_map(
        per_device, mesh=mesh, in_specs=in_specs, out_specs=out_specs, check_vma=False
    )
```

profile of v0, /device:TPU:197, one launch (start us, length us, event | category | flops | bytes accessed | tf_op | source)
XLA Modules:
  0.0 548.6 jit_solution(13660856780126761549)
XLA Ops:
  6.5 0.7 all-gather.3.cloned.1.call-update
  7.3 1.2 convert_reduce_fusion.2
  8.5 1.3 fusion.13
  9.8 144.3 %all-gather.3.cloned.1.call-done = bf16[1024,16,192]{0,2,1:T(8,128)(2,1)} async-done(((bf16[1024,1,192]{0,2,1:T(8,128)(2,1)}), bf16[1024,16,192]{0,2,1:T(8,128)(2,1)}) %all-gather.3.cloned.1.call-update) | async-done | bytes 6291472 | tf_op jit(solution)/shard_map/all_gather | solution.py:110
  154.1 5.0 fusion.17
  159.1 1.4 convert_element_type.53
  160.5 7.6 %all-to-all-start = ((bf16[256,16,192]{0,2,1:T(8,128)(2,1)}), bf16[256,16,192]{0,2,1:T(8,128)(2,1)S(1)}, u32[]{:S(2)}, u32[]{:S(2)}) async-start(bf16[256,16,192]{0,2,1:T(8,128)(2,1)} %convert_element_type.53), calls=%async_computation | async-start | bytes 3145728 | tf_op jit(solution)/shard_map/all_to_all | solution.py:113
  169.1 0.6 convert_reduce_fusion.1
  170.0 34.0 %all-to-all-done = bf16[256,16,192]{0,2,1:T(8,128)(2,1)S(1)} async-done(((bf16[256,16,192]{0,2,1:T(8,128)(2,1)}), bf16[256,16,192]{0,2,1:T(8,128)(2,1)S(1)}, u32[]{:S(2)}, u32[]{:S(2)}) %all-to-all-start) | async-done | bytes 1572896 | tf_op jit(solution)/shard_map/all_to_all | solution.py:113
  204.2 1.3 fusion.35
  205.5 2.3 copy.42
  207.8 2.3 reshape_reshape.3
  210.1 2.4 fusion.9
  212.5 3.2 copy.52
  215.7 14.4 %all-to-all-start.1 = ((bf16[32,4,128,128]{3,2,1,0:T(8,128)(2,1)}), bf16[32,4,128,128]{3,2,1,0:T(8,128)(2,1)}, u32[]{:S(2)}, u32[]{:S(2)}) async-start(bf16[32,4,128,128]{3,2,1,0:T(8,128)(2,1)} %bitcast.131), calls=%async_computation.1 | async-start | bytes 8388608 | tf_op jit(solution)/shard_map/all_to_all | solution.py:144
  230.2 0.7 all-gather.5.cloned.1.call-update
  231.5 5.6 %while.24 = (s32[]{:T(128)}, s32[17,256]{1,0:T(8,128)S(1)}, s32[1024]{0:T(1024)S(1)}, s32[17,256]{1,0:T(8,128)S(1)}) while((s32[]{:T(128)}, s32[17,256]{1,0:T(8,128)S(1)}, s32[1024]{0:T(1024)S(1)}, s32[17,256]{1,0:T(8,128)S(1)}) %tuple.67), condition=%wide.region_6.7_spmd.clone, body=%wide.region_4.0_spmd.sunk.clone | while | flops 786178 | bytes 10301 | solution.py:52
  237.3 4.6 collective-permute-start
  241.9 1.9 collective-permute-start.1
  243.9 0.9 copy.54
  244.8 199.1 %psum.7 = bf16[128,128]{0,1:T(8,128)(2,1)S(1)} all-reduce(bf16[128,128]{0,1:T(8,128)(2,1)S(1)} %broadcast_select_fusion), channel_id=1, replica_groups=mesh['ctx'=32,'head'=16] {'ctx'}, use_global_device_ids=true, to_apply=%region_9.10 | all-reduce | flops 16384 | bytes 65536 | tf_op jit(solution)/shard_map/psum | solution.py:34
  443.9 1.1 maximum_bitcast_fusion
  445.0 5.1 convolution_convert_fusion.1
  450.1 3.4 reshape.152
  453.5 62.3 %while.25 = (s32[]{:T(128)}, bf16[8,4,128,1,64]{2,1,0,4,3:T(4,128)(2,1)}, s32[8]{0:T(128)S(1)}, bf16[4352,1,128]{0,2,1:T(8,128)(2,1)}, bf16[128,128]{0,1:T(8,128...) while((s32[]{:T(128)}, ...), condition=%wide.region_13.14_spmd.clone, body=%wide.region_10.13_spmd.sunk.clone | while | flops 126422544 | bytes 11633483 | solution.py:178
  454.6 1.1 dynamic-slice_bitcast_fusion.10
  456.3 1.0 constant_dynamic-slice_fusion.10
  458.1 0.9 constant_dynamic-slice_fusion.11
  460.6 0.7 copy_dynamic-update-slice_fusion.3
  462.4 1.1 dynamic-slice_bitcast_fusion.10
  464.1 1.0 constant_dynamic-slice_fusion.10
  465.9 0.9 constant_dynamic-slice_fusion.11
  467.8 0.6 fusion.55
  468.4 0.7 copy_dynamic-update-slice_fusion.3
  470.2 1.1 dynamic-slice_bitcast_fusion.10
  471.9 1.0 constant_dynamic-slice_fusion.10
  473.6 0.9 constant_dynamic-slice_fusion.11
  476.2 0.7 copy_dynamic-update-slice_fusion.3
  478.0 1.1 dynamic-slice_bitcast_fusion.10
  479.6 1.0 constant_dynamic-slice_fusion.10
  481.4 0.9 constant_dynamic-slice_fusion.11
  483.4 0.6 fusion.55
  484.0 0.7 copy_dynamic-update-slice_fusion.3
  485.8 1.1 dynamic-slice_bitcast_fusion.10
  487.4 1.0 constant_dynamic-slice_fusion.10
  489.2 0.9 constant_dynamic-slice_fusion.11
  491.8 0.7 copy_dynamic-update-slice_fusion.3
  493.5 1.1 dynamic-slice_bitcast_fusion.10
  495.2 1.0 constant_dynamic-slice_fusion.10
  497.0 0.9 constant_dynamic-slice_fusion.11
  499.5 0.7 copy_dynamic-update-slice_fusion.3
  501.3 1.1 dynamic-slice_bitcast_fusion.10
  503.0 1.0 constant_dynamic-slice_fusion.10
  504.8 0.9 constant_dynamic-slice_fusion.11
  507.3 0.7 copy_dynamic-update-slice_fusion.3
  509.1 1.1 dynamic-slice_bitcast_fusion.10
  510.8 1.0 constant_dynamic-slice_fusion.10
  512.6 0.9 constant_dynamic-slice_fusion.11
  515.1 0.7 copy_dynamic-update-slice_fusion.3
  515.8 1.4 all_to_all.35
  517.2 1.0 copy.46
  518.1 3.6 all-to-all-start.2
  521.7 16.8 %all-to-all-done.2 = bf16[16,256,64]{1,2,0:T(8,128)(2,1)S(1)} async-done(((bf16[16,256,64]{1,2,0:T(8,128)(2,1)}), bf16[16,256,64]{1,2,0:T(8,128)(2,1)S(1)}, u32[]{:S(2)}, u32[]{:S(2)}) %all-to-all-start.2) | async-done | bytes 524320 | tf_op jit(solution)/shard_map/all_to_all | solution.py:180
  538.6 3.1 fusion.10
  (218 shorter events, 28.9 us)
Async XLA Ops:
  6.5 147.5 %all-gather.3.cloned.1.call-start = ((), (), s32[]{:S(2)}) async-start(), calls=%async_computation.3 | async-start | bytes 6684672 | tf_op jit(solution)/shard_map/all_gather | solution.py:110
  160.5 7.6 %copy-start.1 = (s32[1024,3]{0,1:T(4,128)S(1)}, s32[1024,3]{0,1:T(4,128)}, u32[]{:S(2)}) copy-start(s32[1024,3]{0,1:T(4,128)} %param.20) | copy-start | bytes 36868
  160.5 8.1 %copy-start.2 = (s32[1024,3]{0,1:T(4,128)S(1)}, s32[1024,3]{0,1:T(4,128)}, u32[]{:S(2)}) copy-start(s32[1024,3]{0,1:T(4,128)} %param.21) | copy-start | bytes 36868
  160.5 43.5 %all-to-all-start = ((bf16[256,16,192]{0,2,1:T(8,128)(2,1)}), bf16[256,16,192]{0,2,1:T(8,128)(2,1)S(1)}, u32[]{:S(2)}, u32[]{:S(2)}) async-start(bf16[256,16,192]{0,2,1:T(8,128)(2,1)} %convert_element_type.53), calls=%async_computation | async-start | bytes 3145728 | tf_op jit(solution)/shard_map/all_to_all | solution.py:113
  215.7 15.2 %copy-start.3 = (s32[1024]{0:T(1024)S(1)}, s32[1024]{0:T(1024)}, u32[]{:S(2)}) copy-start(s32[1024]{0:T(1024)} %param.19) | copy-start | bytes 12292
  215.7 229.2 %all-to-all-start.1 = ((bf16[32,4,128,128]{3,2,1,0:T(8,128)(2,1)}), bf16[32,4,128,128]{3,2,1,0:T(8,128)(2,1)}, u32[]{:S(2)}, u32[]{:S(2)}) async-start(bf16[32,4,128,128]{3,2,1,0:T(8,128)(2,1)} %bitcast.131), calls=%async_computation.1 | async-start | bytes 8388608 | tf_op jit(solution)/shard_map/all_to_all | solution.py:144
  230.1 291.6 %all-gather.5.cloned.1.call-start = ((), (), s32[]{:S(2)}) async-start(), calls=%async_computation.4 | async-start | bytes 2228224 | tf_op jit(solution)/shard_map/all_gather | solution.py:183
  237.3 206.6 %collective-permute-start = (bf16[128,128]{0,1:T(8,128)(2,1)S(1)}, bf16[128,128]{0,1:T(8,128)(2,1)S(1)}, u32[]{:S(2)}, u32[]{:S(2)}) collective-permute-start(bf16[128,128]{0,1:T(8,128)(2,1)S(1)} %get-tuple-element.198), channel_id=1, source_target_pairs={{0,16},{16,32},{32,48},{48,64},{64,80},{80,96},{96,112},{112,128},... | collective-permute-start | bytes 98312 | tf_op jit(solution)/shard_map/ppermute | solution.py:23
  241.9 202.0 %collective-permute-start.1 = (bf16[128,128]{0,1:T(8,128)(2,1)S(1)}, bf16[128,128]{0,1:T(8,128)(2,1)S(1)}, u32[]{:S(2)}, u32[]{:S(2)}) collective-permute-start(bf16[128,128]{0,1:T(8,128)(2,1)S(1)} %get-tuple-element.199), channel_id=1, source_target_pairs={{16,0},{32,16},{48,32},{64,48},{80,64},{96,80},{112,96},{128,112},... | collective-permute-start | bytes 98312 | tf_op jit(solution)/shard_map/ppermute | solution.py:25
  515.8 22.8 %copy-start = (f32[1024]{0:T(1024)S(1)}, f32[1024]{0:T(1024)}, u32[]{:S(2)}) copy-start(f32[1024]{0:T(1024)} %param.18) | copy-start | bytes 12292
  518.1 20.5 %all-to-all-start.2 = ((bf16[16,256,64]{1,2,0:T(8,128)(2,1)}), bf16[16,256,64]{1,2,0:T(8,128)(2,1)S(1)}, u32[]{:S(2)}, u32[]{:S(2)}) async-start(bf16[16,256,64]{1,2,0:T(8,128)(2,1)} %copy.46), calls=%async_computation.2 | async-start | bytes 1048576 | tf_op jit(solution)/shard_map/all_to_all | solution.py:180
Sparse Core Ops, SparseCore 0:
  9.4 144.5 all-gather.2
  233.0 95.7 all-gather.4
where the time goes:
time: 550 us; the launch traced here: 549 us
  blocking collectives  199 us (36%)
  waiting for transfers between devices  197 us (36%)
  local copies, waits for them, and re-layouts  55.9 us (10%)
  starting transfers between devices  32.1 us (6%)
  matrix products  24.9 us (5%)
  other arithmetic  16.3 us (3%)
  between operations  13.7 us (2%)
  loops' own time  10 us (2%)
    psum x1, blocking collectives, from_root(): return lax.psum(kept, axis)  199 us
    all_gather x1, waiting for transfers between devices, per_device(): lax.all_gather(qkv_weight, 'head', axis=1, tiled=True)  144 us
    all_to_all x1, waiting for transfers between devices, per_device(): lax.all_to_all(every_head, 'head', split_axis=1, concat_axis=0, tiled=True)  34 us
    all_to_all x1, waiting for transfers between devices, per_device(): lax.all_to_all(attended, 'head', split_axis=0, concat_axis=1, tiled=True)  16.8 us
    all_to_all x1, starting transfers between devices, per_device(): lax.all_to_all(outgoing, 'ctx', split_axis=0, concat_axis=0, tiled=True)  14.4 us
  transfers between devices with their start and end apart: 7, of which 3 were waited for; matrix products, arithmetic and copies ran while one was open for 14% of the time, Pallas kernels for 0%

commit v1 on v0

v1 whole, which is shorter than its diff:
```python
import jax
import jax.numpy as jnp
from jax import lax
from jax.experimental import pallas as pl
from jax.experimental.pallas import tpu as pltpu
from jax.sharding import PartitionSpec as P

BLK = 128
RAND = 3
CAP = 4
EPS = 1e-05
NEG = float("-inf")


def ln_kernel(tok_ref, gain_ref, bias_ref, norm_ref, normt_ref):
    values = tok_ref[...].astype(jnp.float32)
    center = values - jnp.mean(values, axis=-1, keepdims=True)
    spread = jnp.mean(center * center, axis=-1, keepdims=True)
    normed = center * lax.rsqrt(spread + EPS) * gain_ref[...] + bias_ref[...]
    norm_ref[...] = normed.astype(jnp.bfloat16)
    normt_ref[...] = jnp.transpose(normed).astype(jnp.bfloat16).reshape(normt_ref.shape)


def layer_norm(tokens, gain, bias, heads):
    rows, width = tokens.shape
    return pl.pallas_call(
        ln_kernel,
        out_shape=(
            jax.ShapeDtypeStruct((rows, width), jnp.bfloat16),
            jax.ShapeDtypeStruct((heads, width // heads, rows), jnp.bfloat16),
        ),
        name="layer_norm",
    )(tokens, gain.reshape(1, width), bias.reshape(1, width))


def pick_kernel(ids_ref, cells_ref, out_ref):
    def step(slot, carry):
        block = ids_ref[slot]
        cols = pl.ds(pl.multiple_of((block % 2) * BLK, BLK), BLK)
        out_ref[slot] = cells_ref[block // 2, :, cols]
        return carry

    lax.fori_loop(0, out_ref.shape[0], step, 0, unroll=4)


def pick_blocks(ids, cells):
    return pl.pallas_call(
        pick_kernel,
        out_shape=jax.ShapeDtypeStruct((ids.shape[0], cells.shape[1], BLK), jnp.bfloat16),
        in_specs=[
            pl.BlockSpec(memory_space=pltpu.SMEM),
            pl.BlockSpec(memory_space=pltpu.VMEM),
        ],
        out_specs=pl.BlockSpec(memory_space=pltpu.VMEM),
        name="pick_blocks",
    )(ids, cells)


def place_kernel(pos_ref, slots_ref, shared_ref, out_ref):
    per_dev = out_ref.shape[2] // BLK - 1

    def step(dev, carry):
        for j in range(per_dev):
            out_ref[dev, :, j * BLK : (j + 1) * BLK] = slots_ref[pos_ref[dev * per_dev + j]]
        out_ref[dev, :, per_dev * BLK :] = shared_ref[...]
        return carry

    lax.fori_loop(0, out_ref.shape[0], step, 0)


def place_blocks(pos, slots, shared, heads):
    per_dev = pos.shape[0] // heads
    return pl.pallas_call(
        place_kernel,
        out_shape=jax.ShapeDtypeStruct(
            (heads, slots.shape[1], (per_dev + 1) * BLK), jnp.bfloat16
        ),
        in_specs=[
            pl.BlockSpec(memory_space=pltpu.SMEM),
            pl.BlockSpec(memory_space=pltpu.VMEM),
            pl.BlockSpec(memory_space=pltpu.VMEM),
        ],
        out_specs=pl.BlockSpec(memory_space=pltpu.VMEM),
        name="place_blocks",
    )(pos, slots, shared)


def attend_kernel(q_ref, kl_ref, vl_ref, kr_ref, vr_ref, mask_ref, out_ref):
    lane = lax.broadcasted_iota(jnp.int32, (BLK, BLK), 1)
    first = lane < BLK // 2
    spread = RAND * BLK
    nt = (((1,), (1,)), ((), ()))
    f32 = jnp.float32
    for b in range(2):
        rows = slice(b * BLK, (b + 1) * BLK)
        near = slice(b * BLK, (b + 3) * BLK)
        far = slice(b * spread, (b + 1) * spread)
        shared = slice(2 * spread, 2 * spread + BLK)
        q_pair = q_ref[rows, :]
        parts = []
        for h in range(2):
            mine = first if h == 0 else jnp.logical_not(first)
            q = jnp.where(mine, q_pair, jnp.zeros_like(q_pair))
            s1 = jnp.dot(q, kl_ref[:, near], preferred_element_type=f32) + mask_ref[b]
            s2 = jnp.dot(q, kr_ref[:, far], preferred_element_type=f32)
            s3 = jnp.dot(q, kr_ref[:, shared], preferred_element_type=f32)
            top = jnp.maximum(
                jnp.max(jnp.maximum(s1, s2), axis=-1, keepdims=True),
                jnp.max(s3, axis=-1, keepdims=True),
            )
            p1 = jnp.exp(s1 - top)
            p2 = jnp.exp(s2 - top)
            p3 = jnp.exp(s3 - top)
            total = jnp.sum(p1 + p2, axis=-1, keepdims=True) + jnp.sum(
                p3, axis=-1, keepdims=True
            )
            acc = lax.dot_general(
                p1.astype(jnp.bfloat16), vl_ref[:, near], nt, preferred_element_type=f32
            )
            acc += lax.dot_general(
                p2.astype(jnp.bfloat16), vr_ref[:, far], nt, preferred_element_type=f32
            )
            acc += lax.dot_general(
                p3.astype(jnp.bfloat16), vr_ref[:, shared], nt, preferred_element_type=f32
            )
            parts.append(acc / total)
        out_ref[rows, :] = jnp.where(first, parts[0], parts[1]).astype(jnp.bfloat16)


def attend(q, kv_near, kv_far, mask):
    rows, width = q.shape
    pairs = width // BLK
    near, far = kv_near.shape[1], kv_far.shape[1]
    return pl.pallas_call(
        attend_kernel,
        out_shape=jax.ShapeDtypeStruct((rows, width), jnp.bfloat16),
        grid=(pairs,),
        in_specs=[
            pl.BlockSpec((rows, BLK), lambda i: (0, i)),
            pl.BlockSpec((BLK, near), lambda i: (i, 0)),
            pl.BlockSpec((BLK, near), lambda i: (i + pairs, 0)),
            pl.BlockSpec((BLK, far), lambda i: (i, 0)),
            pl.BlockSpec((BLK, far), lambda i: (i + pairs, 0)),
            pl.BlockSpec(mask.shape, lambda i: (0, 0, 0)),
        ],
        out_specs=pl.BlockSpec((rows, BLK), lambda i: (0, i)),
        name="attend",
    )(q, kv_near, kv_near, kv_far, kv_far, mask)


def exchange_plan(pairs_dev, pairs_off, ctx_count, ctx_index, lower):
    pair_count = lower.shape[0]
    all_dev = pairs_dev.reshape(ctx_count, pair_count)
    all_off = pairs_off.reshape(ctx_count, pair_count)
    own = all_dev == ctx_index
    rank = jnp.sum((own[:, None, :] & lower[None]).astype(jnp.int32), axis=2)
    slot = jnp.arange(CAP, dtype=jnp.int32)
    chosen = own[:, None, :] & (rank[:, None, :] == slot[None, :, None])
    send = jnp.sum(jnp.where(chosen, all_off[:, None, :], 0), axis=2).reshape(-1)
    own_dev = lax.dynamic_index_in_dim(all_dev, ctx_index, 0, keepdims=False)
    earlier = (own_dev[:, None] == own_dev[None, :]) & lower
    take = own_dev * CAP + jnp.sum(earlier.astype(jnp.int32), axis=1)
    return send, take


def window_mask(lengths, first_pos, doc_tokens, rows):
    line_end = jnp.cumsum(lengths)
    positions = first_pos - BLK + jnp.arange(rows + 2 * BLK, dtype=jnp.int32)
    line = jnp.sum((line_end[None, :] <= positions[:, None]).astype(jnp.int32), axis=1)
    inside = (positions >= 0) & (positions < doc_tokens)
    line = jnp.where(inside, line, -1)
    masks = []
    for b in range(rows // BLK):
        keys = line[b * BLK : (b + 3) * BLK]
        queries = line[(b + 1) * BLK : (b + 2) * BLK]
        masks.append(jnp.where(queries[:, None] == keys[None, :], 0.0, NEG))
    return jnp.stack(masks).astype(jnp.float32)


def per_device(
    tokens, ln_gain, ln_bias, qkv_weight, out_weight, out_bias, lengths, pairs_dev, pairs_off
):
    ctx_count = lax.axis_size("ctx")
    heads = lax.axis_size("head")
    devices = ctx_count * heads
    ctx_index = lax.axis_index("ctx")
    head_index = lax.axis_index("head")
    rows, width = tokens.shape
    hd = width // heads

    wt = jnp.transpose(qkv_weight[:, 0, :])
    shard = jnp.concatenate([wt[hd : 2 * hd], wt[2 * hd :], wt[:hd], out_weight])
    shard = shard.reshape(4, hd, width)
    gathered = lax.all_gather(shard, "head", axis=1, tiled=True)

    normed, normed_t = layer_norm(tokens, ln_gain, ln_bias, heads)
    cells = lax.all_to_all(normed_t, "head", split_axis=0, concat_axis=0, tiled=True)

    both = ("ctx", "head")
    right = [(i, i + 1) for i in range(devices - 1)]
    left = [(i + 1, i) for i in range(devices - 1)]
    before = lax.ppermute(normed_t[:, :, rows - BLK :], both, right)
    after = lax.ppermute(normed_t[:, :, :BLK], both, left)
    near = jnp.concatenate([before, normed_t, after], axis=2).reshape(width, rows + 2 * BLK)

    pair_count = (heads * rows // BLK) * RAND
    order = jnp.arange(pair_count, dtype=jnp.int32)
    lower = order[None, :] < order[:, None]
    send, take = exchange_plan(pairs_dev, pairs_off, ctx_count, ctx_index, lower)
    outgoing = pick_blocks(send, cells).reshape(ctx_count, CAP * hd, BLK)
    slots = lax.all_to_all(outgoing, "ctx", split_axis=0, concat_axis=0, tiled=True)
    slots = slots.reshape(ctx_count * CAP, hd, BLK)

    shared = jnp.where(ctx_index == 0, cells[0, :, :BLK], 0).astype(jnp.bfloat16)
    reach = 1
    while reach < ctx_count:
        hop = [(i, i + reach) for i in range(reach)]
        shared = shared + lax.ppermute(shared, "ctx", hop)
        reach *= 2

    placed = place_blocks(take, slots, shared, heads)
    far = lax.all_to_all(placed, "head", split_axis=0, concat_axis=0, tiled=True)
    far = far.reshape(width, far.shape[2])

    mask = window_mask(
        lengths, (ctx_index * heads + head_index) * rows, devices * rows, rows
    )

    f32 = jnp.float32
    w_kv = gathered[:2].reshape(2 * width, width)
    w_q = gathered[2]
    q = lax.dot_general(normed, w_q, (((1,), (1,)), ((), ())), preferred_element_type=f32)
    q = (q.astype(jnp.bfloat16).astype(f32) * hd**-0.5).astype(jnp.bfloat16)
    kv_near = jnp.dot(w_kv, near, preferred_element_type=f32).astype(jnp.bfloat16)
    kv_far = jnp.dot(w_kv, far, preferred_element_type=f32).astype(jnp.bfloat16)
    attended = attend(q, kv_near, kv_far, mask)
    projected = jnp.dot(attended, gathered[3], preferred_element_type=f32)
    return (projected + out_bias).astype(jnp.bfloat16)


def solution(mesh):
    in_specs = (
        P(("ctx", "head"), None),
        P(),
        P(),
        P(None, "head", None),
        P("head", None),
        P(),
        P(),
        P(),
        P(),
    )
    return jax.shard_map(
        per_device,
        mesh=mesh,
        in_specs=in_specs,
        out_specs=P(("ctx", "head"), None),
        check_vma=False,
    )
```

time: 550 us -> 305 us (0.55)
  the two profiles are of different devices: /device:TPU:197 before, /device:TPU:7 now
where the time goes in v1:
time: 305 us; the launch traced here: 302 us
  waiting for transfers between devices  182 us (60%)
  starting transfers between devices  44.1 us (14%)
  Pallas kernels  24 us (8%)
  matrix products  18.4 us (6%)
  between operations  13.6 us (4%)
  local copies, waits for them, and re-layouts  11.5 us (4%)
  other arithmetic  8.23 us (3%)
    all_gather x1, waiting for transfers between devices, per_device(): gathered = lax.all_gather(shard, 'head', axis=1, tiled=True)  72 us
    ppermute x1, waiting for transfers between devices, per_device(): before = lax.ppermute(normed_t[:, :, rows - BLK:], both, right)  55.2 us
    ppermute x5, waiting for transfers between devices, per_device(): shared = shared + lax.ppermute(shared, 'ctx', hop)  40 us
    all_to_all x1, starting transfers between devices, per_device(): lax.all_to_all(outgoing, 'ctx', split_axis=0, concat_axis=0, tiled=True)  18 us
    pallas_call x1, Pallas kernels, attend(): pl.pallas_call(attend_kernel, out_shape=jax.ShapeDtypeStruct((rows, width...  14.5 us
    all_to_all x1, waiting for transfers between devices, per_device(): lax.all_to_all(normed_t, 'head', split_axis=0, concat_axis=0, tiled=True)  11.9 us
    dot_general x1, matrix products, per_device(): kv_far = jnp.dot(w_kv, far, preferred_element_type=f32).astype(jnp.bfloat16)  8.27 us
    all_to_all x1, starting transfers between devices, per_device(): lax.all_to_all(normed_t, 'head', split_axis=0, concat_axis=0, tiled=True)  8.01 us
  transfers between devices with their start and end apart: 11, of which 8 were waited for; matrix products, arithmetic and copies ran while one was open for 4% of the time, Pallas kernels for 3%

profile of v1, /device:TPU:7, one launch (start us, length us, event | category | flops | bytes accessed | tf_op | source)
XLA Modules:
  0.0 302.0 jit_solution(8185839818576407256)
XLA Ops:
  6.5 1.0 slice.59
  7.5 0.9 slice.60
  8.4 0.0 copy-start.6
  8.5 1.8 pad_maximum_fusion.1
  10.2 0.0 all-gather.2.cloned.1.call-update
  10.2 2.5 layer_norm.1
  12.7 8.0 %all-to-all-start = ((bf16[16,64,256]{2,1,0:T(8,128)(2,1)}), bf16[16,64,256]{2,1,0:T(8,128)(2,1)S(1)}, u32[]{:S(2)}, u32[]{:S(2)}) async-start(bf16[16,64,256]{2,1,0:T(8,128)(2,1)} %get-tuple-element.8), calls=%async_computation | async-start | bytes 1048576 | tf_op jit(solution)/shard_map/all_to_all | solution.py:197
  20.7 0.2 copy.12
  20.9 0.3 reshape.180
  21.2 0.0 copy-done.6
  21.2 0.2 copy.13
  21.5 0.3 broadcast_in_dim.48
  21.8 0.6 convert_reduce_fusion.1
  22.4 0.1 select_reduce_fusion
  22.5 0.1 copy.14
  22.6 0.7 reshape.181.ids_ref
  23.3 11.9 %all-to-all-done.cells_ref = bf16[16,64,256]{2,1,0:T(8,128)(2,1)S(1)} async-done(((bf16[16,64,256]{2,1,0:T(8,128)(2,1)}), bf16[16,64,256]{2,1,0:T(8,128)(2,1)S(1)}, u32[]{:S(2)}, u32[]{:S(2)}) %all-to-all-start) | async-done | bytes 524320 | tf_op jit(solution)/shard_map/all_to_all | solution.py:197
  35.2 0.8 copy-done.3
  36.0 3.7 %pick_blocks.1 = bf16[128,64,128]{2,1,0:T(8,128)(2,1)} custom-call(s32[128]{0:T(128)} %reshape.181.ids_ref, bf16[16,64,256]{2,1,0:T(8,128)(2,1)} %copy-done.3), custom_call_target="tpu_custom_call" | custom-call | tf_op jit(solution)/shard_map/pick_blocks/pallas_call | solution.py:47
  39.7 18.0 %all-to-all-start.1 = ((bf16[32,256,128]{2,1,0:T(8,128)(2,1)}), bf16[32,256,128]{2,1,0:T(8,128)(2,1)S(1)}, u32[]{:S(2)}, u32[]{:S(2)}) async-start(bf16[32,256,128]{2,1,0:T(8,128)(2,1)} %bitcast.47), calls=%async_computation.1 | async-start | bytes 4194304 | tf_op jit(solution)/shard_map/all_to_all | solution.py:211
  57.7 0.7 fusion.9
  58.4 0.7 collective-permute-start.2
  59.1 0.0 collective-permute-done.2
  59.1 0.7 fusion.19
  59.8 1.3 collective-permute-start.3
  61.1 17.7 %collective-permute-done.3 = bf16[64,128]{1,0:T(8,128)(2,1)S(1)} collective-permute-done((bf16[64,128]{1,0:T(8,128)(2,1)S(1)}, bf16[64,128]{1,0:T(8,128)(2,1)S(1)}, u32[]{:S(2)}, u32[]{:S(2)}) %collective-permute-start.3) | collective-permute-done | bytes 16416 | tf_op jit(solution)/shard_map/ppermute | solution.py:218
  78.8 1.3 collective-permute-start.4
  80.1 21.3 %collective-permute-done.4 = bf16[64,128]{1,0:T(8,128)(2,1)S(1)} collective-permute-done((bf16[64,128]{1,0:T(8,128)(2,1)S(1)}, bf16[64,128]{1,0:T(8,128)(2,1)S(1)}, u32[]{:S(2)}, u32[]{:S(2)}) %collective-permute-start.4) | collective-permute-done | bytes 16416 | tf_op jit(solution)/shard_map/ppermute | solution.py:218
  101.5 1.3 collective-permute-start.5
  102.8 0.2 convert_reduce_fusion.2
  103.0 0.7 collective-permute-done.5
  103.6 1.3 collective-permute-start.6
  104.9 0.6 multiply_add_fusion.pos_ref
  105.6 0.2 collective-permute-done.6
  105.8 0.6 add.50.shared_ref
  106.4 3.1 %all-to-all-done.1 = bf16[32,256,128]{2,1,0:T(8,128)(2,1)S(1)} async-done(((bf16[32,256,128]{2,1,0:T(8,128)(2,1)}), bf16[32,256,128]{2,1,0:T(8,128)(2,1)S(1)}, u32[]{:S(2)}, u32[]{:S(2)}) %all-to-all-start.1) | async-done | bytes 2097184 | tf_op jit(solution)/shard_map/all_to_all | solution.py:211
  109.5 1.4 copy-done
  110.8 3.3 %place_blocks.1 = bf16[16,64,896]{2,1,0:T(8,128)(2,1)} custom-call(s32[96]{0:T(128)} %multiply_add_fusion.pos_ref, bf16[128,64,128]{2,1,0:T(8,128)(2,1)} %bitcast.46, bf16[64,128]{1,0:T(8,128)(2,1)} %add.50.shared_ref), custom_call_target="tpu_custom_call" | custom-call | tf_op jit(solution)/shard_map/place_blocks/pallas_call | solution.py:73
  114.1 6.8 %all-to-all-start.2 = ((bf16[16,64,896]{2,1,0:T(8,128)(2,1)}), bf16[16,64,896]{2,1,0:T(8,128)(2,1)S(1)}, u32[]{:S(2)}, u32[]{:S(2)}) async-start(bf16[16,64,896]{2,1,0:T(8,128)(2,1)} %place_blocks.1), calls=%async_computation.2 | async-start | bytes 3670016 | tf_op jit(solution)/shard_map/all_to_all | solution.py:222
  121.0 0.0 copy-done.1
  121.0 0.1 fusion.10
  121.1 3.1 %collective-permute-start = (bf16[16,64,128]{2,1,0:T(8,128)(2,1)S(1)}, bf16[16,64,128]{2,1,0:T(8,128)(2,1)S(1)}, u32[]{:S(2)}, u32[]{:S(2)}) collective-permute-start(bf16[16,64,128]{2,1,0:T(8,128)(2,1)S(1)} %get-tuple-element.9), channel_id=1, source_target_pairs={{0,1},{1,2},{2,3},{3,4},{4,5},{5,6},{6,7},{7,8},{8,9},{9,10},{10,1... | collective-permute-start | bytes 786440 | tf_op jit(solution)/shard_map/ppermute | solution.py:202
  124.2 2.4 collective-permute-start.1
  126.6 0.0 copy-done.7
  126.6 0.3 reduce-window.9
  126.9 0.1 slice.52
  127.0 0.1 slice_reduce_fusion
  127.1 0.1 add_bitcast_fusion
  127.2 0.4 convert_reduce_fusion
  127.6 0.1 compare_select_fusion
  127.7 0.8 pad_maximum_fusion.2.mask_ref
  128.5 55.2 %collective-permute-done = bf16[16,64,128]{2,1,0:T(8,128)(2,1)S(1)} collective-permute-done((bf16[16,64,128]{2,1,0:T(8,128)(2,1)S(1)}, bf16[16,64,128]{2,1,0:T(8,128)(2,1)S(1)}, u32[]{:S(2)}, u32[]{:S(2)}) %collective-permute-start) | collective-permute-done | bytes 262176 | tf_op jit(solution)/shard_map/ppermute | solution.py:202
  183.7 0.7 copy-done.4
  184.4 0.0 collective-permute-done.1
  184.4 1.2 pad_maximum_fusion
  185.6 72.0 %all-gather.2.cloned.1.call-done = bf16[4,1024,1024]{2,1,0:T(8,128)(2,1)} async-done(((bf16[4,64,1024]{2,1,0:T(8,128)(2,1)}), bf16[4,1024,1024]{2,1,0:T(8,128)(2,1)}) %all-gather.2.cloned.1.call-update) | async-done | bytes 8388624 | tf_op jit(solution)/shard_map/all_gather | solution.py:194
  257.6 4.6 %slice.62 = bf16[2,1024,1024]{2,1,0:T(8,128)(2,1)} slice(bf16[4,1024,1024]{2,1,0:T(8,128)(2,1)} %all-gather.2.cloned.1.call-done), slice={[0:2], [0:1024], [0:1024]} | slice | bytes 8388608 | tf_op jit(solution)/shard_map/slice | solution.py:230
  262.2 0.0 all-to-all-done.2
  262.2 8.3 %convolution_convert_fusion.kr_ref.vr_ref = bf16[2048,896]{1,0:T(8,128)(2,1)} fusion(bf16[2048,1024]{1,0:T(8,128)(2,1)} %bitcast.48, bf16[1024,896]{1,0:T(8,128)(2,1)S(1)} %bitcast.51), kind=kOutput, calls=%fused_computation | convolution fusion | flops 3759931392 | bytes 9699328 | tf_op jit(solution)/shard_map/dot_general | solution.py:235
  270.5 3.7 %convolution_convert_fusion.1.kl_ref.vl_ref = bf16[2048,512]{1,0:T(8,128)(2,1)} fusion(bf16[2048,1024]{1,0:T(8,128)(2,1)S(1)} %bitcast.49, bf16[1024,512]{1,0:T(8,128)(2,1)S(1)} %bitcast.52), kind=kOutput, calls=%fused_computation.1 | convolution fusion | flops 2148532224 | bytes 7340032 | tf_op jit(solution)/shard_map/dot_general | solution.py:234
  274.2 3.2 %fusion.6.q_ref = bf16[256,1024]{1,0:T(8,128)(2,1)} fusion(bf16[256,1024]{1,0:T(8,128)(2,1)S(1)} %copy-done.8, bf16[4,1024,1024]{2,1,0:T(8,128)(2,1)} %all-gather.2.cloned.1.call-done), kind=kOutput, calls=%fused_computation.12 | convolution fusion | flops 537919488 | bytes 3145728 | tf_op jit(solution)/shard_map/dot_general | solution.py:232
  277.4 14.5 %attend.1 = bf16[256,1024]{1,0:T(8,128)(2,1)} custom-call(bf16[256,1024]{1,0:T(8,128)(2,1)} %fusion.6.q_ref, bf16[2048,512]{1,0:T(8,128)(2,1)} %convolution_convert_fusion.1.kl_ref.vl_ref, bf16[2048,512]{1,0:T(8,128)(2,1)} %convolution_convert_fusion.1.kl_ref.vl_ref, bf16[2048,896]{1,0:T(8,128)(2,1)} %convolution_convert_fusion.kr_ref.vr_ref, ...), custom_call_target="tpu_custom_call" | custom-call | tf_op jit(solution)/shard_map/attend/pallas_call | solution.py:134
  291.9 0.0 copy-done.9
  291.9 3.3 %fusion.7 = bf16[256,1024]{1,0:T(8,128)(2,1)} fusion(bf16[256,1024]{1,0:T(8,128)(2,1)} %attend.1, bf16[4,1024,1024]{2,1,0:T(8,128)(2,1)} %all-gather.2.cloned.1.call-done, f32[1024]{0:T(1024)S(1)} %copy-done.9), kind=kOutput, calls=%fused_computation.13 | convolution fusion | flops 537395200 | bytes 3149824 | tf_op jit(solution)/shard_map/dot_general | solution.py:237
  (24 shorter events, 0.1 us)
Async XLA Ops:
  6.5 14.2 %copy-start.5 = (s32[1024,3]{0,1:T(4,128)S(1)}, s32[1024,3]{0,1:T(4,128)}, u32[]{:S(2)}) copy-start(s32[1024,3]{0,1:T(4,128)} %param.16) | copy-start | bytes 36868
  6.5 251.1 %all-gather.2.cloned.1.call-start = ((), (), s32[]{:S(2)}) async-start(), calls=%async_computation.3 | async-start | bytes 8912896 | tf_op jit(solution)/shard_map/all_gather | solution.py:194
  8.4 12.8 %copy-start.6 = (s32[1024,3]{0,1:T(4,128)S(1)}, s32[1024,3]{0,1:T(4,128)}, u32[]{:S(2)}) copy-start(s32[1024,3]{0,1:T(4,128)} %param.17) | copy-start | bytes 36868
  12.7 22.5 %all-to-all-start = ((bf16[16,64,256]{2,1,0:T(8,128)(2,1)}), bf16[16,64,256]{2,1,0:T(8,128)(2,1)S(1)}, u32[]{:S(2)}, u32[]{:S(2)}) async-start(bf16[16,64,256]{2,1,0:T(8,128)(2,1)} %get-tuple-element.8), calls=%async_computation | async-start | bytes 1048576 | tf_op jit(solution)/shard_map/all_to_all | solution.py:197
  35.2 0.8 copy-start.3
  39.7 69.8 %all-to-all-start.1 = ((bf16[32,256,128]{2,1,0:T(8,128)(2,1)}), bf16[32,256,128]{2,1,0:T(8,128)(2,1)S(1)}, u32[]{:S(2)}, u32[]{:S(2)}) async-start(bf16[32,256,128]{2,1,0:T(8,128)(2,1)} %bitcast.47), calls=%async_computation.1 | async-start | bytes 4194304 | tf_op jit(solution)/shard_map/all_to_all | solution.py:211
  58.4 0.7 collective-permute-start.2
  59.8 19.0 %collective-permute-start.3 = (bf16[64,128]{1,0:T(8,128)(2,1)S(1)}, bf16[64,128]{1,0:T(8,128)(2,1)S(1)}, u32[]{:S(2)}, u32[]{:S(2)}) collective-permute-start(bf16[64,128]{1,0:T(8,128)(2,1)S(1)} %fusion.19), channel_id=1, source_target_pairs={{0,32},{16,48},{1,33},{17,49},{2,34},{18,50},{3,35},{19,51},{4,36}... | collective-permute-start | bytes 49160 | tf_op jit(solution)/shard_map/ppermute | solution.py:218
  78.8 22.7 %collective-permute-start.4 = (bf16[64,128]{1,0:T(8,128)(2,1)S(1)}, bf16[64,128]{1,0:T(8,128)(2,1)S(1)}, u32[]{:S(2)}, u32[]{:S(2)}) collective-permute-start(bf16[64,128]{1,0:T(8,128)(2,1)S(1)} %add.47), channel_id=1, source_target_pairs={{0,64},{16,80},{32,96},{48,112},{1,65},{17,81},{33,97},{49,113},{2... | collective-permute-start | bytes 49160 | tf_op jit(solution)/shard_map/ppermute | solution.py:218
  101.5 2.1 collective-permute-start.5
  103.6 2.1 collective-permute-start.6
  109.5 1.4 copy-start
  114.1 6.8 %copy-start.1 = (bf16[16,64,256]{2,1,0:T(8,128)(2,1)S(1)}, bf16[16,64,256]{2,1,0:T(8,128)(2,1)}, u32[]{:S(2)}) copy-start(bf16[16,64,256]{2,1,0:T(8,128)(2,1)} %get-tuple-element.8) | copy-start | bytes 1572868
  114.1 12.5 %copy-start.7 = (s32[1024]{0:T(1024)S(1)}, s32[1024]{0:T(1024)}, u32[]{:S(2)}) copy-start(s32[1024]{0:T(1024)} %param.15) | copy-start | bytes 12292
  114.1 148.1 %all-to-all-start.2 = ((bf16[16,64,896]{2,1,0:T(8,128)(2,1)}), bf16[16,64,896]{2,1,0:T(8,128)(2,1)S(1)}, u32[]{:S(2)}, u32[]{:S(2)}) async-start(bf16[16,64,896]{2,1,0:T(8,128)(2,1)} %place_blocks.1), calls=%async_computation.2 | async-start | bytes 3670016 | tf_op jit(solution)/shard_map/all_to_all | solution.py:222
  121.1 62.6 %collective-permute-start = (bf16[16,64,128]{2,1,0:T(8,128)(2,1)S(1)}, bf16[16,64,128]{2,1,0:T(8,128)(2,1)S(1)}, u32[]{:S(2)}, u32[]{:S(2)}) collective-permute-start(bf16[16,64,128]{2,1,0:T(8,128)(2,1)S(1)} %get-tuple-element.9), channel_id=1, source_target_pairs={{0,1},{1,2},{2,3},{3,4},{4,5},{5,6},{6,7},{7,8},{8,9},{9,10},{10,1... | collective-permute-start | bytes 786440 | tf_op jit(solution)/shard_map/ppermute | solution.py:202
  124.2 60.2 %collective-permute-start.1 = (bf16[16,64,128]{2,1,0:T(8,128)(2,1)S(1)}, bf16[16,64,128]{2,1,0:T(8,128)(2,1)}, u32[]{:S(2)}, u32[]{:S(2)}) collective-permute-start(bf16[16,64,128]{2,1,0:T(8,128)(2,1)S(1)} %get-tuple-element.10), channel_id=1, source_target_pairs={{1,0},{2,1},{3,2},{4,3},{5,4},{6,5},{7,6},{8,7},{9,8},{10,9},{11,1... | collective-permute-start | bytes 786440 | tf_op jit(solution)/shard_map/ppermute | solution.py:203
  183.7 0.7 copy-start.4
  262.2 8.3 %copy-start.2 = (bf16[2,1024,1024]{2,1,0:T(8,128)(2,1)S(1)}, bf16[2,1024,1024]{2,1,0:T(8,128)(2,1)}, u32[]{:S(2)}) copy-start(bf16[2,1024,1024]{2,1,0:T(8,128)(2,1)} %slice.62) | copy-start | bytes 12582916
  270.5 3.7 %copy-start.8 = (bf16[256,1024]{1,0:T(8,128)(2,1)S(1)}, bf16[256,1024]{1,0:T(8,128)(2,1)}, u32[]{:S(2)}) copy-start(bf16[256,1024]{1,0:T(8,128)(2,1)} %get-tuple-element.7) | copy-start | bytes 1572868
  277.4 14.5 %copy-start.9 = (f32[1024]{0:T(1024)S(1)}, f32[1024]{0:T(1024)}, u32[]{:S(2)}) copy-start(f32[1024]{0:T(1024)} %param.14) | copy-start | bytes 12292
Sparse Core Ops, SparseCore 0:
  10.4 247.2 all-gather.1

commit v2 on v1

v2 whole, which is shorter than its diff:
```python
import jax
import jax.numpy as jnp
from jax import lax
from jax.experimental import pallas as pl
from jax.experimental.pallas import tpu as pltpu
from jax.sharding import PartitionSpec as P

BLK = 128
RAND = 3
CAP = 4
EPS = 1e-05
NEG = float("-inf")
NT = (((1,), (1,)), ((), ()))


def ln_kernel(tok_ref, gain_ref, bias_ref, norm_ref, normt_ref):
    values = tok_ref[...].astype(jnp.float32)
    center = values - jnp.mean(values, axis=-1, keepdims=True)
    spread = jnp.mean(center * center, axis=-1, keepdims=True)
    normed = center * lax.rsqrt(spread + EPS) * gain_ref[...] + bias_ref[...]
    norm_ref[...] = normed.astype(jnp.bfloat16)
    normt_ref[...] = jnp.transpose(normed).astype(jnp.bfloat16).reshape(normt_ref.shape)


def layer_norm(tokens, gain, bias, heads):
    rows, width = tokens.shape
    return pl.pallas_call(
        ln_kernel,
        out_shape=(
            jax.ShapeDtypeStruct((rows, width), jnp.bfloat16),
            jax.ShapeDtypeStruct((heads, width // heads, rows), jnp.bfloat16),
        ),
        name="layer_norm",
    )(tokens, gain.reshape(1, width), bias.reshape(1, width))


def pick_kernel(ids_ref, cells_ref, out_ref):
    def step(slot, carry):
        block = ids_ref[slot]
        cols = pl.ds(pl.multiple_of((block % 2) * BLK, BLK), BLK)
        out_ref[slot] = cells_ref[block // 2, :, cols]
        return carry

    lax.fori_loop(0, out_ref.shape[0], step, 0, unroll=4)


def pick_blocks(ids, cells):
    return pl.pallas_call(
        pick_kernel,
        out_shape=jax.ShapeDtypeStruct((ids.shape[0], cells.shape[1], BLK), jnp.bfloat16),
        in_specs=[
            pl.BlockSpec(memory_space=pltpu.SMEM),
            pl.BlockSpec(memory_space=pltpu.VMEM),
        ],
        out_specs=pl.BlockSpec(memory_space=pltpu.VMEM),
        name="pick_blocks",
    )(ids, cells)


def place_kernel(pos_ref, slots_ref, out_ref):
    per_dev = out_ref.shape[2] // BLK

    def step(dev, carry):
        for j in range(per_dev):
            out_ref[dev, :, j * BLK : (j + 1) * BLK] = slots_ref[pos_ref[dev * per_dev + j]]
        return carry

    lax.fori_loop(0, out_ref.shape[0], step, 0)


def place_blocks(pos, slots, heads):
    per_dev = pos.shape[0] // heads
    return pl.pallas_call(
        place_kernel,
        out_shape=jax.ShapeDtypeStruct((heads, slots.shape[1], per_dev * BLK), jnp.bfloat16),
        in_specs=[
            pl.BlockSpec(memory_space=pltpu.SMEM),
            pl.BlockSpec(memory_space=pltpu.VMEM),
        ],
        out_specs=pl.BlockSpec(memory_space=pltpu.VMEM),
        name="place_blocks",
    )(pos, slots)


def head_lanes():
    return lax.broadcasted_iota(jnp.int32, (BLK, BLK), 1) < BLK // 2


def near_kernel(q_ref, k_ref, v_ref, mask_ref, acc_ref, top_ref, sum_ref):
    first = head_lanes()
    f32 = jnp.float32
    shared = slice(4 * BLK, 5 * BLK)
    for b in range(2):
        rows = slice(b * BLK, (b + 1) * BLK)
        near = slice(b * BLK, (b + 3) * BLK)
        q_pair = q_ref[rows, :]
        accs, tops, sums = [], [], []
        for mine in (first, jnp.logical_not(first)):
            q = jnp.where(mine, q_pair, jnp.zeros_like(q_pair))
            s = jnp.dot(q, k_ref[:, near], preferred_element_type=f32) + mask_ref[b]
            g = jnp.dot(q, k_ref[:, shared], preferred_element_type=f32)
            top = jnp.maximum(
                jnp.max(s, axis=-1, keepdims=True), jnp.max(g, axis=-1, keepdims=True)
            )
            p = jnp.exp(s - top)
            pg = jnp.exp(g - top)
            sums.append(
                jnp.sum(p, axis=-1, keepdims=True) + jnp.sum(pg, axis=-1, keepdims=True)
            )
            tops.append(top)
            accs.append(
                lax.dot_general(
                    p.astype(jnp.bfloat16), v_ref[:, near], NT, preferred_element_type=f32
                )
                + lax.dot_general(
                    pg.astype(jnp.bfloat16), v_ref[:, shared], NT, preferred_element_type=f32
                )
            )
        acc_ref[rows, :] = jnp.where(first, accs[0], accs[1])
        top_ref[rows, :] = jnp.where(first, tops[0], tops[1])
        sum_ref[rows, :] = jnp.where(first, sums[0], sums[1])


def near_attention(q, k, v, mask):
    rows, width = q.shape
    keys = k.shape[1]
    square = pl.BlockSpec((rows, BLK), lambda i: (0, i))
    wide = pl.BlockSpec((BLK, keys), lambda i: (i, 0))
    part = jax.ShapeDtypeStruct((rows, width), jnp.float32)
    return pl.pallas_call(
        near_kernel,
        out_shape=(part, part, part),
        grid=(width // BLK,),
        in_specs=[square, wide, wide, pl.BlockSpec(mask.shape, lambda i: (0, 0, 0))],
        out_specs=(square, square, square),
        name="near_attention",
    )(q, k, v, mask)


def far_kernel(q_ref, k_ref, v_ref, acc_ref, top_ref, sum_ref, out_ref):
    first = head_lanes()
    f32 = jnp.float32
    spread = RAND * BLK
    for b in range(2):
        rows = slice(b * BLK, (b + 1) * BLK)
        far = slice(b * spread, (b + 1) * spread)
        q_pair = q_ref[rows, :]
        outs = []
        for h, mine in enumerate((first, jnp.logical_not(first))):
            q = jnp.where(mine, q_pair, jnp.zeros_like(q_pair))
            s2 = jnp.dot(q, k_ref[:, far], preferred_element_type=f32)
            lane = h * (BLK // 2)
            old_top = top_ref[rows, lane : lane + 1]
            top = jnp.maximum(jnp.max(s2, axis=-1, keepdims=True), old_top)
            p2 = jnp.exp(s2 - top)
            scale = jnp.exp(old_top - top)
            total = jnp.sum(p2, axis=-1, keepdims=True)
            total += sum_ref[rows, lane : lane + 1] * scale
            acc = lax.dot_general(
                p2.astype(jnp.bfloat16), v_ref[:, far], NT, preferred_element_type=f32
            )
            acc += acc_ref[rows, :] * scale
            outs.append(acc / total)
        out_ref[rows, :] = jnp.where(first, outs[0], outs[1]).astype(jnp.bfloat16)


def far_attention(q, k, v, parts):
    rows, width = q.shape
    keys = k.shape[1]
    square = pl.BlockSpec((rows, BLK), lambda i: (0, i))
    wide = pl.BlockSpec((BLK, keys), lambda i: (i, 0))
    return pl.pallas_call(
        far_kernel,
        out_shape=jax.ShapeDtypeStruct((rows, width), jnp.bfloat16),
        grid=(width // BLK,),
        in_specs=[square, wide, wide, square, square, square],
        out_specs=square,
        name="far_attention",
    )(q, k, v, *parts)


def run_copies(copies):
    for copy in copies:
        copy.start()
    for copy in copies:
        copy.wait()


def piece_kernel(core_ref, wt_ref, out_w_ref, piece_ref, sems):
    rows, cols = wt_ref.shape[0], piece_ref.shape[1]
    mine = pl.ds(pl.multiple_of(core_ref[0] * cols, cols), cols)
    run_copies(
        [
            pltpu.make_async_copy(wt_ref.at[:, mine], piece_ref.at[:rows], sems.at[0]),
            pltpu.make_async_copy(out_w_ref.at[:, mine], piece_ref.at[rows:], sems.at[1]),
        ]
    )


def any_specs(count):
    return [pl.BlockSpec(memory_space=pl.ANY)] * count


def own_piece(core, wt, out_w):
    rows = wt.shape[0] + out_w.shape[0]
    return pl.pallas_call(
        piece_kernel,
        out_shape=jax.ShapeDtypeStruct((rows, wt.shape[1] // 2), jnp.bfloat16),
        in_specs=[pl.BlockSpec(memory_space=pltpu.SMEM)] + any_specs(2),
        out_specs=pl.BlockSpec(memory_space=pl.ANY),
        scratch_shapes=[pltpu.SemaphoreType.DMA((2,))],
        name="own_piece",
    )(core, wt, out_w)


def join_kernel(*refs):
    parts, out_ref, sems = refs[:-2], refs[-2], refs[-1]
    copies, row = [], 0
    for n, part in enumerate(parts):
        into = out_ref.at[pl.ds(row, part.shape[0])]
        copies.append(pltpu.make_async_copy(part, into, sems.at[n]))
        row += part.shape[0]
    run_copies(copies)


def join(*parts):
    rows = sum(part.shape[0] for part in parts)
    return pl.pallas_call(
        join_kernel,
        out_shape=jax.ShapeDtypeStruct((rows,) + parts[0].shape[1:], jnp.bfloat16),
        in_specs=any_specs(len(parts)),
        out_specs=pl.BlockSpec(memory_space=pl.ANY),
        scratch_shapes=[pltpu.SemaphoreType.DMA((len(parts),))],
        name="join",
    )(*parts)


def assemble_kernel(core_ref, *refs):
    sems = refs[-1]
    outs, parts = refs[-5:-1], refs[:-5]
    hd, width = outs[0].shape[1], outs[0].shape[2]
    cols = width // 2
    half = len(parts) // 2
    copies = []
    for n, part in enumerate(parts):
        side = core_ref[0] if n < half else 1 - core_ref[0]
        into_cols = pl.ds(pl.multiple_of(side * cols, cols), cols)
        count = part.shape[0]
        into_heads = pl.ds((n % half) * count, count)
        for k, out in enumerate(outs):
            copies.append(
                pltpu.make_async_copy(
                    part.at[:, pl.ds(k * hd, hd)],
                    out.at[into_heads, :, into_cols],
                    sems.at[n * len(outs) + k],
                )
            )
    run_copies(copies)


def assemble(core, parts, heads):
    count, rows, cols = parts[0].shape
    hd = rows // 4
    one = jax.ShapeDtypeStruct((heads, hd, 2 * cols), jnp.bfloat16)
    return pl.pallas_call(
        assemble_kernel,
        out_shape=(one,) * 4,
        in_specs=[pl.BlockSpec(memory_space=pltpu.SMEM)] + any_specs(len(parts)),
        out_specs=tuple(any_specs(4)),
        scratch_shapes=[pltpu.SemaphoreType.DMA((4 * len(parts),))],
        name="assemble",
    )(core, *parts)


def tied(value, *others):
    return lax.optimization_barrier((value,) + others)[0]


def shift(value, by, heads):
    pairs = [(i, (i + by) % heads) for i in range(heads)]
    return lax.ppermute(value, "head", pairs)


def swap(value, bits, devices):
    return lax.ppermute(value, ("ctx", "head"), [(i, i ^ bits) for i in range(devices)])


def widen(value, holders, steps):
    for step in steps:
        hop = [(i, i + step) for i in holders]
        value = value + lax.ppermute(value, ("ctx", "head"), hop)
        holders = holders + [i + step for i in holders]
    return value, holders


def exchange_plan(pairs_dev, pairs_off, ctx_count, ctx_index, lower):
    pair_count = lower.shape[0]
    all_dev = pairs_dev.reshape(ctx_count, pair_count)
    all_off = pairs_off.reshape(ctx_count, pair_count)
    own = all_dev == ctx_index
    rank = jnp.sum((own[:, None, :] & lower[None]).astype(jnp.int32), axis=2)
    slot = jnp.arange(CAP, dtype=jnp.int32)
    chosen = own[:, None, :] & (rank[:, None, :] == slot[None, :, None])
    send = jnp.sum(jnp.where(chosen, all_off[:, None, :], 0), axis=2).reshape(-1)
    own_dev = lax.dynamic_index_in_dim(all_dev, ctx_index, 0, keepdims=False)
    earlier = (own_dev[:, None] == own_dev[None, :]) & lower
    take = own_dev * CAP + jnp.sum(earlier.astype(jnp.int32), axis=1)
    return send, take


def window_mask(lengths, first_pos, doc_tokens, rows):
    line_end = jnp.cumsum(lengths)
    positions = first_pos - BLK + jnp.arange(rows + 2 * BLK, dtype=jnp.int32)
    line = jnp.sum((line_end[None, :] <= positions[:, None]).astype(jnp.int32), axis=1)
    inside = (positions >= 0) & (positions < doc_tokens)
    line = jnp.where(inside, line, -1)
    masks = []
    for b in range(rows // BLK):
        keys = line[b * BLK : (b + 3) * BLK]
        queries = line[(b + 1) * BLK : (b + 2) * BLK]
        masks.append(jnp.where(queries[:, None] == keys[None, :], 0.0, NEG))
    return jnp.stack(masks).astype(jnp.float32)


def per_device(
    tokens, ln_gain, ln_bias, qkv_weight, out_weight, out_bias, lengths, pairs_dev, pairs_off
):
    ctx_count = lax.axis_size("ctx")
    heads = lax.axis_size("head")
    devices = ctx_count * heads
    ctx_index = lax.axis_index("ctx")
    head_index = lax.axis_index("head")
    rows, width = tokens.shape
    hd = width // heads

    wt = jnp.transpose(qkv_weight[:, 0, :])
    core = (ctx_index % 2).astype(jnp.int32).reshape(1)
    place = ctx_index * heads + head_index

    normed, normed_t = layer_norm(tokens, ln_gain, ln_bias, heads)
    cells = lax.all_to_all(normed_t, "head", split_axis=0, concat_axis=0, tiled=True)

    own = own_piece(core, wt, out_weight)
    u1, d1 = shift(own, 2, heads), shift(own, -2, heads)

    shared = jnp.where(place == 0, normed_t[:, :, :BLK], 0).astype(jnp.bfloat16)
    holders = [0]
    shared, holders = widen(shared, holders, [16 * heads, 8 * heads])

    both = ("ctx", "head")
    right = [(i, i + 1) for i in range(devices - 1)]
    left = [(i + 1, i) for i in range(devices - 1)]
    before = lax.ppermute(normed_t[:, :, rows - BLK :], both, right)
    after = lax.ppermute(normed_t[:, :, :BLK], both, left)

    pair_count = (heads * rows // BLK) * RAND
    order = jnp.arange(pair_count, dtype=jnp.int32)
    lower = order[None, :] < order[:, None]
    send, take = exchange_plan(pairs_dev, pairs_off, ctx_count, ctx_index, lower)
    outgoing = pick_blocks(tied(send, u1, d1, shared), cells)
    outgoing = outgoing.reshape(ctx_count, CAP * hd, BLK)
    slots = lax.all_to_all(outgoing, "ctx", split_axis=0, concat_axis=0, tiled=True)
    slots = slots.reshape(ctx_count * CAP, hd, BLK)

    mid = own.shape[0] // 2
    u2, d2 = shift(u1, 2, heads), shift(d1, -2, heads)
    u3, d3 = shift(u2, 2, heads), shift(d2, -2, heads)
    u4, d4 = shift(u3[:mid], 2, heads), shift(d3[mid:], -2, heads)
    shape = (heads // 4,) + own.shape
    a = join(own, u1, d1, u2).reshape(shape)
    b = join(d2, u3, d3, u4, d4).reshape(shape)
    c = swap(a, 1, devices)
    d = swap(b, 2 * heads + 1, devices)
    shared, holders = widen(shared, holders, [4 * heads, heads, 2 * heads, 8, 4, 2, 1])

    placed = place_blocks(tied(take, c, d, shared), slots, heads)
    far = lax.all_to_all(placed, "head", split_axis=0, concat_axis=0, tiled=True)
    far = far.reshape(width, far.shape[2])

    mine = [a, b, c, d]
    other = [swap(part, heads, devices) for part in mine]
    near = jnp.concatenate([before, normed_t, after, shared], axis=2)
    near = near.reshape(width, near.shape[2])

    mask = window_mask(lengths, place * rows, devices * rows, rows)

    f32 = jnp.float32
    bf16 = jnp.bfloat16
    w_q, w_k, w_v, w_o = (
        w.reshape(width, width)
        for w in assemble(core, mine + other, heads)
    )
    q = lax.dot_general(normed, w_q, NT, preferred_element_type=f32)
    q = (q.astype(bf16).astype(f32) * hd**-0.5).astype(bf16)
    k_near = jnp.dot(w_k, near, preferred_element_type=f32).astype(bf16)
    v_near = jnp.dot(w_v, near, preferred_element_type=f32).astype(bf16)
    parts = near_attention(q, k_near, v_near, mask)
    k_far = jnp.dot(w_k, far, preferred_element_type=f32).astype(bf16)
    v_far = jnp.dot(w_v, far, preferred_element_type=f32).astype(bf16)
    attended = far_attention(q, k_far, v_far, parts)
    projected = jnp.dot(attended, w_o, preferred_element_type=f32)
    return (projected + out_bias).astype(bf16)


def solution(mesh):
    in_specs = (
        P(("ctx", "head"), None),
        P(),
        P(),
        P(None, "head", None),
        P("head", None),
        P(),
        P(),
        P(),
        P(),
    )
    return jax.shard_map(
        per_device,
        mesh=mesh,
        in_specs=in_specs,
        out_specs=P(("ctx", "head"), None),
        check_vma=False,
    )
```

time: 305 us -> 579 us (1.90)
  Pallas kernels: 24 us -> 366 us
  waiting for transfers between devices: 182 us -> 39.2 us
  starting transfers between devices: 44.1 us -> 125 us
  between operations: 13.6 us -> 0.65 us
    pallas_call x1 -> x6, Pallas kernels: 14.5 us -> 357 us  [the longest x1 255 us: assemble(): pl.pallas_call(assemble_kernel, out_shape=(one,) * 4, in_specs=[pl.BlockS...]
    ppermute x5 -> x23, starting transfers between devices: 5.8 us -> 90.9 us  [the longest x6 57.4 us: swap(): lax.ppermute(value, ('ctx', 'head'), [(i, i ^ bits) for i in range(device...]
    all_gather x1 -> x0, waiting for transfers between devices: 72 us -> none  [per_device(): gathered = lax.all_gather(shard, 'head', axis=1, tiled=True)]
    ppermute x1, waiting for transfers between devices: 55.2 us -> 7.62 us  [per_device(): before = lax.ppermute(normed_t[:, :, rows - BLK:], both, right)]
    ppermute x5 -> x23, waiting for transfers between devices: 40 us -> 19.5 us  [the longest x9 11.4 us: widen(): value = value + lax.ppermute(value, ('ctx', 'head'), hop)]
    ppermute x1, waiting for transfers between devices: 0.03 us -> 12.1 us  [per_device(): after = lax.ppermute(normed_t[:, :, :BLK], both, left)]
    all_to_all x1, waiting for transfers between devices: 11.9 us -> 0.01 us  [per_device(): lax.all_to_all(normed_t, 'head', split_axis=0, concat_axis=0, tiled=True)]
    dot_general x4 -> x6, matrix products: 18.4 us -> 21 us  [the longest x1 5 us: per_device(): k_far = jnp.dot(w_k, far, preferred_element_type=f32).astype(bf16)]
  transfers between devices with their start and end apart: 11 -> 28, of which waited for: 8 -> 9; matrix products, arithmetic and copies ran while one was open for 4% -> 4% of each run, Pallas kernels for 3% -> 60%
where the time goes in v2:
time: 579 us; the launch traced here: 572 us
  Pallas kernels  366 us (63%)
  starting transfers between devices  125 us (22%)
  waiting for transfers between devices  39.2 us (7%)
  matrix products  21 us (4%)
  other arithmetic  9.86 us (2%)
  local copies, waits for them, and re-layouts  9.42 us (2%)
    pallas_call x1, Pallas kernels, assemble(): pl.pallas_call(assemble_kernel, out_shape=(one,) * 4, in_specs=[pl.BlockS...  255 us
    pallas_call x2, Pallas kernels, join(): pl.pallas_call(join_kernel, out_shape=jax.ShapeDtypeStruct((rows,) + part...  65.8 us
    ppermute x6, starting transfers between devices, swap(): lax.ppermute(value, ('ctx', 'head'), [(i, i ^ bits) for i in range(device...  57.4 us
    ppermute x8, starting transfers between devices, shift(): return lax.ppermute(value, 'head', pairs)  25.3 us
    all_to_all x1, starting transfers between devices, per_device(): lax.all_to_all(outgoing, 'ctx', split_axis=0, concat_axis=0, tiled=True)  15.4 us
    pallas_call x1, Pallas kernels, far_attention(): pl.pallas_call(far_kernel, out_shape=jax.ShapeDtypeStruct((rows, width),...  14.2 us
    pallas_call x1, Pallas kernels, near_attention(): pl.pallas_call(near_kernel, out_shape=(part, part, part), grid=(width //...  12.2 us
    ppermute x1, waiting for transfers between devices, per_device(): after = lax.ppermute(normed_t[:, :, :BLK], both, left)  12.1 us
  transfers between devices with their start and end apart: 28, of which 9 were waited for; matrix products, arithmetic and copies ran while one was open for 4% of the time, Pallas kernels for 60%

profile of v2, /device:TPU:7, one launch (start us, length us, event | category | flops | bytes accessed | tf_op | source)
XLA Modules:
  0.0 571.6 jit_solution(11956524156680545953)
XLA Ops:
  0.0 2.5 layer_norm.1
  2.5 8.0 %all-to-all-start = ((bf16[16,64,256]{2,1,0:T(8,128)(2,1)}), bf16[16,64,256]{2,1,0:T(8,128)(2,1)S(1)}, u32[]{:S(2)}, u32[]{:S(2)}) async-start(bf16[16,64,256]{2,1,0:T(8,128)(2,1)} %get-tuple-element.19), calls=%async_computation | async-start | bytes 1048576 | tf_op jit(solution)/shard_map/all_to_all | solution.py:341
  10.5 1.9 fusion.5
  12.4 0.7 collective-permute-start.14
  13.1 9.1 %own_piece.1.refs_0_ = bf16[256,512]{1,0:T(8,128)(2,1)} custom-call(s32[1]{0:T(128)} %bitcast.2.core_ref, bf16[192,1024]{1,0:T(8,128)(2,1)} %bitcast.45, bf16[64,1024]{1,0:T(8,128)(2,1)} %out_w_ref.1), custom_call_target="tpu_custom_call" | custom-call | tf_op jit(solution)/shard_map/own_piece/pallas_call | solution.py:206
  22.2 3.1 collective-permute-start
  25.3 3.4 collective-permute-start.1
  29.3 0.7 collective-permute-start.15
  30.5 0.6 convert_reduce_fusion.1
  32.1 1.6 collective-permute-done.1.refs_2_
  33.7 0.8 copy-done.4
  34.6 3.7 pick_blocks.1
  38.3 15.4 %all-to-all-start.1 = ((bf16[32,256,128]{2,1,0:T(8,128)(2,1)}), bf16[32,256,128]{2,1,0:T(8,128)(2,1)S(1)}, u32[]{:S(2)}, u32[]{:S(2)}) async-start(bf16[32,256,128]{2,1,0:T(8,128)(2,1)} %bitcast.36), calls=%async_computation.1 | async-start | bytes 4194304 | tf_op jit(solution)/shard_map/all_to_all | solution.py:362
  53.7 0.7 collective-permute-start.16
  54.4 3.1 collective-permute-start.2
  57.5 3.4 collective-permute-start.3
  61.0 0.7 collective-permute-start.17
  61.7 3.3 collective-permute-done.2.refs_3_
  65.0 1.9 collective-permute-start.4
  67.5 4.0 collective-permute-start.5
  71.6 0.7 collective-permute-start.18
  72.3 2.4 collective-permute-done.4.refs_1_
  74.8 0.7 slice.42
  75.5 1.9 collective-permute-start.6
  77.5 0.7 slice.43
  78.2 4.5 collective-permute-start.7
  82.8 1.4 collective-permute-start.19
  84.2 32.9 %join.2 = bf16[1024,512]{1,0:T(8,128)(2,1)} custom-call(bf16[256,512]{1,0:T(8,128)(2,1)} %own_piece.1.refs_0_, bf16[256,512]{1,0:T(8,128)(2,1)} %copy-done.14, bf16[256,512]{1,0:T(8,128)(2,1)} %copy-done.15, bf16[256,512]{1,0:T(8,128)(2,1)} %copy-done.17), custom_call_target="tpu_custom_call" | custom-call | tf_op jit(solution)/shard_map/join/pallas_call | solution.py:228
  117.1 32.3 %collective-permute-start.8 = (bf16[4,256,512]{2,1,0:T(8,128)(2,1)}, bf16[4,256,512]{2,1,0:T(8,128)(2,1)S(1)}, u32[]{:S(2)}, u32[]{:S(2)}) collective-permute-start(bf16[4,256,512]{2,1,0:T(8,128)(2,1)} %bitcast.37), channel_id=1, source_target_pairs={{0,1},{1,0},{2,3},{3,2},{4,5},{5,4},{6,7},{7,6},{8,9},{9,8},{10,11... | collective-permute-start | bytes 3145736 | tf_op jit(solution)/shard_map/ppermute | solution.py:285
  149.5 0.6 copy-done.18
  150.1 32.9 %join.3 = bf16[1024,512]{1,0:T(8,128)(2,1)} custom-call(bf16[256,512]{1,0:T(8,128)(2,1)} %copy-done.16, bf16[256,512]{1,0:T(8,128)(2,1)} %copy-done.10, bf16[256,512]{1,0:T(8,128)(2,1)} %copy-done.11, bf16[128,512]{1,0:T(8,128)(2,1)} %copy-done.18, bf16[128,512]{1,0:T(8,128)(2,1)} %collective-permute-done.7.refs_4_), custom_call_target="tpu_custom_call" | custom-call | tf_op jit(solution)/shard_map/join/pallas_call | solution.py:228
  183.0 5.6 collective-permute-start.9
  188.6 1.0 add.69
  189.6 0.7 collective-permute-start.20
  190.4 1.4 collective-permute-start.21
  191.8 1.0 add.71
  192.9 1.3 collective-permute-start.22
  194.9 11.4 %collective-permute-done.22 = bf16[16,64,128]{2,1,0:T(8,128)(2,1)S(1)} collective-permute-done((bf16[16,64,128]{2,1,0:T(8,128)(2,1)S(1)}, bf16[16,64,128]{2,1,0:T(8,128)(2,1)S(1)}, u32[]{:S(2)}, u32[]{:S(2)}) %collective-permute-start.22) | collective-permute-done | bytes 262176 | tf_op jit(solution)/shard_map/ppermute | solution.py:291
  206.4 0.9 copy-done.6
  207.3 0.7 copy-done
  208.0 3.2 place_blocks.1
  211.2 6.9 %all-to-all-start.2 = ((bf16[16,64,768]{2,1,0:T(8,128)(2,1)}), bf16[16,64,768]{2,1,0:T(8,128)(2,1)}, u32[]{:S(2)}, u32[]{:S(2)}) async-start(bf16[16,64,768]{2,1,0:T(8,128)(2,1)} %place_blocks.1), calls=%async_computation.2 | async-start | bytes 3145728 | tf_op jit(solution)/shard_map/all_to_all | solution.py:377
  218.1 2.1 collective-permute-start.24
  221.1 13.3 %collective-permute-start.10 = (bf16[4,256,512]{2,1,0:T(8,128)(2,1)S(1)}, bf16[4,256,512]{2,1,0:T(8,128)(2,1)S(1)}, u32[]{:S(2)}, u32[]{:S(2)}) collective-permute-start(bf16[4,256,512]{2,1,0:T(8,128)(2,1)S(1)} %bitcast.39), channel_id=1, source_target_pairs={{0,16},{1,17},{2,18},{3,19},{4,20},{5,21},{6,22},{7,23},{8,24},{9,... | collective-permute-start | bytes 3145736 | tf_op jit(solution)/shard_map/ppermute | solution.py:285
  234.4 1.9 collective-permute-start.11
  236.4 2.4 collective-permute-start.12
  238.8 1.9 collective-permute-start.13
  240.7 12.1 %collective-permute-done.24 = bf16[16,64,128]{2,1,0:T(8,128)(2,1)S(1)} collective-permute-done((bf16[16,64,128]{2,1,0:T(8,128)(2,1)S(1)}, bf16[16,64,128]{2,1,0:T(8,128)(2,1)S(1)}, u32[]{:S(2)}, u32[]{:S(2)}) %collective-permute-start.24) | collective-permute-done | bytes 262176 | tf_op jit(solution)/shard_map/ppermute | solution.py:354
  252.8 2.1 collective-permute-start.23
  255.0 0.8 pad_maximum_fusion.1.mask_ref
  255.8 7.6 %collective-permute-done.23 = bf16[16,64,128]{2,1,0:T(8,128)(2,1)S(1)} collective-permute-done((bf16[16,64,128]{2,1,0:T(8,128)(2,1)}, bf16[16,64,128]{2,1,0:T(8,128)(2,1)S(1)}, u32[]{:S(2)}, u32[]{:S(2)}) %collective-permute-start.23) | collective-permute-done | bytes 262176 | tf_op jit(solution)/shard_map/ppermute | solution.py:353
  263.4 2.3 pad_maximum_fusion
  265.7 1.0 copy-done.7
  266.7 1.0 copy-done.8
  267.7 1.0 copy-done.9
  268.7 255.5 %assemble.1 = (bf16[16,64,1024]{2,1,0:T(8,128)(2,1)}, bf16[16,64,1024]{2,1,0:T(8,128)(2,1)}, bf16[16,64,1024]{2,1,0:T(8,128)(2,1)}, bf16[16,64,1024]{2,1,0:T(8,128)(2,1)}) custom-call(s32[1]{0:T(128)} %bitcast.2.core_ref, bf16[4,256,512]{2,1,0:T(8,128)(2,1)} %bitcast.38, bf16[4,256,512]{2,1,0:T(8,128)(2,1)} %bitcast.41, bf16[4,256,512]{2,1,0:T(8,128)(2,1)} %copy-done.6, ...), custom_call_target="tpu_custom_call" | custom-call | tf_op jit(solution)/shard_map/assemble/pallas_call | solution.py:265
  524.2 3.3 fusion.2.q_ref
  527.5 2.9 convolution_convert_fusion.3.k_ref
  530.4 2.9 convolution_convert_fusion.2.v_ref
  533.3 12.2 %near_attention.1 = (f32[256,1024]{1,0:T(8,128)}, f32[256,1024]{1,0:T(8,128)}, f32[256,1024]{1,0:T(8,128)}) custom-call(bf16[256,1024]{1,0:T(8,128)(2,1)} %fusion.2.q_ref, bf16[1024,640]{1,0:T(8,128)(2,1)} %convolution_convert_fusion.3.k_ref, bf16[1024,640]{1,0:T(8,128)(2,1)} %convolution_convert_fusion.2.v_ref, f32[2,128,384]{2,1,0:T(8,128)} %pad_maximum_fusion.1.mask_ref), custom_call_target="tpu_custom_call" | custom-call | tf_op jit(solution)/shard_map/near_attention/pallas_call | solution.py:130
  545.5 5.0 convolution_convert_fusion.1.k_ref
  550.5 4.4 convolution_convert_fusion.v_ref
  554.8 14.2 %far_attention.1 = bf16[256,1024]{1,0:T(8,128)(2,1)} custom-call(bf16[256,1024]{1,0:T(8,128)(2,1)} %fusion.2.q_ref, bf16[1024,768]{1,0:T(8,128)(2,1)} %convolution_convert_fusion.1.k_ref, bf16[1024,768]{1,0:T(8,128)(2,1)} %convolution_convert_fusion.v_ref, f32[256,1024]{1,0:T(8,128)} %get-tuple-element.23.acc_ref, f32[256,1024]{1,0:T(8,128)} %get-tuple-element.24.top_ref, ...), custom_call_target="tpu_custom_call" | custom-call | tf_op jit(solution)/shard_map/far_attention/pallas_call | solution.py:172
  569.0 2.5 fusion.3
  (99 shorter events, 5.0 us)
Async XLA Ops:
  0.0 28.7 %copy-start.19 = (s32[1024,3]{0,1:T(4,128)S(1)}, s32[1024,3]{0,1:T(4,128)}, u32[]{:S(2)}) copy-start(s32[1024,3]{0,1:T(4,128)} %param.16) | copy-start | bytes 36868
  2.5 31.2 %all-to-all-start = ((bf16[16,64,256]{2,1,0:T(8,128)(2,1)}), bf16[16,64,256]{2,1,0:T(8,128)(2,1)S(1)}, u32[]{:S(2)}, u32[]{:S(2)}) async-start(bf16[16,64,256]{2,1,0:T(8,128)(2,1)} %get-tuple-element.19), calls=%async_computation | async-start | bytes 1048576 | tf_op jit(solution)/shard_map/all_to_all | solution.py:341
  10.5 19.5 %copy-start.20 = (s32[1024,3]{0,1:T(4,128)S(1)}, s32[1024,3]{0,1:T(4,128)}, u32[]{:S(2)}) copy-start(s32[1024,3]{0,1:T(4,128)} %param.17) | copy-start | bytes 36868
  12.4 16.8 %collective-permute-start.14 = (bf16[16,64,128]{2,1,0:T(8,128)(2,1)S(1)}, bf16[16,64,128]{2,1,0:T(8,128)(2,1)S(1)}, u32[]{:S(2)}, u32[]{:S(2)}) collective-permute-start(bf16[16,64,128]{2,1,0:T(8,128)(2,1)S(1)} %get-tuple-element.28), channel_id=1, source_target_pairs={{0,256}} | collective-permute-start | bytes 786440 | tf_op jit(solution)/shard_map/ppermute | solution.py:291
  22.2 9.9 %collective-permute-start = (bf16[256,512]{1,0:T(8,128)(2,1)}, bf16[256,512]{1,0:T(8,128)(2,1)S(1)}, u32[]{:S(2)}, u32[]{:S(2)}) collective-permute-start(bf16[256,512]{1,0:T(8,128)(2,1)} %own_piece.1.refs_0_), channel_id=1, source_target_pairs={{0,2},{1,3},{2,4},{3,5},{4,6},{5,7},{6,8},{7,9},{8,10},{9,11},{10,... | collective-permute-start | bytes 786440 | tf_op jit(solution)/shard_map/ppermute | solution.py:281
  25.3 8.4 %collective-permute-start.1 = (bf16[256,512]{1,0:T(8,128)(2,1)}, bf16[256,512]{1,0:T(8,128)(2,1)S(1)}, u32[]{:S(2)}, u32[]{:S(2)}) collective-permute-start(bf16[256,512]{1,0:T(8,128)(2,1)} %own_piece.1.refs_0_), channel_id=1, source_target_pairs={{0,14},{1,15},{2,0},{3,1},{4,2},{5,3},{6,4},{7,5},{8,6},{9,7},{10,... | collective-permute-start | bytes 786440 | tf_op jit(solution)/shard_map/ppermute | solution.py:281
  29.3 2.7 collective-permute-start.15
  32.1 52.1 %copy-start.14 = (bf16[256,512]{1,0:T(8,128)(2,1)}, bf16[256,512]{1,0:T(8,128)(2,1)S(1)}, u32[]{:S(2)}) copy-start(bf16[256,512]{1,0:T(8,128)(2,1)S(1)} %collective-permute-done.refs_1_) | copy-start | bytes 786436
  33.7 50.5 %copy-start.15 = (bf16[256,512]{1,0:T(8,128)(2,1)}, bf16[256,512]{1,0:T(8,128)(2,1)S(1)}, u32[]{:S(2)}) copy-start(bf16[256,512]{1,0:T(8,128)(2,1)S(1)} %collective-permute-done.1.refs_2_) | copy-start | bytes 786436
  33.7 0.8 copy-start.4
  38.3 168.1 %all-to-all-start.1 = ((bf16[32,256,128]{2,1,0:T(8,128)(2,1)}), bf16[32,256,128]{2,1,0:T(8,128)(2,1)S(1)}, u32[]{:S(2)}, u32[]{:S(2)}) async-start(bf16[32,256,128]{2,1,0:T(8,128)(2,1)} %bitcast.36), calls=%async_computation.1 | async-start | bytes 4194304 | tf_op jit(solution)/shard_map/all_to_all | solution.py:362
  53.7 7.2 %collective-permute-start.16 = (bf16[16,64,128]{2,1,0:T(8,128)(2,1)S(1)}, bf16[16,64,128]{2,1,0:T(8,128)(2,1)S(1)}, u32[]{:S(2)}, u32[]{:S(2)}) collective-permute-start(bf16[16,64,128]{2,1,0:T(8,128)(2,1)S(1)} %add.65), channel_id=1, source_target_pairs={{0,64},{256,320},{128,192},{384,448}} | collective-permute-start | bytes 786440 | tf_op jit(solution)/shard_map/ppermute | solution.py:291
  54.4 10.7 %collective-permute-start.2 = (bf16[256,512]{1,0:T(8,128)(2,1)S(1)}, bf16[256,512]{1,0:T(8,128)(2,1)S(1)}, u32[]{:S(2)}, u32[]{:S(2)}) collective-permute-start(bf16[256,512]{1,0:T(8,128)(2,1)S(1)} %collective-permute-done.refs_1_), channel_id=1, source_target_pairs={{0,2},{1,3},{2,4},{3,5},{4,6},{5,7},{6,8},{7,9},{8,10},{9,11},{10,... | collective-permute-start | bytes 786440 | tf_op jit(solution)/shard_map/ppermute | solution.py:281
  57.5 10.0 %collective-permute-start.3 = (bf16[256,512]{1,0:T(8,128)(2,1)S(1)}, bf16[256,512]{1,0:T(8,128)(2,1)S(1)}, u32[]{:S(2)}, u32[]{:S(2)}) collective-permute-start(bf16[256,512]{1,0:T(8,128)(2,1)S(1)} %collective-permute-done.1.refs_2_), channel_id=1, source_target_pairs={{0,14},{1,15},{2,0},{3,1},{4,2},{5,3},{6,4},{7,5},{8,6},{9,7},{10,... | collective-permute-start | bytes 786440 | tf_op jit(solution)/shard_map/ppermute | solution.py:281
  61.0 10.5 %collective-permute-start.17 = (bf16[16,64,128]{2,1,0:T(8,128)(2,1)S(1)}, bf16[16,64,128]{2,1,0:T(8,128)(2,1)S(1)}, u32[]{:S(2)}, u32[]{:S(2)}) collective-permute-start(bf16[16,64,128]{2,1,0:T(8,128)(2,1)S(1)} %add.66), channel_id=1, source_target_pairs={{0,16},{256,272},{128,144},{384,400},{64,80},{320,336},{192,208},{... | collective-permute-start | bytes 786440 | tf_op jit(solution)/shard_map/ppermute | solution.py:291
  65.0 19.2 %copy-start.17 = (bf16[256,512]{1,0:T(8,128)(2,1)}, bf16[256,512]{1,0:T(8,128)(2,1)S(1)}, u32[]{:S(2)}) copy-start(bf16[256,512]{1,0:T(8,128)(2,1)S(1)} %collective-permute-done.2.refs_3_) | copy-start | bytes 786436
  65.0 9.7 %collective-permute-start.4 = (bf16[256,512]{1,0:T(8,128)(2,1)S(1)}, bf16[256,512]{1,0:T(8,128)(2,1)S(1)}, u32[]{:S(2)}, u32[]{:S(2)}) collective-permute-start(bf16[256,512]{1,0:T(8,128)(2,1)S(1)} %collective-permute-done.2.refs_3_), channel_id=1, source_target_pairs={{0,2},{1,3},{2,4},{3,5},{4,6},{5,7},{6,8},{7,9},{8,10},{9,11},{10,... | collective-permute-start | bytes 786440 | tf_op jit(solution)/shard_map/ppermute | solution.py:281
  67.5 15.3 %copy-start.16 = (bf16[256,512]{1,0:T(8,128)(2,1)}, bf16[256,512]{1,0:T(8,128)(2,1)S(1)}, u32[]{:S(2)}) copy-start(bf16[256,512]{1,0:T(8,128)(2,1)S(1)} %collective-permute-done.3.refs_0_) | copy-start | bytes 786436
  67.5 10.0 %collective-permute-start.5 = (bf16[256,512]{1,0:T(8,128)(2,1)S(1)}, bf16[256,512]{1,0:T(8,128)(2,1)S(1)}, u32[]{:S(2)}, u32[]{:S(2)}) collective-permute-start(bf16[256,512]{1,0:T(8,128)(2,1)S(1)} %collective-permute-done.3.refs_0_), channel_id=1, source_target_pairs={{0,14},{1,15},{2,0},{3,1},{4,2},{5,3},{6,4},{7,5},{8,6},{9,7},{10,... | collective-permute-start | bytes 786440 | tf_op jit(solution)/shard_map/ppermute | solution.py:281
  71.6 11.1 %collective-permute-start.18 = (bf16[16,64,128]{2,1,0:T(8,128)(2,1)S(1)}, bf16[16,64,128]{2,1,0:T(8,128)(2,1)S(1)}, u32[]{:S(2)}, u32[]{:S(2)}) collective-permute-start(bf16[16,64,128]{2,1,0:T(8,128)(2,1)S(1)} %add.67), channel_id=1, source_target_pairs={{0,32},{256,288},{128,160},{384,416},{64,96},{320,352},{192,224},{... | collective-permute-start | bytes 786440 | tf_op jit(solution)/shard_map/ppermute | solution.py:291
  74.8 8.0 %copy-start.10 = (bf16[256,512]{1,0:T(8,128)(2,1)}, bf16[256,512]{1,0:T(8,128)(2,1)S(1)}, u32[]{:S(2)}) copy-start(bf16[256,512]{1,0:T(8,128)(2,1)S(1)} %collective-permute-done.4.refs_1_) | copy-start | bytes 786436
  75.5 74.0 %collective-permute-start.6 = (bf16[128,512]{1,0:T(8,128)(2,1)}, bf16[128,512]{1,0:T(8,128)(2,1)S(1)}, u32[]{:S(2)}, u32[]{:S(2)}) collective-permute-start(bf16[128,512]{1,0:T(8,128)(2,1)} %slice.42), channel_id=1, source_target_pairs={{0,2},{1,3},{2,4},{3,5},{4,6},{5,7},{6,8},{7,9},{8,10},{9,11},{10,... | collective-permute-start | bytes 393224 | tf_op jit(solution)/shard_map/ppermute | solution.py:281
  77.5 5.3 copy-start.11
  78.2 71.2 %collective-permute-start.7 = (bf16[128,512]{1,0:T(8,128)(2,1)}, bf16[128,512]{1,0:T(8,128)(2,1)}, u32[]{:S(2)}, u32[]{:S(2)}) collective-permute-start(bf16[128,512]{1,0:T(8,128)(2,1)} %slice.43), channel_id=1, source_target_pairs={{0,14},{1,15},{2,0},{3,1},{4,2},{5,3},{6,4},{7,5},{8,6},{9,7},{10,... | collective-permute-start | bytes 393224 | tf_op jit(solution)/shard_map/ppermute | solution.py:281
  82.8 105.8 %collective-permute-start.19 = (bf16[16,64,128]{2,1,0:T(8,128)(2,1)S(1)}, bf16[16,64,128]{2,1,0:T(8,128)(2,1)}, u32[]{:S(2)}, u32[]{:S(2)}) collective-permute-start(bf16[16,64,128]{2,1,0:T(8,128)(2,1)S(1)} %add.68), channel_id=1, source_target_pairs={{0,8},{256,264},{128,136},{384,392},{64,72},{320,328},{192,200},{4... | collective-permute-start | bytes 786440 | tf_op jit(solution)/shard_map/ppermute | solution.py:291
  117.1 89.2 %collective-permute-start.8 = (bf16[4,256,512]{2,1,0:T(8,128)(2,1)}, bf16[4,256,512]{2,1,0:T(8,128)(2,1)S(1)}, u32[]{:S(2)}, u32[]{:S(2)}) collective-permute-start(bf16[4,256,512]{2,1,0:T(8,128)(2,1)} %bitcast.37), channel_id=1, source_target_pairs={{0,1},{1,0},{2,3},{3,2},{4,5},{5,4},{6,7},{7,6},{8,9},{9,8},{10,11... | collective-permute-start | bytes 3145736 | tf_op jit(solution)/shard_map/ppermute | solution.py:285
  149.5 0.6 copy-start.18
  183.0 23.3 %collective-permute-start.9 = (bf16[4,256,512]{2,1,0:T(8,128)(2,1)}, bf16[4,256,512]{2,1,0:T(8,128)(2,1)}, u32[]{:S(2)}, u32[]{:S(2)}) collective-permute-start(bf16[4,256,512]{2,1,0:T(8,128)(2,1)} %bitcast.40), channel_id=1, source_target_pairs={{0,33},{1,32},{2,35},{3,34},{4,37},{5,36},{6,39},{7,38},{8,41},{9,... | collective-permute-start | bytes 3145736 | tf_op jit(solution)/shard_map/ppermute | solution.py:285
  189.6 0.7 collective-permute-start.20
  190.4 1.4 collective-permute-start.21
  192.9 13.4 %collective-permute-start.22 = (bf16[16,64,128]{2,1,0:T(8,128)(2,1)S(1)}, bf16[16,64,128]{2,1,0:T(8,128)(2,1)S(1)}, u32[]{:S(2)}, u32[]{:S(2)}) collective-permute-start(bf16[16,64,128]{2,1,0:T(8,128)(2,1)S(1)} %add.71), channel_id=1, source_target_pairs={{0,1},{256,257},{128,129},{384,385},{64,65},{320,321},{192,193},{4... | collective-permute-start | bytes 786440 | tf_op jit(solution)/shard_map/ppermute | solution.py:291
  206.3 1.0 copy-start.6
  206.4 1.7 copy-start
  211.2 6.9 %copy-start.12 = (bf16[16,64,128]{2,1,0:T(8,128)(2,1)S(1)}, bf16[16,64,128]{2,1,0:T(8,128)(2,1)}, u32[]{:S(2)}) copy-start(bf16[16,64,128]{2,1,0:T(8,128)(2,1)} %get-tuple-element.29) | copy-start | bytes 786436
  211.2 9.0 %copy-start.21 = (s32[1024]{0:T(1024)S(1)}, s32[1024]{0:T(1024)}, u32[]{:S(2)}) copy-start(s32[1024]{0:T(1024)} %param.15) | copy-start | bytes 12292
  211.2 9.9 %copy-start.2 = (bf16[1024,512]{1,0:T(8,128)(2,1)S(1)}, bf16[1024,512]{1,0:T(8,128)(2,1)}, u32[]{:S(2)}) copy-start(bf16[1024,512]{1,0:T(8,128)(2,1)} %join.2) | copy-start | bytes 3145732
  211.2 23.2 %copy-start.3 = (bf16[1024,512]{1,0:T(8,128)(2,1)S(1)}, bf16[1024,512]{1,0:T(8,128)(2,1)}, u32[]{:S(2)}) copy-start(bf16[1024,512]{1,0:T(8,128)(2,1)} %join.3) | copy-start | bytes 3145732
  211.2 52.2 %copy-start.1 = (bf16[16,64,256]{2,1,0:T(8,128)(2,1)S(1)}, bf16[16,64,256]{2,1,0:T(8,128)(2,1)}, u32[]{:S(2)}) copy-start(bf16[16,64,256]{2,1,0:T(8,128)(2,1)} %get-tuple-element.19) | copy-start | bytes 1572868
  211.2 334.3 %all-to-all-start.2 = ((bf16[16,64,768]{2,1,0:T(8,128)(2,1)}), bf16[16,64,768]{2,1,0:T(8,128)(2,1)}, u32[]{:S(2)}, u32[]{:S(2)}) async-start(bf16[16,64,768]{2,1,0:T(8,128)(2,1)} %place_blocks.1), calls=%async_computation.2 | async-start | bytes 3145728 | tf_op jit(solution)/shard_map/all_to_all | solution.py:377
  218.1 34.7 %collective-permute-start.24 = (bf16[16,64,128]{2,1,0:T(8,128)(2,1)S(1)}, bf16[16,64,128]{2,1,0:T(8,128)(2,1)S(1)}, u32[]{:S(2)}, u32[]{:S(2)}) collective-permute-start(bf16[16,64,128]{2,1,0:T(8,128)(2,1)S(1)} %copy-done.12), channel_id=1, source_target_pairs={{1,0},{2,1},{3,2},{4,3},{5,4},{6,5},{7,6},{8,7},{9,8},{10,9},{11,1... | collective-permute-start | bytes 786440 | tf_op jit(solution)/shard_map/ppermute | solution.py:354
  221.1 44.6 %collective-permute-start.10 = (bf16[4,256,512]{2,1,0:T(8,128)(2,1)S(1)}, bf16[4,256,512]{2,1,0:T(8,128)(2,1)S(1)}, u32[]{:S(2)}, u32[]{:S(2)}) collective-permute-start(bf16[4,256,512]{2,1,0:T(8,128)(2,1)S(1)} %bitcast.39), channel_id=1, source_target_pairs={{0,16},{1,17},{2,18},{3,19},{4,20},{5,21},{6,22},{7,23},{8,24},{9,... | collective-permute-start | bytes 3145736 | tf_op jit(solution)/shard_map/ppermute | solution.py:285
  234.4 31.3 %collective-permute-start.11 = (bf16[4,256,512]{2,1,0:T(8,128)(2,1)S(1)}, bf16[4,256,512]{2,1,0:T(8,128)(2,1)S(1)}, u32[]{:S(2)}, u32[]{:S(2)}) collective-permute-start(bf16[4,256,512]{2,1,0:T(8,128)(2,1)S(1)} %bitcast.42), channel_id=1, source_target_pairs={{0,16},{1,17},{2,18},{3,19},{4,20},{5,21},{6,22},{7,23},{8,24},{9,... | collective-permute-start | bytes 3145736 | tf_op jit(solution)/shard_map/ppermute | solution.py:285
  236.4 30.3 %collective-permute-start.12 = (bf16[4,256,512]{2,1,0:T(8,128)(2,1)}, bf16[4,256,512]{2,1,0:T(8,128)(2,1)S(1)}, u32[]{:S(2)}, u32[]{:S(2)}) collective-permute-start(bf16[4,256,512]{2,1,0:T(8,128)(2,1)} %copy-done.6), channel_id=1, source_target_pairs={{0,16},{1,17},{2,18},{3,19},{4,20},{5,21},{6,22},{7,23},{8,24},{9,... | collective-permute-start | bytes 3145736 | tf_op jit(solution)/shard_map/ppermute | solution.py:285
  238.8 29.9 %collective-permute-start.13 = (bf16[4,256,512]{2,1,0:T(8,128)(2,1)}, bf16[4,256,512]{2,1,0:T(8,128)(2,1)}, u32[]{:S(2)}, u32[]{:S(2)}) collective-permute-start(bf16[4,256,512]{2,1,0:T(8,128)(2,1)} %collective-permute-done.9.refs_3_), channel_id=1, source_target_pairs={{0,16},{1,17},{2,18},{3,19},{4,20},{5,21},{6,22},{7,23},{8,24},{9,... | collective-permute-start | bytes 3145736 | tf_op jit(solution)/shard_map/ppermute | solution.py:285
  252.8 2.1 copy-start.13
  252.8 10.6 %collective-permute-start.23 = (bf16[16,64,128]{2,1,0:T(8,128)(2,1)}, bf16[16,64,128]{2,1,0:T(8,128)(2,1)S(1)}, u32[]{:S(2)}, u32[]{:S(2)}) collective-permute-start(bf16[16,64,128]{2,1,0:T(8,128)(2,1)} %get-tuple-element.27), channel_id=1, source_target_pairs={{0,1},{1,2},{2,3},{3,4},{4,5},{5,6},{6,7},{7,8},{8,9},{9,10},{10,1... | collective-permute-start | bytes 786440 | tf_op jit(solution)/shard_map/ppermute | solution.py:353
  265.7 258.5 %copy-start.25 = (bf16[256,1024]{1,0:T(8,128)(2,1)S(1)}, bf16[256,1024]{1,0:T(8,128)(2,1)}, u32[]{:S(2)}) copy-start(bf16[256,1024]{1,0:T(8,128)(2,1)} %get-tuple-element.16) | copy-start | bytes 1572868
  265.7 1.0 copy-start.7
  266.7 1.0 copy-start.8
  267.7 1.0 copy-start.9
  524.2 3.3 copy-start.5
  524.2 3.3 copy-start.24
  527.5 2.9 copy-start.23
  554.8 14.2 %copy-start.22 = (bf16[16,64,1024]{2,1,0:T(8,128)(2,1)S(1)}, bf16[16,64,1024]{2,1,0:T(8,128)(2,1)}, u32[]{:S(2)}) copy-start(bf16[16,64,1024]{2,1,0:T(8,128)(2,1)} %get-tuple-element.26) | copy-start | bytes 6291460
  554.8 14.2 %copy-start.26 = (f32[1024]{0:T(1024)S(1)}, f32[1024]{0:T(1024)}, u32[]{:S(2)}) copy-start(f32[1024]{0:T(1024)} %param.14) | copy-start | bytes 12292

commit v3 on v2

--- a/solution.py
+++ b/solution.py
@@ -10,15 +10,14 @@
 CAP = 4
 EPS = 1e-05
 NEG = float("-inf")
-NT = (((1,), (1,)), ((), ()))
-
-
-def ln_kernel(tok_ref, gain_ref, bias_ref, norm_ref, normt_ref):
+TN = (((0,), (1,)), ((), ()))
+
+
+def ln_kernel(tok_ref, gain_ref, bias_ref, normt_ref):
     values = tok_ref[...].astype(jnp.float32)
     center = values - jnp.mean(values, axis=-1, keepdims=True)
     spread = jnp.mean(center * center, axis=-1, keepdims=True)
     normed = center * lax.rsqrt(spread + EPS) * gain_ref[...] + bias_ref[...]
-    norm_ref[...] = normed.astype(jnp.bfloat16)
     normt_ref[...] = jnp.transpose(normed).astype(jnp.bfloat16).reshape(normt_ref.shape)
 
 
@@ -26,10 +25,7 @@
     rows, width = tokens.shape
     return pl.pallas_call(
         ln_kernel,
-        out_shape=(
-            jax.ShapeDtypeStruct((rows, width), jnp.bfloat16),
-            jax.ShapeDtypeStruct((heads, width // heads, rows), jnp.bfloat16),
-        ),
+        out_shape=jax.ShapeDtypeStruct((heads, width // heads, rows), jnp.bfloat16),
         name="layer_norm",
     )(tokens, gain.reshape(1, width), bias.reshape(1, width))
 
@@ -82,101 +78,99 @@
     )(pos, slots)
 
 
-def head_lanes():
-    return lax.broadcasted_iota(jnp.int32, (BLK, BLK), 1) < BLK // 2
-
-
-def near_kernel(q_ref, k_ref, v_ref, mask_ref, acc_ref, top_ref, sum_ref):
-    first = head_lanes()
+def both_heads(qt_pair):
+    half = qt_pair.shape[0] // 2
+    none = jnp.zeros((half, qt_pair.shape[1]), qt_pair.dtype)
+    top = jnp.concatenate([qt_pair[:half], none], axis=1)
+    return jnp.concatenate([top, jnp.concatenate([none, qt_pair[half:]], axis=1)], axis=0)
+
+
+def own_halves(wide):
+    half, cols = wide.shape[0] // 2, wide.shape[1] // 2
+    return jnp.concatenate([wide[:half, :cols], wide[half:, cols:]], axis=0)
+
+
+def spread_rows(row, half):
+    cols = row.shape[1] // 2
+    top = jnp.broadcast_to(row[:, :cols], (half, cols))
+    return jnp.concatenate([top, jnp.broadcast_to(row[:, cols:], (half, cols))], axis=0)
+
+
+def near_kernel(qt_ref, k_ref, vt_ref, mask_ref, acc_ref, top_ref, sum_ref):
     f32 = jnp.float32
     shared = slice(4 * BLK, 5 * BLK)
     for b in range(2):
-        rows = slice(b * BLK, (b + 1) * BLK)
+        cols = slice(b * BLK, (b + 1) * BLK)
         near = slice(b * BLK, (b + 3) * BLK)
-        q_pair = q_ref[rows, :]
-        accs, tops, sums = [], [], []
-        for mine in (first, jnp.logical_not(first)):
-            q = jnp.where(mine, q_pair, jnp.zeros_like(q_pair))
-            s = jnp.dot(q, k_ref[:, near], preferred_element_type=f32) + mask_ref[b]
-            g = jnp.dot(q, k_ref[:, shared], preferred_element_type=f32)
-            top = jnp.maximum(
-                jnp.max(s, axis=-1, keepdims=True), jnp.max(g, axis=-1, keepdims=True)
-            )
-            p = jnp.exp(s - top)
-            pg = jnp.exp(g - top)
-            sums.append(
-                jnp.sum(p, axis=-1, keepdims=True) + jnp.sum(pg, axis=-1, keepdims=True)
-            )
-            tops.append(top)
-            accs.append(
-                lax.dot_general(
-                    p.astype(jnp.bfloat16), v_ref[:, near], NT, preferred_element_type=f32
-                )
-                + lax.dot_general(
-                    pg.astype(jnp.bfloat16), v_ref[:, shared], NT, preferred_element_type=f32
-                )
-            )
-        acc_ref[rows, :] = jnp.where(first, accs[0], accs[1])
-        top_ref[rows, :] = jnp.where(first, tops[0], tops[1])
-        sum_ref[rows, :] = jnp.where(first, sums[0], sums[1])
-
-
-def near_attention(q, k, v, mask):
-    rows, width = q.shape
-    keys = k.shape[1]
-    square = pl.BlockSpec((rows, BLK), lambda i: (0, i))
-    wide = pl.BlockSpec((BLK, keys), lambda i: (i, 0))
-    part = jax.ShapeDtypeStruct((rows, width), jnp.float32)
-    return pl.pallas_call(
-        near_kernel,
-        out_shape=(part, part, part),
-        grid=(width // BLK,),
-        in_specs=[square, wide, wide, pl.BlockSpec(mask.shape, lambda i: (0, 0, 0))],
-        out_specs=(square, square, square),
-        name="near_attention",
-    )(q, k, v, mask)
-
-
-def far_kernel(q_ref, k_ref, v_ref, acc_ref, top_ref, sum_ref, out_ref):
-    first = head_lanes()
+        q = both_heads(qt_ref[:, cols])
+        mask = mask_ref[b]
+        s = jnp.dot(k_ref[near, :], q, preferred_element_type=f32)
+        s = s + jnp.concatenate([mask, mask], axis=1)
+        g = jnp.dot(k_ref[shared, :], q, preferred_element_type=f32)
+        top = jnp.maximum(jnp.max(s, axis=0, keepdims=True), jnp.max(g, axis=0, keepdims=True))
+        p = jnp.exp(s - top)
+        pg = jnp.exp(g - top)
+        total = jnp.sum(p, axis=0, keepdims=True) + jnp.sum(pg, axis=0, keepdims=True)
+        acc = jnp.dot(vt_ref[:, near], p.astype(jnp.bfloat16), preferred_element_type=f32)
+        acc += jnp.dot(vt_ref[:, shared], pg.astype(jnp.bfloat16), preferred_element_type=f32)
+        acc_ref[:, cols] = own_halves(acc)
+        top_ref[0, b] = jnp.broadcast_to(top, top_ref.shape[2:])
+        sum_ref[0, b] = jnp.broadcast_to(total, sum_ref.shape[2:])
+
+
+def far_kernel(qt_ref, k_ref, vt_ref, acc_ref, top_ref, sum_ref, out_ref):
     f32 = jnp.float32
     spread = RAND * BLK
     for b in range(2):
-        rows = slice(b * BLK, (b + 1) * BLK)
+        cols = slice(b * BLK, (b + 1) * BLK)
         far = slice(b * spread, (b + 1) * spread)
-        q_pair = q_ref[rows, :]
-        outs = []
-        for h, mine in enumerate((first, jnp.logical_not(first))):
-            q = jnp.where(mine, q_pair, jnp.zeros_like(q_pair))
-            s2 = jnp.dot(q, k_ref[:, far], preferred_element_type=f32)
-            lane = h * (BLK // 2)
-            old_top = top_ref[rows, lane : lane + 1]
-            top = jnp.maximum(jnp.max(s2, axis=-1, keepdims=True), old_top)
-            p2 = jnp.exp(s2 - top)
-            scale = jnp.exp(old_top - top)
-            total = jnp.sum(p2, axis=-1, keepdims=True)
-            total += sum_ref[rows, lane : lane + 1] * scale
-            acc = lax.dot_general(
-                p2.astype(jnp.bfloat16), v_ref[:, far], NT, preferred_element_type=f32
-            )
-            acc += acc_ref[rows, :] * scale
-            outs.append(acc / total)
-        out_ref[rows, :] = jnp.where(first, outs[0], outs[1]).astype(jnp.bfloat16)
-
-
-def far_attention(q, k, v, parts):
-    rows, width = q.shape
-    keys = k.shape[1]
-    square = pl.BlockSpec((rows, BLK), lambda i: (0, i))
-    wide = pl.BlockSpec((BLK, keys), lambda i: (i, 0))
+        q = both_heads(qt_ref[:, cols])
+        s = jnp.dot(k_ref[far, :], q, preferred_element_type=f32)
+        old_top = top_ref[0, b, :1]
+        top = jnp.maximum(jnp.max(s, axis=0, keepdims=True), old_top)
+        p = jnp.exp(s - top)
+        scale = jnp.exp(old_top - top)
+        total = jnp.sum(p, axis=0, keepdims=True) + sum_ref[0, b, :1] * scale
+        acc = jnp.dot(vt_ref[:, far], p.astype(jnp.bfloat16), preferred_element_type=f32)
+        half = acc.shape[0] // 2
+        acc = own_halves(acc) + acc_ref[:, cols] * spread_rows(scale, half)
+        out_ref[:, cols] = (acc / spread_rows(total, half)).astype(jnp.bfloat16)
+
+
+def pair_specs(rows, keys):
+    tall = pl.BlockSpec((BLK, rows), lambda i: (i, 0))
+    k_spec = pl.BlockSpec((keys, BLK), lambda i: (0, i))
+    vt_spec = pl.BlockSpec((BLK, keys), lambda i: (i, 0))
+    row = pl.BlockSpec((1, rows // BLK, 8, 2 * BLK), lambda i: (i, 0, 0, 0))
+    return tall, k_spec, vt_spec, row
+
+
+def near_attention(qt, k, vt, mask):
+    width, rows = qt.shape
+    pairs = width // BLK
+    tall, k_spec, vt_spec, row = pair_specs(rows, k.shape[0])
+    stat = jax.ShapeDtypeStruct((pairs, rows // BLK, 8, 2 * BLK), jnp.float32)
+    return pl.pallas_call(
+        near_kernel,
+        out_shape=(jax.ShapeDtypeStruct((width, rows), jnp.float32), stat, stat),
+        grid=(pairs,),
+        in_specs=[tall, k_spec, vt_spec, pl.BlockSpec(mask.shape, lambda i: (0, 0, 0))],
+        out_specs=(tall, row, row),
+        name="near_attention",
+    )(qt, k, vt, mask)
+
+
+def far_attention(qt, k, vt, parts):
+    width, rows = qt.shape
+    tall, k_spec, vt_spec, row = pair_specs(rows, k.shape[0])
     return pl.pallas_call(
         far_kernel,
-        out_shape=jax.ShapeDtypeStruct((rows, width), jnp.bfloat16),
+        out_shape=jax.ShapeDtypeStruct((width, rows), jnp.bfloat16),
         grid=(width // BLK,),
-        in_specs=[square, wide, wide, square, square, square],
-        out_specs=square,
+        in_specs=[tall, k_spec, vt_spec, tall, row, row],
+        out_specs=tall,
         name="far_attention",
-    )(q, k, v, *parts)
+    )(qt, k, vt, *parts)
 
 
 def run_copies(copies):
@@ -207,7 +201,7 @@
         piece_kernel,
         out_shape=jax.ShapeDtypeStruct((rows, wt.shape[1] // 2), jnp.bfloat16),
         in_specs=[pl.BlockSpec(memory_space=pltpu.SMEM)] + any_specs(2),
-        out_specs=pl.BlockSpec(memory_space=pl.ANY),
+        out_specs=pl.BlockSpec(memory_space=pltpu.VMEM),
         scratch_shapes=[pltpu.SemaphoreType.DMA((2,))],
         name="own_piece",
     )(core, wt, out_w)
@@ -229,7 +223,7 @@
         join_kernel,
         out_shape=jax.ShapeDtypeStruct((rows,) + parts[0].shape[1:], jnp.bfloat16),
         in_specs=any_specs(len(parts)),
-        out_specs=pl.BlockSpec(memory_space=pl.ANY),
+        out_specs=pl.BlockSpec(memory_space=pltpu.VMEM),
         scratch_shapes=[pltpu.SemaphoreType.DMA((len(parts),))],
         name="join",
     )(*parts)
@@ -266,7 +260,7 @@
         assemble_kernel,
         out_shape=(one,) * 4,
         in_specs=[pl.BlockSpec(memory_space=pltpu.SMEM)] + any_specs(len(parts)),
-        out_specs=tuple(any_specs(4)),
+        out_specs=(pl.BlockSpec(memory_space=pltpu.VMEM),) * 4,
         scratch_shapes=[pltpu.SemaphoreType.DMA((4 * len(parts),))],
         name="assemble",
     )(core, *parts)
@@ -318,7 +312,7 @@
     for b in range(rows // BLK):
         keys = line[b * BLK : (b + 3) * BLK]
         queries = line[(b + 1) * BLK : (b + 2) * BLK]
-        masks.append(jnp.where(queries[:, None] == keys[None, :], 0.0, NEG))
+        masks.append(jnp.where(keys[:, None] == queries[None, :], 0.0, NEG))
     return jnp.stack(masks).astype(jnp.float32)
 
 
@@ -337,7 +331,7 @@
     core = (ctx_index % 2).astype(jnp.int32).reshape(1)
     place = ctx_index * heads + head_index
 
-    normed, normed_t = layer_norm(tokens, ln_gain, ln_bias, heads)
+    normed_t = layer_norm(tokens, ln_gain, ln_bias, heads)
     cells = lax.all_to_all(normed_t, "head", split_axis=0, concat_axis=0, tiled=True)
 
     own = own_piece(core, wt, out_weight)
@@ -345,7 +339,7 @@
 
     shared = jnp.where(place == 0, normed_t[:, :, :BLK], 0).astype(jnp.bfloat16)
     holders = [0]
-    shared, holders = widen(shared, holders, [16 * heads, 8 * heads])
+    shared, holders = widen(shared, holders, [16 * heads, 8 * heads, 4 * heads])
 
     both = ("ctx", "head")
     right = [(i, i + 1) for i in range(devices - 1)]
@@ -371,9 +365,9 @@
     b = join(d2, u3, d3, u4, d4).reshape(shape)
     c = swap(a, 1, devices)
     d = swap(b, 2 * heads + 1, devices)
-    shared, holders = widen(shared, holders, [4 * heads, heads, 2 * heads, 8, 4, 2, 1])
-
-    placed = place_blocks(tied(take, c, d, shared), slots, heads)
+    shared, holders = widen(shared, holders, [heads, 2 * heads, 8, 4, 2, 1])
+
+    placed = place_blocks(tied(take, c, d, shared, before, after), slots, heads)
     far = lax.all_to_all(placed, "head", split_axis=0, concat_axis=0, tiled=True)
     far = far.reshape(width, far.shape[2])
 
@@ -386,19 +380,20 @@
 
     f32 = jnp.float32
     bf16 = jnp.bfloat16
-    w_q, w_k, w_v, w_o = (
-        w.reshape(width, width)
-        for w in assemble(core, mine + other, heads)
+    weights = assemble(core, mine + other, heads)
+    w_q, w_k, w_v, w_o = (w.reshape(width, width) for w in weights)
+    own_t = normed_t.reshape(width, rows)
+    qt = jnp.dot(w_q, own_t, preferred_element_type=f32).astype(bf16)
+    qt = (qt.astype(f32) * hd**-0.5).astype(bf16)
+    k_near = lax.dot_general(near, w_k, TN, preferred_element_type=f32).astype(bf16)
+    vt_near = jnp.dot(w_v, near, preferred_element_type=f32).astype(bf16)
+    parts = near_attention(qt, k_near, vt_near, mask)
+    k_far = lax.dot_general(far, w_k, TN, preferred_element_type=f32).astype(bf16)
+    vt_far = jnp.dot(w_v, far, preferred_element_type=f32).astype(bf16)
+    attended = far_attention(qt, k_far, vt_far, parts)
+    projected = lax.dot_general(
+        attended, w_o, (((0,), (0,)), ((), ())), preferred_element_type=f32
     )
-    q = lax.dot_general(normed, w_q, NT, preferred_element_type=f32)
-    q = (q.astype(bf16).astype(f32) * hd**-0.5).astype(bf16)
-    k_near = jnp.dot(w_k, near, preferred_element_type=f32).astype(bf16)
-    v_near = jnp.dot(w_v, near, preferred_element_type=f32).astype(bf16)
-    parts = near_attention(q, k_near, v_near, mask)
-    k_far = jnp.dot(w_k, far, preferred_element_type=f32).astype(bf16)
-    v_far = jnp.dot(w_v, far, preferred_element_type=f32).astype(bf16)
-    attended = far_attention(q, k_far, v_far, parts)
-    projected = jnp.dot(attended, w_o, preferred_element_type=f32)
     return (projected + out_bias).astype(bf16)
 
 

time: 579 us -> 213 us (0.37); the launches traced: 572 us -> 211 us
  Pallas kernels: 366 us -> 42 us
  starting transfers between devices: 125 us -> 95.3 us
  waiting for transfers between devices: 39.2 us -> 33.3 us
    pallas_call x1, Pallas kernels: 255 us -> 6.91 us  [assemble(): pl.pallas_call(assemble_kernel, out_shape=(one,) * 4, in_specs=[pl.BlockS...]
    pallas_call x2, Pallas kernels: 65.8 us -> 4.38 us  [join(): pl.pallas_call(join_kernel, out_shape=jax.ShapeDtypeStruct((rows,) + part...]
    ppermute x6, starting transfers between devices: 57.4 us -> 24.9 us  [swap(): lax.ppermute(value, ('ctx', 'head'), [(i, i ^ bits) for i in range(device...]
    ppermute x1, waiting for transfers between devices: 12.1 us -> 0.01 us  [per_device(): after = lax.ppermute(normed_t[:, :, :BLK], both, left)]
    ppermute x9, waiting for transfers between devices: 11.4 us -> 22.7 us  [widen(): value = value + lax.ppermute(value, ('ctx', 'head'), hop)]
    ppermute x1, waiting for transfers between devices: 7.62 us -> 0.01 us  [per_device(): before = lax.ppermute(normed_t[:, :, rows - BLK:], both, right)]
    pallas_call x1, Pallas kernels: 9.06 us -> 1.64 us  [own_piece(): pl.pallas_call(piece_kernel, out_shape=jax.ShapeDtypeStruct((rows, wt.sha...]
    pallas_call x3, Pallas kernels: 28.9 us -> 22.1 us  [the longest x1 10 us: near_attention(): pl.pallas_call(near_kernel, out_shape=(jax.ShapeDtypeStruct((width, rows)...]
  transfers between devices with their start and end apart: 28 -> 28, of which waited for: 9 -> 4; matrix products, arithmetic and copies ran while one was open for 4% -> 10% of each run, Pallas kernels for 60% -> 11%
where the time goes in v3:
time: 213 us; the launch traced here: 211 us
  starting transfers between devices  95.3 us (45%)
  Pallas kernels  42 us (20%)
  waiting for transfers between devices  33.3 us (16%)
  matrix products  20.8 us (10%)
  other arithmetic  9.99 us (5%)
  local copies, waits for them, and re-layouts  9.55 us (4%)
    ppermute x8, starting transfers between devices, shift(): return lax.ppermute(value, 'head', pairs)  25.9 us
    ppermute x6, starting transfers between devices, swap(): lax.ppermute(value, ('ctx', 'head'), [(i, i ^ bits) for i in range(device...  24.9 us
    ppermute x9, waiting for transfers between devices, widen(): value = value + lax.ppermute(value, ('ctx', 'head'), hop)  22.7 us
    all_to_all x1, starting transfers between devices, per_device(): lax.all_to_all(outgoing, 'ctx', split_axis=0, concat_axis=0, tiled=True)  14.4 us
    ppermute x8, waiting for transfers between devices, shift(): return lax.ppermute(value, 'head', pairs)  10.5 us
    pallas_call x1, Pallas kernels, near_attention(): pl.pallas_call(near_kernel, out_shape=(jax.ShapeDtypeStruct((width, rows)...  10 us
    pallas_call x1, Pallas kernels, far_attention(): pl.pallas_call(far_kernel, out_shape=jax.ShapeDtypeStruct((width, rows),...  9.81 us
    all_to_all x1, starting transfers between devices, per_device(): lax.all_to_all(normed_t, 'head', split_axis=0, concat_axis=0, tiled=True)  8.15 us
  transfers between devices with their start and end apart: 28, of which 4 were waited for; matrix products, arithmetic and copies ran while one was open for 10% of the time, Pallas kernels for 11%

profile of v3, /device:TPU:7, one launch (start us, length us, event | category | flops | bytes accessed | tf_op | source)
XLA Modules:
  0.0 211.5 jit_solution(3732877352292951288)
XLA Ops:
  0.0 2.3 %layer_norm.1 = bf16[16,64,256]{2,1,0:T(8,128)(2,1)} custom-call(bf16[256,1024]{1,0:T(8,128)(2,1)} %tok_ref.1, f32[1,1024]{1,0:T(1,128)} %bitcast.49, f32[1,1024]{1,0:T(1,128)} %bitcast.50), custom_call_target="tpu_custom_call" | custom-call | tf_op jit(solution)/shard_map/layer_norm/pallas_call | solution.py:26
  2.3 8.1 %all-to-all-start = ((bf16[16,64,256]{2,1,0:T(8,128)(2,1)}), bf16[16,64,256]{2,1,0:T(8,128)(2,1)S(1)}, u32[]{:S(2)}, u32[]{:S(2)}) async-start(bf16[16,64,256]{2,1,0:T(8,128)(2,1)} %layer_norm.1), calls=%async_computation | async-start | bytes 1048576 | tf_op jit(solution)/shard_map/all_to_all | solution.py:335
  10.5 1.9 fusion.5
  12.4 0.7 collective-permute-start.14
  13.1 0.7 collective-permute-start.15
  13.8 1.6 own_piece.1.refs_0_
  15.5 3.1 %collective-permute-start = (bf16[256,512]{1,0:T(8,128)(2,1)}, bf16[256,512]{1,0:T(8,128)(2,1)S(1)}, u32[]{:S(2)}, u32[]{:S(2)}) collective-permute-start(bf16[256,512]{1,0:T(8,128)(2,1)} %own_piece.1.refs_0_), channel_id=1, source_target_pairs={{0,2},{1,3},{2,4},{3,5},{4,6},{5,7},{6,8},{7,9},{8,10},{9,11},{10,... | collective-permute-start | bytes 786440 | tf_op jit(solution)/shard_map/ppermute | solution.py:275
  18.6 3.4 %collective-permute-start.1 = (bf16[256,512]{1,0:T(8,128)(2,1)}, bf16[256,512]{1,0:T(8,128)(2,1)S(1)}, u32[]{:S(2)}, u32[]{:S(2)}) collective-permute-start(bf16[256,512]{1,0:T(8,128)(2,1)} %own_piece.1.refs_0_), channel_id=1, source_target_pairs={{0,14},{1,15},{2,0},{3,1},{4,2},{5,3},{6,4},{7,5},{8,6},{9,7},{10,... | collective-permute-start | bytes 786440 | tf_op jit(solution)/shard_map/ppermute | solution.py:275
  22.6 0.7 collective-permute-start.16
  23.8 0.6 convert_reduce_fusion.1
  24.7 0.7 reshape.198.ids_ref
  25.5 4.7 %collective-permute-done.refs_1_ = bf16[256,512]{1,0:T(8,128)(2,1)S(1)} collective-permute-done((bf16[256,512]{1,0:T(8,128)(2,1)}, bf16[256,512]{1,0:T(8,128)(2,1)S(1)}, u32[]{:S(2)}, u32[]{:S(2)}) %collective-permute-start) | collective-permute-done | bytes 262176 | tf_op jit(solution)/shard_map/ppermute | solution.py:275
  30.2 0.8 copy-done.5
  31.0 3.7 %pick_blocks.1 = bf16[128,64,128]{2,1,0:T(8,128)(2,1)} custom-call(s32[128]{0:T(128)} %reshape.198.ids_ref, bf16[16,64,256]{2,1,0:T(8,128)(2,1)} %copy-done.5), custom_call_target="tpu_custom_call" | custom-call | tf_op jit(solution)/shard_map/pick_blocks/pallas_call | solution.py:44
  34.7 14.4 %all-to-all-start.1 = ((bf16[32,256,128]{2,1,0:T(8,128)(2,1)}), bf16[32,256,128]{2,1,0:T(8,128)(2,1)S(1)}, u32[]{:S(2)}, u32[]{:S(2)}) async-start(bf16[32,256,128]{2,1,0:T(8,128)(2,1)} %bitcast.38), calls=%async_computation.1 | async-start | bytes 4194304 | tf_op jit(solution)/shard_map/all_to_all | solution.py:356
  49.2 1.9 collective-permute-start.2
  51.1 4.6 %collective-permute-start.3 = (bf16[256,512]{1,0:T(8,128)(2,1)S(1)}, bf16[256,512]{1,0:T(8,128)(2,1)S(1)}, u32[]{:S(2)}, u32[]{:S(2)}) collective-permute-start(bf16[256,512]{1,0:T(8,128)(2,1)S(1)} %collective-permute-done.1.refs_2_), channel_id=1, source_target_pairs={{0,14},{1,15},{2,0},{3,1},{4,2},{5,3},{6,4},{7,5},{8,6},{9,7},{10,... | collective-permute-start | bytes 786440 | tf_op jit(solution)/shard_map/ppermute | solution.py:275
  55.7 0.7 collective-permute-start.17
  56.4 3.4 %collective-permute-done.2.refs_3_ = bf16[256,512]{1,0:T(8,128)(2,1)S(1)} collective-permute-done((bf16[256,512]{1,0:T(8,128)(2,1)S(1)}, bf16[256,512]{1,0:T(8,128)(2,1)S(1)}, u32[]{:S(2)}, u32[]{:S(2)}) %collective-permute-start.2) | collective-permute-done | bytes 262176 | tf_op jit(solution)/shard_map/ppermute | solution.py:275
  59.7 1.9 collective-permute-start.4
  61.7 4.6 %collective-permute-start.5 = (bf16[256,512]{1,0:T(8,128)(2,1)S(1)}, bf16[256,512]{1,0:T(8,128)(2,1)S(1)}, u32[]{:S(2)}, u32[]{:S(2)}) collective-permute-start(bf16[256,512]{1,0:T(8,128)(2,1)S(1)} %collective-permute-done.3.refs_0_), channel_id=1, source_target_pairs={{0,14},{1,15},{2,0},{3,1},{4,2},{5,3},{6,4},{7,5},{8,6},{9,7},{10,... | collective-permute-start | bytes 786440 | tf_op jit(solution)/shard_map/ppermute | solution.py:275
  66.4 0.7 collective-permute-start.18
  67.0 2.4 %collective-permute-done.4.refs_1_ = bf16[256,512]{1,0:T(8,128)(2,1)S(1)} collective-permute-done((bf16[256,512]{1,0:T(8,128)(2,1)S(1)}, bf16[256,512]{1,0:T(8,128)(2,1)S(1)}, u32[]{:S(2)}, u32[]{:S(2)}) %collective-permute-start.4) | collective-permute-done | bytes 262176 | tf_op jit(solution)/shard_map/ppermute | solution.py:275
  69.5 0.7 slice.42
  70.2 1.9 collective-permute-start.6
  72.1 0.7 slice.43
  72.8 4.6 %collective-permute-start.7 = (bf16[128,512]{1,0:T(8,128)(2,1)}, bf16[128,512]{1,0:T(8,128)(2,1)}, u32[]{:S(2)}, u32[]{:S(2)}) collective-permute-start(bf16[128,512]{1,0:T(8,128)(2,1)} %slice.43), channel_id=1, source_target_pairs={{0,14},{1,15},{2,0},{3,1},{4,2},{5,3},{6,4},{7,5},{8,6},{9,7},{10,... | collective-permute-start | bytes 393224 | tf_op jit(solution)/shard_map/ppermute | solution.py:275
  77.5 1.4 collective-permute-start.19
  78.9 2.2 %join.2 = bf16[1024,512]{1,0:T(8,128)(2,1)} custom-call(bf16[256,512]{1,0:T(8,128)(2,1)} %own_piece.1.refs_0_, bf16[256,512]{1,0:T(8,128)(2,1)} %copy-done.13, bf16[256,512]{1,0:T(8,128)(2,1)} %copy-done.14, bf16[256,512]{1,0:T(8,128)(2,1)} %copy-done.16), custom_call_target="tpu_custom_call" | custom-call | tf_op jit(solution)/shard_map/join/pallas_call | solution.py:222
  81.1 11.4 %collective-permute-start.8 = (bf16[4,256,512]{2,1,0:T(8,128)(2,1)}, bf16[4,256,512]{2,1,0:T(8,128)(2,1)S(1)}, u32[]{:S(2)}, u32[]{:S(2)}) collective-permute-start(bf16[4,256,512]{2,1,0:T(8,128)(2,1)} %bitcast.39), channel_id=1, source_target_pairs={{0,1},{1,0},{2,3},{3,2},{4,5},{5,4},{6,7},{7,6},{8,9},{9,8},{10,11... | collective-permute-start | bytes 3145736 | tf_op jit(solution)/shard_map/ppermute | solution.py:279
  92.6 0.7 copy-done.17
  93.3 2.2 %join.3 = bf16[1024,512]{1,0:T(8,128)(2,1)} custom-call(bf16[256,512]{1,0:T(8,128)(2,1)} %copy-done.15, bf16[256,512]{1,0:T(8,128)(2,1)} %copy-done.11, bf16[256,512]{1,0:T(8,128)(2,1)} %copy-done.12, bf16[128,512]{1,0:T(8,128)(2,1)} %copy-done.17, bf16[128,512]{1,0:T(8,128)(2,1)} %collective-permute-done.7.refs_4_), custom_call_target="tpu_custom_call" | custom-call | tf_op jit(solution)/shard_map/join/pallas_call | solution.py:222
  95.5 3.2 %collective-permute-start.9 = (bf16[4,256,512]{2,1,0:T(8,128)(2,1)}, bf16[4,256,512]{2,1,0:T(8,128)(2,1)}, u32[]{:S(2)}, u32[]{:S(2)}) collective-permute-start(bf16[4,256,512]{2,1,0:T(8,128)(2,1)} %bitcast.42), channel_id=1, source_target_pairs={{0,33},{1,32},{2,35},{3,34},{4,37},{5,36},{6,39},{7,38},{8,41},{9,... | collective-permute-start | bytes 3145736 | tf_op jit(solution)/shard_map/ppermute | solution.py:279
  98.7 1.0 add.69
  99.7 0.7 collective-permute-start.20
  100.5 1.4 collective-permute-start.21
  101.8 1.9 collective-permute-start.23
  103.7 7.3 %collective-permute-start.24 = (bf16[16,64,128]{2,1,0:T(8,128)(2,1)}, bf16[16,64,128]{2,1,0:T(8,128)(2,1)}, u32[]{:S(2)}, u32[]{:S(2)}) collective-permute-start(bf16[16,64,128]{2,1,0:T(8,128)(2,1)} %get-tuple-element.23), channel_id=1, source_target_pairs={{1,0},{2,1},{3,2},{4,3},{5,4},{6,5},{7,6},{8,7},{9,8},{10,9},{11,1... | collective-permute-start | bytes 786440 | tf_op jit(solution)/shard_map/ppermute | solution.py:348
  111.1 1.0 add.71
  112.1 1.3 collective-permute-start.22
  113.6 0.5 multiply_add_fusion.pos_ref
  114.1 22.7 %collective-permute-done.22 = bf16[16,64,128]{2,1,0:T(8,128)(2,1)S(1)} collective-permute-done((bf16[16,64,128]{2,1,0:T(8,128)(2,1)S(1)}, bf16[16,64,128]{2,1,0:T(8,128)(2,1)S(1)}, u32[]{:S(2)}, u32[]{:S(2)}) %collective-permute-start.22) | collective-permute-done | bytes 262176 | tf_op jit(solution)/shard_map/ppermute | solution.py:285
  136.9 0.9 copy-done.7
  137.9 0.7 copy-done.1
  138.6 3.2 %place_blocks.1 = bf16[16,64,768]{2,1,0:T(8,128)(2,1)} custom-call(s32[96]{0:T(128)} %multiply_add_fusion.pos_ref, bf16[128,64,128]{2,1,0:T(8,128)(2,1)} %bitcast.37), custom_call_target="tpu_custom_call" | custom-call | tf_op jit(solution)/shard_map/place_blocks/pallas_call | solution.py:69
  141.8 4.6 %all-to-all-start.2 = ((bf16[16,64,768]{2,1,0:T(8,128)(2,1)}), bf16[16,64,768]{2,1,0:T(8,128)(2,1)}, u32[]{:S(2)}, u32[]{:S(2)}) async-start(bf16[16,64,768]{2,1,0:T(8,128)(2,1)} %place_blocks.1), calls=%async_computation.2 | async-start | bytes 3145728 | tf_op jit(solution)/shard_map/all_to_all | solution.py:371
  147.3 3.8 %collective-permute-start.10 = (bf16[4,256,512]{2,1,0:T(8,128)(2,1)S(1)}, bf16[4,256,512]{2,1,0:T(8,128)(2,1)S(1)}, u32[]{:S(2)}, u32[]{:S(2)}) collective-permute-start(bf16[4,256,512]{2,1,0:T(8,128)(2,1)S(1)} %bitcast.41), channel_id=1, source_target_pairs={{0,16},{1,17},{2,18},{3,19},{4,20},{5,21},{6,22},{7,23},{8,24},{9,... | collective-permute-start | bytes 3145736 | tf_op jit(solution)/shard_map/ppermute | solution.py:279
  151.2 1.9 collective-permute-start.11
  153.1 2.4 %collective-permute-start.12 = (bf16[4,256,512]{2,1,0:T(8,128)(2,1)}, bf16[4,256,512]{2,1,0:T(8,128)(2,1)S(1)}, u32[]{:S(2)}, u32[]{:S(2)}) collective-permute-start(bf16[4,256,512]{2,1,0:T(8,128)(2,1)} %copy-done.7), channel_id=1, source_target_pairs={{0,16},{1,17},{2,18},{3,19},{4,20},{5,21},{6,22},{7,23},{8,24},{9,... | collective-permute-start | bytes 3145736 | tf_op jit(solution)/shard_map/ppermute | solution.py:279
  155.5 2.1 collective-permute-start.13
  157.8 0.8 pad_maximum_fusion.1.mask_ref
  158.6 2.3 %pad_maximum_fusion = bf16[16,64,640]{2,1,0:T(8,128)(2,1)} fusion(bf16[16,64,128]{2,1,0:T(8,128)(2,1)S(1)} %add.72, bf16[16,64,128]{2,1,0:T(8,128)(2,1)} %collective-permute-done.24, bf16[16,64,256]{2,1,0:T(8,128)(2,1)S(1)} %copy-done, bf16[16,64,128]{2,1,0:T(8,128)(2,1)} %collective-permute-done.23), kind=kLoop, calls=%fused_computation.7 | loop fusion | flops 5242880 | bytes 2621440 | tf_op jit(solution)/shard_map/concatenate | solution.py:376
  161.0 1.0 copy-done.8
  162.0 1.0 copy-done.9
  163.0 1.0 copy-done.10
  163.9 6.9 %assemble.1 = (bf16[16,64,1024]{2,1,0:T(8,128)(2,1)}, bf16[16,64,1024]{2,1,0:T(8,128)(2,1)}, bf16[16,64,1024]{2,1,0:T(8,128)(2,1)}, bf16[16,64,1024]{2,1,0:T(8,128)(2,1)}) custom-call(s32[1]{0:T(128)} %bitcast.core_ref, bf16[4,256,512]{2,1,0:T(8,128)(2,1)} %bitcast.40, bf16[4,256,512]{2,1,0:T(8,128)(2,1)} %bitcast.43, bf16[4,256,512]{2,1,0:T(8,128)(2,1)} %copy-done.7, ...), custom_call_target="tpu_custom_call" | custom-call | tf_op jit(solution)/shard_map/assemble/pallas_call | solution.py:259
  170.9 3.2 %fusion.2.qt_ref = bf16[1024,256]{1,0:T(8,128)(2,1)} fusion(bf16[1024,1024]{1,0:T(8,128)(2,1)} %bitcast.56, bf16[1024,256]{1,0:T(8,128)(2,1)S(1)} %bitcast.36), kind=kOutput, calls=%fused_computation.11 | convolution fusion | flops 537919488 | bytes 3145728 | tf_op jit(solution)/shard_map/dot_general | solution.py:386
  174.1 2.6 %convolution_convert_fusion.3.k_ref = bf16[640,1024]{1,0:T(8,128)(2,1)} fusion(bf16[1024,640]{1,0:T(8,128)(2,1)S(1)} %bitcast.46, bf16[1024,1024]{1,0:T(8,128)(2,1)S(1)} %bitcast.55), kind=kOutput, calls=%fused_computation.4 | convolution fusion | flops 1342832640 | bytes 4718592 | tf_op jit(solution)/shard_map/dot_general | solution.py:388
  176.8 2.9 %convolution_convert_fusion.2.vt_ref = bf16[1024,640]{1,0:T(8,128)(2,1)} fusion(bf16[1024,1024]{1,0:T(8,128)(2,1)S(1)} %bitcast.52, bf16[1024,640]{1,0:T(8,128)(2,1)S(1)} %bitcast.47), kind=kOutput, calls=%fused_computation.3 | convolution fusion | flops 1342832640 | bytes 4718592 | tf_op jit(solution)/shard_map/dot_general | solution.py:389
  179.7 10.0 %near_attention.1 = (f32[1024,256]{1,0:T(8,128)}, f32[8,2,8,256]{3,2,1,0:T(8,128)}, f32[8,2,8,256]{3,2,1,0:T(8,128)}) custom-call(bf16[1024,256]{1,0:T(8,128)(2,1)} %fusion.2.qt_ref, bf16[640,1024]{1,0:T(8,128)(2,1)} %convolution_convert_fusion.3.k_ref, bf16[1024,640]{1,0:T(8,128)(2,1)} %convolution_convert_fusion.2.vt_ref, ...), custom_call_target="tpu_custom_call" | custom-call | tf_op jit(solution)/shard_map/near_attention/pallas_call | solution.py:153
  189.7 5.1 %convolution_convert_fusion.1.k_ref = bf16[768,1024]{1,0:T(8,128)(2,1)} fusion(bf16[1024,768]{1,0:T(8,128)(2,1)} %bitcast.12, bf16[1024,1024]{1,0:T(8,128)(2,1)} %bitcast.54), kind=kOutput, calls=%fused_computation.2 | convolution fusion | flops 1611399168 | bytes 5242880 | tf_op jit(solution)/shard_map/dot_general | solution.py:391
  194.7 4.3 %convolution_convert_fusion.vt_ref = bf16[1024,768]{1,0:T(8,128)(2,1)} fusion(bf16[1024,1024]{1,0:T(8,128)(2,1)S(1)} %bitcast.53, bf16[1024,768]{1,0:T(8,128)(2,1)} %bitcast.12), kind=kOutput, calls=%fused_computation.1 | convolution fusion | flops 1611399168 | bytes 5242880 | tf_op jit(solution)/shard_map/dot_general | solution.py:392
  199.1 9.8 %far_attention.1 = bf16[1024,256]{1,0:T(8,128)(2,1)} custom-call(bf16[1024,256]{1,0:T(8,128)(2,1)} %fusion.2.qt_ref, bf16[768,1024]{1,0:T(8,128)(2,1)} %convolution_convert_fusion.1.k_ref, bf16[1024,768]{1,0:T(8,128)(2,1)} %convolution_convert_fusion.vt_ref, f32[1024,256]{1,0:T(8,128)} %get-tuple-element.19.acc_ref, ...), custom_call_target="tpu_custom_call" | custom-call | tf_op jit(solution)/shard_map/far_attention/pallas_call | solution.py:166
  208.9 2.6 %fusion.3 = bf16[256,1024]{1,0:T(8,128)(2,1)} fusion(bf16[1024,256]{1,0:T(8,128)(2,1)} %far_attention.1, bf16[1024,1024]{1,0:T(8,128)(2,1)S(1)} %bitcast.45, f32[1024]{0:T(1024)S(1)} %copy-done.18), kind=kOutput, calls=%fused_computation.12 | convolution fusion | flops 537395200 | bytes 3149824 | tf_op jit(solution)/shard_map/dot_general | solution.py:394
  (93 shorter events, 3.2 us)
Async XLA Ops:
  2.3 19.7 %copy-start.19 = (s32[1024,3]{0,1:T(4,128)S(1)}, s32[1024,3]{0,1:T(4,128)}, u32[]{:S(2)}) copy-start(s32[1024,3]{0,1:T(4,128)} %param.16) | copy-start | bytes 36868
  2.3 27.9 %all-to-all-start = ((bf16[16,64,256]{2,1,0:T(8,128)(2,1)}), bf16[16,64,256]{2,1,0:T(8,128)(2,1)S(1)}, u32[]{:S(2)}, u32[]{:S(2)}) async-start(bf16[16,64,256]{2,1,0:T(8,128)(2,1)} %layer_norm.1), calls=%async_computation | async-start | bytes 1048576 | tf_op jit(solution)/shard_map/all_to_all | solution.py:335
  10.5 12.8 %copy-start.20 = (s32[1024,3]{0,1:T(4,128)S(1)}, s32[1024,3]{0,1:T(4,128)}, u32[]{:S(2)}) copy-start(s32[1024,3]{0,1:T(4,128)} %param.17) | copy-start | bytes 36868
  12.4 0.7 collective-permute-start.14
  13.1 9.4 %collective-permute-start.15 = (bf16[16,64,128]{2,1,0:T(8,128)(2,1)S(1)}, bf16[16,64,128]{2,1,0:T(8,128)(2,1)S(1)}, u32[]{:S(2)}, u32[]{:S(2)}) collective-permute-start(bf16[16,64,128]{2,1,0:T(8,128)(2,1)S(1)} %add.64), channel_id=1, source_target_pairs={{0,128},{256,384}} | collective-permute-start | bytes 786440 | tf_op jit(solution)/shard_map/ppermute | solution.py:285
  15.5 14.7 %collective-permute-start = (bf16[256,512]{1,0:T(8,128)(2,1)}, bf16[256,512]{1,0:T(8,128)(2,1)S(1)}, u32[]{:S(2)}, u32[]{:S(2)}) collective-permute-start(bf16[256,512]{1,0:T(8,128)(2,1)} %own_piece.1.refs_0_), channel_id=1, source_target_pairs={{0,2},{1,3},{2,4},{3,5},{4,6},{5,7},{6,8},{7,9},{8,10},{9,11},{10,... | collective-permute-start | bytes 786440 | tf_op jit(solution)/shard_map/ppermute | solution.py:275
  18.6 11.6 %collective-permute-start.1 = (bf16[256,512]{1,0:T(8,128)(2,1)}, bf16[256,512]{1,0:T(8,128)(2,1)S(1)}, u32[]{:S(2)}, u32[]{:S(2)}) collective-permute-start(bf16[256,512]{1,0:T(8,128)(2,1)} %own_piece.1.refs_0_), channel_id=1, source_target_pairs={{0,14},{1,15},{2,0},{3,1},{4,2},{5,3},{6,4},{7,5},{8,6},{9,7},{10,... | collective-permute-start | bytes 786440 | tf_op jit(solution)/shard_map/ppermute | solution.py:275
  22.6 2.8 %collective-permute-start.16 = (bf16[16,64,128]{2,1,0:T(8,128)(2,1)S(1)}, bf16[16,64,128]{2,1,0:T(8,128)(2,1)S(1)}, u32[]{:S(2)}, u32[]{:S(2)}) collective-permute-start(bf16[16,64,128]{2,1,0:T(8,128)(2,1)S(1)} %add.65), channel_id=1, source_target_pairs={{0,64},{256,320},{128,192},{384,448}} | collective-permute-start | bytes 786440 | tf_op jit(solution)/shard_map/ppermute | solution.py:285
  30.2 48.8 %copy-start.13 = (bf16[256,512]{1,0:T(8,128)(2,1)}, bf16[256,512]{1,0:T(8,128)(2,1)S(1)}, u32[]{:S(2)}) copy-start(bf16[256,512]{1,0:T(8,128)(2,1)S(1)} %collective-permute-done.refs_1_) | copy-start | bytes 786436
  30.2 48.8 %copy-start.14 = (bf16[256,512]{1,0:T(8,128)(2,1)}, bf16[256,512]{1,0:T(8,128)(2,1)S(1)}, u32[]{:S(2)}) copy-start(bf16[256,512]{1,0:T(8,128)(2,1)S(1)} %collective-permute-done.1.refs_2_) | copy-start | bytes 786436
  30.2 0.8 copy-start.5
  34.7 102.2 %all-to-all-start.1 = ((bf16[32,256,128]{2,1,0:T(8,128)(2,1)}), bf16[32,256,128]{2,1,0:T(8,128)(2,1)S(1)}, u32[]{:S(2)}, u32[]{:S(2)}) async-start(bf16[32,256,128]{2,1,0:T(8,128)(2,1)} %bitcast.38), calls=%async_computation.1 | async-start | bytes 4194304 | tf_op jit(solution)/shard_map/all_to_all | solution.py:356
  49.2 10.6 %collective-permute-start.2 = (bf16[256,512]{1,0:T(8,128)(2,1)S(1)}, bf16[256,512]{1,0:T(8,128)(2,1)S(1)}, u32[]{:S(2)}, u32[]{:S(2)}) collective-permute-start(bf16[256,512]{1,0:T(8,128)(2,1)S(1)} %collective-permute-done.refs_1_), channel_id=1, source_target_pairs={{0,2},{1,3},{2,4},{3,5},{4,6},{5,7},{6,8},{7,9},{8,10},{9,11},{10,... | collective-permute-start | bytes 786440 | tf_op jit(solution)/shard_map/ppermute | solution.py:275
  51.1 10.6 %collective-permute-start.3 = (bf16[256,512]{1,0:T(8,128)(2,1)S(1)}, bf16[256,512]{1,0:T(8,128)(2,1)S(1)}, u32[]{:S(2)}, u32[]{:S(2)}) collective-permute-start(bf16[256,512]{1,0:T(8,128)(2,1)S(1)} %collective-permute-done.1.refs_2_), channel_id=1, source_target_pairs={{0,14},{1,15},{2,0},{3,1},{4,2},{5,3},{6,4},{7,5},{8,6},{9,7},{10,... | collective-permute-start | bytes 786440 | tf_op jit(solution)/shard_map/ppermute | solution.py:275
  55.7 10.6 %collective-permute-start.17 = (bf16[16,64,128]{2,1,0:T(8,128)(2,1)S(1)}, bf16[16,64,128]{2,1,0:T(8,128)(2,1)S(1)}, u32[]{:S(2)}, u32[]{:S(2)}) collective-permute-start(bf16[16,64,128]{2,1,0:T(8,128)(2,1)S(1)} %add.66), channel_id=1, source_target_pairs={{0,16},{256,272},{128,144},{384,400},{64,80},{320,336},{192,208},{... | collective-permute-start | bytes 786440 | tf_op jit(solution)/shard_map/ppermute | solution.py:285
  59.7 17.8 %copy-start.16 = (bf16[256,512]{1,0:T(8,128)(2,1)}, bf16[256,512]{1,0:T(8,128)(2,1)S(1)}, u32[]{:S(2)}) copy-start(bf16[256,512]{1,0:T(8,128)(2,1)S(1)} %collective-permute-done.2.refs_3_) | copy-start | bytes 786436
  59.7 9.7 %collective-permute-start.4 = (bf16[256,512]{1,0:T(8,128)(2,1)S(1)}, bf16[256,512]{1,0:T(8,128)(2,1)S(1)}, u32[]{:S(2)}, u32[]{:S(2)}) collective-permute-start(bf16[256,512]{1,0:T(8,128)(2,1)S(1)} %collective-permute-done.2.refs_3_), channel_id=1, source_target_pairs={{0,2},{1,3},{2,4},{3,5},{4,6},{5,7},{6,8},{7,9},{8,10},{9,11},{10,... | collective-permute-start | bytes 786440 | tf_op jit(solution)/shard_map/ppermute | solution.py:275
  61.7 15.8 %copy-start.15 = (bf16[256,512]{1,0:T(8,128)(2,1)}, bf16[256,512]{1,0:T(8,128)(2,1)S(1)}, u32[]{:S(2)}) copy-start(bf16[256,512]{1,0:T(8,128)(2,1)S(1)} %collective-permute-done.3.refs_0_) | copy-start | bytes 786436
  61.7 10.4 %collective-permute-start.5 = (bf16[256,512]{1,0:T(8,128)(2,1)S(1)}, bf16[256,512]{1,0:T(8,128)(2,1)S(1)}, u32[]{:S(2)}, u32[]{:S(2)}) collective-permute-start(bf16[256,512]{1,0:T(8,128)(2,1)S(1)} %collective-permute-done.3.refs_0_), channel_id=1, source_target_pairs={{0,14},{1,15},{2,0},{3,1},{4,2},{5,3},{6,4},{7,5},{8,6},{9,7},{10,... | collective-permute-start | bytes 786440 | tf_op jit(solution)/shard_map/ppermute | solution.py:275
  66.4 11.1 %collective-permute-start.18 = (bf16[16,64,128]{2,1,0:T(8,128)(2,1)S(1)}, bf16[16,64,128]{2,1,0:T(8,128)(2,1)S(1)}, u32[]{:S(2)}, u32[]{:S(2)}) collective-permute-start(bf16[16,64,128]{2,1,0:T(8,128)(2,1)S(1)} %add.67), channel_id=1, source_target_pairs={{0,32},{256,288},{128,160},{384,416},{64,96},{320,352},{192,224},{... | collective-permute-start | bytes 786440 | tf_op jit(solution)/shard_map/ppermute | solution.py:285
  69.5 8.1 %copy-start.11 = (bf16[256,512]{1,0:T(8,128)(2,1)}, bf16[256,512]{1,0:T(8,128)(2,1)S(1)}, u32[]{:S(2)}) copy-start(bf16[256,512]{1,0:T(8,128)(2,1)S(1)} %collective-permute-done.4.refs_1_) | copy-start | bytes 786436
  70.2 22.4 %collective-permute-start.6 = (bf16[128,512]{1,0:T(8,128)(2,1)}, bf16[128,512]{1,0:T(8,128)(2,1)S(1)}, u32[]{:S(2)}, u32[]{:S(2)}) collective-permute-start(bf16[128,512]{1,0:T(8,128)(2,1)} %slice.42), channel_id=1, source_target_pairs={{0,2},{1,3},{2,4},{3,5},{4,6},{5,7},{6,8},{7,9},{8,10},{9,11},{10,... | collective-permute-start | bytes 393224 | tf_op jit(solution)/shard_map/ppermute | solution.py:275
  72.1 5.4 %copy-start.12 = (bf16[256,512]{1,0:T(8,128)(2,1)}, bf16[256,512]{1,0:T(8,128)(2,1)S(1)}, u32[]{:S(2)}) copy-start(bf16[256,512]{1,0:T(8,128)(2,1)S(1)} %collective-permute-done.5.refs_2_) | copy-start | bytes 786436
  72.8 19.8 %collective-permute-start.7 = (bf16[128,512]{1,0:T(8,128)(2,1)}, bf16[128,512]{1,0:T(8,128)(2,1)}, u32[]{:S(2)}, u32[]{:S(2)}) collective-permute-start(bf16[128,512]{1,0:T(8,128)(2,1)} %slice.43), channel_id=1, source_target_pairs={{0,14},{1,15},{2,0},{3,1},{4,2},{5,3},{6,4},{7,5},{8,6},{9,7},{10,... | collective-permute-start | bytes 393224 | tf_op jit(solution)/shard_map/ppermute | solution.py:275
  77.5 21.1 %collective-permute-start.19 = (bf16[16,64,128]{2,1,0:T(8,128)(2,1)S(1)}, bf16[16,64,128]{2,1,0:T(8,128)(2,1)}, u32[]{:S(2)}, u32[]{:S(2)}) collective-permute-start(bf16[16,64,128]{2,1,0:T(8,128)(2,1)S(1)} %add.68), channel_id=1, source_target_pairs={{0,8},{256,264},{128,136},{384,392},{64,72},{320,328},{192,200},{4... | collective-permute-start | bytes 786440 | tf_op jit(solution)/shard_map/ppermute | solution.py:285
  81.1 55.7 %collective-permute-start.8 = (bf16[4,256,512]{2,1,0:T(8,128)(2,1)}, bf16[4,256,512]{2,1,0:T(8,128)(2,1)S(1)}, u32[]{:S(2)}, u32[]{:S(2)}) collective-permute-start(bf16[4,256,512]{2,1,0:T(8,128)(2,1)} %bitcast.39), channel_id=1, source_target_pairs={{0,1},{1,0},{2,3},{3,2},{4,5},{5,4},{6,7},{7,6},{8,9},{9,8},{10,11... | collective-permute-start | bytes 3145736 | tf_op jit(solution)/shard_map/ppermute | solution.py:279
  92.6 0.7 copy-start.17
  95.5 41.4 %collective-permute-start.9 = (bf16[4,256,512]{2,1,0:T(8,128)(2,1)}, bf16[4,256,512]{2,1,0:T(8,128)(2,1)}, u32[]{:S(2)}, u32[]{:S(2)}) collective-permute-start(bf16[4,256,512]{2,1,0:T(8,128)(2,1)} %bitcast.42), channel_id=1, source_target_pairs={{0,33},{1,32},{2,35},{3,34},{4,37},{5,36},{6,39},{7,38},{8,41},{9,... | collective-permute-start | bytes 3145736 | tf_op jit(solution)/shard_map/ppermute | solution.py:279
  99.7 0.7 collective-permute-start.20
  100.5 10.6 %collective-permute-start.21 = (bf16[16,64,128]{2,1,0:T(8,128)(2,1)S(1)}, bf16[16,64,128]{2,1,0:T(8,128)(2,1)}, u32[]{:S(2)}, u32[]{:S(2)}) collective-permute-start(bf16[16,64,128]{2,1,0:T(8,128)(2,1)S(1)} %add.70), channel_id=1, source_target_pairs={{0,2},{256,258},{128,130},{384,386},{64,66},{320,322},{192,194},{4... | collective-permute-start | bytes 786440 | tf_op jit(solution)/shard_map/ppermute | solution.py:285
  101.8 35.0 %collective-permute-start.23 = (bf16[16,64,128]{2,1,0:T(8,128)(2,1)}, bf16[16,64,128]{2,1,0:T(8,128)(2,1)}, u32[]{:S(2)}, u32[]{:S(2)}) collective-permute-start(bf16[16,64,128]{2,1,0:T(8,128)(2,1)} %get-tuple-element.25), channel_id=1, source_target_pairs={{0,1},{1,2},{2,3},{3,4},{4,5},{5,6},{6,7},{7,8},{8,9},{9,10},{10,1... | collective-permute-start | bytes 786440 | tf_op jit(solution)/shard_map/ppermute | solution.py:347
  103.7 33.1 %collective-permute-start.24 = (bf16[16,64,128]{2,1,0:T(8,128)(2,1)}, bf16[16,64,128]{2,1,0:T(8,128)(2,1)}, u32[]{:S(2)}, u32[]{:S(2)}) collective-permute-start(bf16[16,64,128]{2,1,0:T(8,128)(2,1)} %get-tuple-element.23), channel_id=1, source_target_pairs={{1,0},{2,1},{3,2},{4,3},{5,4},{6,5},{7,6},{8,7},{9,8},{10,9},{11,1... | collective-permute-start | bytes 786440 | tf_op jit(solution)/shard_map/ppermute | solution.py:348
  112.1 24.7 %collective-permute-start.22 = (bf16[16,64,128]{2,1,0:T(8,128)(2,1)S(1)}, bf16[16,64,128]{2,1,0:T(8,128)(2,1)S(1)}, u32[]{:S(2)}, u32[]{:S(2)}) collective-permute-start(bf16[16,64,128]{2,1,0:T(8,128)(2,1)S(1)} %add.71), channel_id=1, source_target_pairs={{0,1},{256,257},{128,129},{384,385},{64,65},{320,321},{192,193},{4... | collective-permute-start | bytes 786440 | tf_op jit(solution)/shard_map/ppermute | solution.py:285
  136.9 1.0 copy-start.7
  136.9 1.6 copy-start.1
  141.8 4.6 %copy-start.21 = (s32[1024]{0:T(1024)S(1)}, s32[1024]{0:T(1024)}, u32[]{:S(2)}) copy-start(s32[1024]{0:T(1024)} %param.15) | copy-start | bytes 12292
  141.8 5.6 %copy-start.2 = (bf16[1024,512]{1,0:T(8,128)(2,1)S(1)}, bf16[1024,512]{1,0:T(8,128)(2,1)}, u32[]{:S(2)}) copy-start(bf16[1024,512]{1,0:T(8,128)(2,1)} %join.2) | copy-start | bytes 3145732
  141.8 9.4 %copy-start.3 = (bf16[1024,512]{1,0:T(8,128)(2,1)S(1)}, bf16[1024,512]{1,0:T(8,128)(2,1)}, u32[]{:S(2)}) copy-start(bf16[1024,512]{1,0:T(8,128)(2,1)} %join.3) | copy-start | bytes 3145732
  141.8 16.9 %copy-start = (bf16[16,64,256]{2,1,0:T(8,128)(2,1)S(1)}, bf16[16,64,256]{2,1,0:T(8,128)(2,1)}, u32[]{:S(2)}) copy-start(bf16[16,64,256]{2,1,0:T(8,128)(2,1)} %layer_norm.1) | copy-start | bytes 1572868
  141.8 47.9 %all-to-all-start.2 = ((bf16[16,64,768]{2,1,0:T(8,128)(2,1)}), bf16[16,64,768]{2,1,0:T(8,128)(2,1)}, u32[]{:S(2)}, u32[]{:S(2)}) async-start(bf16[16,64,768]{2,1,0:T(8,128)(2,1)} %place_blocks.1), calls=%async_computation.2 | async-start | bytes 3145728 | tf_op jit(solution)/shard_map/all_to_all | solution.py:371
  147.3 13.7 %collective-permute-start.10 = (bf16[4,256,512]{2,1,0:T(8,128)(2,1)S(1)}, bf16[4,256,512]{2,1,0:T(8,128)(2,1)S(1)}, u32[]{:S(2)}, u32[]{:S(2)}) collective-permute-start(bf16[4,256,512]{2,1,0:T(8,128)(2,1)S(1)} %bitcast.41), channel_id=1, source_target_pairs={{0,16},{1,17},{2,18},{3,19},{4,20},{5,21},{6,22},{7,23},{8,24},{9,... | collective-permute-start | bytes 3145736 | tf_op jit(solution)/shard_map/ppermute | solution.py:279
  151.2 9.8 %collective-permute-start.11 = (bf16[4,256,512]{2,1,0:T(8,128)(2,1)S(1)}, bf16[4,256,512]{2,1,0:T(8,128)(2,1)S(1)}, u32[]{:S(2)}, u32[]{:S(2)}) collective-permute-start(bf16[4,256,512]{2,1,0:T(8,128)(2,1)S(1)} %bitcast.44), channel_id=1, source_target_pairs={{0,16},{1,17},{2,18},{3,19},{4,20},{5,21},{6,22},{7,23},{8,24},{9,... | collective-permute-start | bytes 3145736 | tf_op jit(solution)/shard_map/ppermute | solution.py:279
  153.1 8.9 %collective-permute-start.12 = (bf16[4,256,512]{2,1,0:T(8,128)(2,1)}, bf16[4,256,512]{2,1,0:T(8,128)(2,1)S(1)}, u32[]{:S(2)}, u32[]{:S(2)}) collective-permute-start(bf16[4,256,512]{2,1,0:T(8,128)(2,1)} %copy-done.7), channel_id=1, source_target_pairs={{0,16},{1,17},{2,18},{3,19},{4,20},{5,21},{6,22},{7,23},{8,24},{9,... | collective-permute-start | bytes 3145736 | tf_op jit(solution)/shard_map/ppermute | solution.py:279
  155.5 8.4 %collective-permute-start.13 = (bf16[4,256,512]{2,1,0:T(8,128)(2,1)}, bf16[4,256,512]{2,1,0:T(8,128)(2,1)}, u32[]{:S(2)}, u32[]{:S(2)}) collective-permute-start(bf16[4,256,512]{2,1,0:T(8,128)(2,1)} %collective-permute-done.9.refs_3_), channel_id=1, source_target_pairs={{0,16},{1,17},{2,18},{3,19},{4,20},{5,21},{6,22},{7,23},{8,24},{9,... | collective-permute-start | bytes 3145736 | tf_op jit(solution)/shard_map/ppermute | solution.py:279
  161.0 1.0 copy-start.8
  162.0 1.0 copy-start.9
  163.0 1.0 copy-start.10
  170.9 3.3 %copy-start.6 = (bf16[16,64,640]{2,1,0:T(8,128)(2,1)S(1)}, bf16[16,64,640]{2,1,0:T(8,128)(2,1)}, u32[]{:S(2)}) copy-start(bf16[16,64,640]{2,1,0:T(8,128)(2,1)} %pad_maximum_fusion) | copy-start | bytes 3932164
  170.9 3.3 %copy-start.23 = (bf16[16,64,1024]{2,1,0:T(8,128)(2,1)S(1)}, bf16[16,64,1024]{2,1,0:T(8,128)(2,1)}, u32[]{:S(2)}) copy-start(bf16[16,64,1024]{2,1,0:T(8,128)(2,1)} %get-tuple-element.17) | copy-start | bytes 6291460
  174.1 2.6 %copy-start.22 = (bf16[16,64,1024]{2,1,0:T(8,128)(2,1)S(1)}, bf16[16,64,1024]{2,1,0:T(8,128)(2,1)}, u32[]{:S(2)}) copy-start(bf16[16,64,1024]{2,1,0:T(8,128)(2,1)} %get-tuple-element.18) | copy-start | bytes 6291460
  199.1 9.8 %copy-start.4 = (bf16[16,64,1024]{2,1,0:T(8,128)(2,1)S(1)}, bf16[16,64,1024]{2,1,0:T(8,128)(2,1)}, u32[]{:S(2)}) copy-start(bf16[16,64,1024]{2,1,0:T(8,128)(2,1)} %get-tuple-element.22) | copy-start | bytes 6291460
  199.1 9.8 %copy-start.18 = (f32[1024]{0:T(1024)S(1)}, f32[1024]{0:T(1024)}, u32[]{:S(2)}) copy-start(f32[1024]{0:T(1024)} %param.14) | copy-start | bytes 12292

commit v4 on v3

--- a/solution.py
+++ b/solution.py
@@ -8,6 +8,7 @@
 BLK = 128
 RAND = 3
 CAP = 4
+SLOTS = CAP + 1
 EPS = 1e-05
 NEG = float("-inf")
 TN = (((0,), (1,)), ((), ()))
@@ -98,7 +99,6 @@
 
 def near_kernel(qt_ref, k_ref, vt_ref, mask_ref, acc_ref, top_ref, sum_ref):
     f32 = jnp.float32
-    shared = slice(4 * BLK, 5 * BLK)
     for b in range(2):
         cols = slice(b * BLK, (b + 1) * BLK)
         near = slice(b * BLK, (b + 3) * BLK)
@@ -106,13 +106,10 @@
         mask = mask_ref[b]
         s = jnp.dot(k_ref[near, :], q, preferred_element_type=f32)
         s = s + jnp.concatenate([mask, mask], axis=1)
-        g = jnp.dot(k_ref[shared, :], q, preferred_element_type=f32)
-        top = jnp.maximum(jnp.max(s, axis=0, keepdims=True), jnp.max(g, axis=0, keepdims=True))
+        top = jnp.max(s, axis=0, keepdims=True)
         p = jnp.exp(s - top)
-        pg = jnp.exp(g - top)
-        total = jnp.sum(p, axis=0, keepdims=True) + jnp.sum(pg, axis=0, keepdims=True)
+        total = jnp.sum(p, axis=0, keepdims=True)
         acc = jnp.dot(vt_ref[:, near], p.astype(jnp.bfloat16), preferred_element_type=f32)
-        acc += jnp.dot(vt_ref[:, shared], pg.astype(jnp.bfloat16), preferred_element_type=f32)
         acc_ref[:, cols] = own_halves(acc)
         top_ref[0, b] = jnp.broadcast_to(top, top_ref.shape[2:])
         sum_ref[0, b] = jnp.broadcast_to(total, sum_ref.shape[2:])
@@ -121,17 +118,23 @@
 def far_kernel(qt_ref, k_ref, vt_ref, acc_ref, top_ref, sum_ref, out_ref):
     f32 = jnp.float32
     spread = RAND * BLK
+    shared = slice(2 * spread, 2 * spread + BLK)
     for b in range(2):
         cols = slice(b * BLK, (b + 1) * BLK)
         far = slice(b * spread, (b + 1) * spread)
         q = both_heads(qt_ref[:, cols])
         s = jnp.dot(k_ref[far, :], q, preferred_element_type=f32)
+        g = jnp.dot(k_ref[shared, :], q, preferred_element_type=f32)
         old_top = top_ref[0, b, :1]
         top = jnp.maximum(jnp.max(s, axis=0, keepdims=True), old_top)
+        top = jnp.maximum(jnp.max(g, axis=0, keepdims=True), top)
         p = jnp.exp(s - top)
+        pg = jnp.exp(g - top)
         scale = jnp.exp(old_top - top)
         total = jnp.sum(p, axis=0, keepdims=True) + sum_ref[0, b, :1] * scale
+        total += jnp.sum(pg, axis=0, keepdims=True)
         acc = jnp.dot(vt_ref[:, far], p.astype(jnp.bfloat16), preferred_element_type=f32)
+        acc += jnp.dot(vt_ref[:, shared], pg.astype(jnp.bfloat16), preferred_element_type=f32)
         half = acc.shape[0] // 2
         acc = own_halves(acc) + acc_ref[:, cols] * spread_rows(scale, half)
         out_ref[:, cols] = (acc / spread_rows(total, half)).astype(jnp.bfloat16)
@@ -279,15 +282,7 @@
     return lax.ppermute(value, ("ctx", "head"), [(i, i ^ bits) for i in range(devices)])
 
 
-def widen(value, holders, steps):
-    for step in steps:
-        hop = [(i, i + step) for i in holders]
-        value = value + lax.ppermute(value, ("ctx", "head"), hop)
-        holders = holders + [i + step for i in holders]
-    return value, holders
-
-
-def exchange_plan(pairs_dev, pairs_off, ctx_count, ctx_index, lower):
+def exchange_plan(pairs_dev, pairs_off, ctx_count, ctx_index, lower, per_dev):
     pair_count = lower.shape[0]
     all_dev = pairs_dev.reshape(ctx_count, pair_count)
     all_off = pairs_off.reshape(ctx_count, pair_count)
@@ -295,11 +290,13 @@
     rank = jnp.sum((own[:, None, :] & lower[None]).astype(jnp.int32), axis=2)
     slot = jnp.arange(CAP, dtype=jnp.int32)
     chosen = own[:, None, :] & (rank[:, None, :] == slot[None, :, None])
-    send = jnp.sum(jnp.where(chosen, all_off[:, None, :], 0), axis=2).reshape(-1)
+    send = jnp.sum(jnp.where(chosen, all_off[:, None, :], 0), axis=2)
+    send = jnp.pad(send, ((0, 0), (0, 1))).reshape(-1)
     own_dev = lax.dynamic_index_in_dim(all_dev, ctx_index, 0, keepdims=False)
     earlier = (own_dev[:, None] == own_dev[None, :]) & lower
-    take = own_dev * CAP + jnp.sum(earlier.astype(jnp.int32), axis=1)
-    return send, take
+    take = own_dev * SLOTS + jnp.sum(earlier.astype(jnp.int32), axis=1)
+    take = jnp.pad(take.reshape(-1, per_dev), ((0, 0), (0, 1)), constant_values=CAP)
+    return send, take.reshape(-1)
 
 
 def window_mask(lengths, first_pos, doc_tokens, rows):
@@ -337,10 +334,6 @@
     own = own_piece(core, wt, out_weight)
     u1, d1 = shift(own, 2, heads), shift(own, -2, heads)
 
-    shared = jnp.where(place == 0, normed_t[:, :, :BLK], 0).astype(jnp.bfloat16)
-    holders = [0]
-    shared, holders = widen(shared, holders, [16 * heads, 8 * heads, 4 * heads])
-
     both = ("ctx", "head")
     right = [(i, i + 1) for i in range(devices - 1)]
     left = [(i + 1, i) for i in range(devices - 1)]
@@ -350,11 +343,13 @@
     pair_count = (heads * rows // BLK) * RAND
     order = jnp.arange(pair_count, dtype=jnp.int32)
     lower = order[None, :] < order[:, None]
-    send, take = exchange_plan(pairs_dev, pairs_off, ctx_count, ctx_index, lower)
-    outgoing = pick_blocks(tied(send, u1, d1, shared), cells)
-    outgoing = outgoing.reshape(ctx_count, CAP * hd, BLK)
+    send, take = exchange_plan(
+        pairs_dev, pairs_off, ctx_count, ctx_index, lower, pair_count // heads
+    )
+    outgoing = pick_blocks(tied(send, u1, d1), cells)
+    outgoing = outgoing.reshape(ctx_count, SLOTS * hd, BLK)
     slots = lax.all_to_all(outgoing, "ctx", split_axis=0, concat_axis=0, tiled=True)
-    slots = slots.reshape(ctx_count * CAP, hd, BLK)
+    slots = slots.reshape(ctx_count * SLOTS, hd, BLK)
 
     mid = own.shape[0] // 2
     u2, d2 = shift(u1, 2, heads), shift(d1, -2, heads)
@@ -365,15 +360,14 @@
     b = join(d2, u3, d3, u4, d4).reshape(shape)
     c = swap(a, 1, devices)
     d = swap(b, 2 * heads + 1, devices)
-    shared, holders = widen(shared, holders, [heads, 2 * heads, 8, 4, 2, 1])
-
-    placed = place_blocks(tied(take, c, d, shared, before, after), slots, heads)
+
+    mine = [a, b, c, d]
+    other = [swap(part, heads, devices) for part in mine]
+    placed = place_blocks(tied(take, before, after, *other), slots, heads)
     far = lax.all_to_all(placed, "head", split_axis=0, concat_axis=0, tiled=True)
     far = far.reshape(width, far.shape[2])
 
-    mine = [a, b, c, d]
-    other = [swap(part, heads, devices) for part in mine]
-    near = jnp.concatenate([before, normed_t, after, shared], axis=2)
+    near = jnp.concatenate([before, normed_t, after], axis=2)
     near = near.reshape(width, near.shape[2])
 
     mask = window_mask(lengths, place * rows, devices * rows, rows)

time: 213 us -> 225 us (1.056)
  waiting for transfers between devices: 33.3 us -> 67.2 us
  starting transfers between devices: 95.3 us -> 80.3 us
  other arithmetic: 9.99 us -> 3.87 us
    ppermute x9 -> x0, waiting for transfers between devices: 22.7 us -> none  [widen(): value = value + lax.ppermute(value, ('ctx', 'head'), hop)]
    ppermute x6, waiting for transfers between devices: 0.02 us -> 21.8 us  [swap(): lax.ppermute(value, ('ctx', 'head'), [(i, i ^ bits) for i in range(device...]
    all_to_all x1, waiting for transfers between devices: 0.01 us -> 15.1 us  [per_device(): lax.all_to_all(placed, 'head', split_axis=0, concat_axis=0, tiled=True)]
    ppermute x9 -> x0, starting transfers between devices: 8.1 us -> none  [widen(): value = value + lax.ppermute(value, ('ctx', 'head'), hop)]
    ppermute x1, waiting for transfers between devices: 0.01 us -> 7.77 us  [per_device(): before = lax.ppermute(normed_t[:, :, rows - BLK:], both, right)]
    ppermute x6, starting transfers between devices: 24.9 us -> 17.8 us  [swap(): lax.ppermute(value, ('ctx', 'head'), [(i, i ^ bits) for i in range(device...]
    ppermute x1, waiting for transfers between devices: 0.01 us -> 6.34 us  [per_device(): after = lax.ppermute(normed_t[:, :, :BLK], both, left)]
    ppermute x8, waiting for transfers between devices: 10.5 us -> 16.2 us  [shift(): return lax.ppermute(value, 'head', pairs)]
  transfers between devices with their start and end apart: 28 -> 19, of which waited for: 4 -> 7; matrix products, arithmetic and copies ran while one was open for 10% -> 7% of each run, Pallas kernels for 11% -> 10%
where the time goes in v4:
time: 225 us; the launch traced here: 222 us
  starting transfers between devices  80.3 us (36%)
  waiting for transfers between devices  67.2 us (30%)
  Pallas kernels  42.8 us (19%)
  matrix products  19.1 us (8%)
  local copies, waits for them, and re-layouts  8.61 us (4%)
  other arithmetic  3.87 us (2%)
    ppermute x8, starting transfers between devices, shift(): return lax.ppermute(value, 'head', pairs)  26.1 us
    ppermute x6, waiting for transfers between devices, swap(): lax.ppermute(value, ('ctx', 'head'), [(i, i ^ bits) for i in range(device...  21.8 us
    ppermute x6, starting transfers between devices, swap(): lax.ppermute(value, ('ctx', 'head'), [(i, i ^ bits) for i in range(device...  17.8 us
    ppermute x8, waiting for transfers between devices, shift(): return lax.ppermute(value, 'head', pairs)  16.2 us
    all_to_all x1, waiting for transfers between devices, per_device(): lax.all_to_all(placed, 'head', split_axis=0, concat_axis=0, tiled=True)  15.1 us
    all_to_all x1, starting transfers between devices, per_device(): lax.all_to_all(outgoing, 'ctx', split_axis=0, concat_axis=0, tiled=True)  14.4 us
    pallas_call x1, Pallas kernels, far_attention(): pl.pallas_call(far_kernel, out_shape=jax.ShapeDtypeStruct((width, rows),...  10.3 us
    all_to_all x1, starting transfers between devices, per_device(): lax.all_to_all(placed, 'head', split_axis=0, concat_axis=0, tiled=True)  9.55 us
  transfers between devices with their start and end apart: 19, of which 7 were waited for; matrix products, arithmetic and copies ran while one was open for 7% of the time, Pallas kernels for 10%

profile of v4, /device:TPU:7, one launch (start us, length us, event | category | flops | bytes accessed | tf_op | source)
XLA Modules:
  0.0 222.3 jit_solution(3428057138566171905)
XLA Ops:
  0.0 2.4 %layer_norm.1 = bf16[16,64,256]{2,1,0:T(8,128)(2,1)} custom-call(bf16[256,1024]{1,0:T(8,128)(2,1)} %tok_ref.1, f32[1,1024]{1,0:T(1,128)} %bitcast.49, f32[1,1024]{1,0:T(1,128)} %bitcast.50), custom_call_target="tpu_custom_call" | custom-call | tf_op jit(solution)/shard_map/layer_norm/pallas_call | solution.py:27
  2.4 8.0 %all-to-all-start = ((bf16[16,64,256]{2,1,0:T(8,128)(2,1)}), bf16[16,64,256]{2,1,0:T(8,128)(2,1)S(1)}, u32[]{:S(2)}, u32[]{:S(2)}) async-start(bf16[16,64,256]{2,1,0:T(8,128)(2,1)} %layer_norm.1), calls=%async_computation | async-start | bytes 1048576 | tf_op jit(solution)/shard_map/all_to_all | solution.py:332
  10.4 1.7 own_piece.1.refs_0_
  12.0 3.1 %collective-permute-start = (bf16[256,512]{1,0:T(8,128)(2,1)}, bf16[256,512]{1,0:T(8,128)(2,1)S(1)}, u32[]{:S(2)}, u32[]{:S(2)}) collective-permute-start(bf16[256,512]{1,0:T(8,128)(2,1)} %own_piece.1.refs_0_), channel_id=1, source_target_pairs={{0,2},{1,3},{2,4},{3,5},{4,6},{5,7},{6,8},{7,9},{8,10},{9,11},{10,... | collective-permute-start | bytes 786440 | tf_op jit(solution)/shard_map/ppermute | solution.py:278
  15.1 3.4 %collective-permute-start.1 = (bf16[256,512]{1,0:T(8,128)(2,1)}, bf16[256,512]{1,0:T(8,128)(2,1)S(1)}, u32[]{:S(2)}, u32[]{:S(2)}) collective-permute-start(bf16[256,512]{1,0:T(8,128)(2,1)} %own_piece.1.refs_0_), channel_id=1, source_target_pairs={{0,14},{1,15},{2,0},{3,1},{4,2},{5,3},{6,4},{7,5},{8,6},{9,7},{10,... | collective-permute-start | bytes 786440 | tf_op jit(solution)/shard_map/ppermute | solution.py:278
  18.6 0.2 copy.12
  18.8 0.3 reshape.205
  19.1 0.2 copy.13
  19.3 0.3 broadcast_in_dim.28
  19.6 0.6 convert_reduce_fusion.1
  20.2 0.1 select_reduce_fusion
  20.5 0.7 reshape.207.ids_ref
  21.1 8.9 %collective-permute-done.refs_1_ = bf16[256,512]{1,0:T(8,128)(2,1)S(1)} collective-permute-done((bf16[256,512]{1,0:T(8,128)(2,1)}, bf16[256,512]{1,0:T(8,128)(2,1)S(1)}, u32[]{:S(2)}, u32[]{:S(2)}) %collective-permute-start) | collective-permute-done | bytes 262176 | tf_op jit(solution)/shard_map/ppermute | solution.py:278
  30.1 0.8 copy-done.3
  30.9 4.2 %pick_blocks.1 = bf16[160,64,128]{2,1,0:T(8,128)(2,1)} custom-call(s32[160]{0:T(256)} %reshape.207.ids_ref, bf16[16,64,256]{2,1,0:T(8,128)(2,1)} %copy-done.3), custom_call_target="tpu_custom_call" | custom-call | tf_op jit(solution)/shard_map/pick_blocks/pallas_call | solution.py:45
  35.1 14.4 %all-to-all-start.1 = ((bf16[32,320,128]{2,1,0:T(8,128)(2,1)}), bf16[32,320,128]{2,1,0:T(8,128)(2,1)S(1)}, u32[]{:S(2)}, u32[]{:S(2)}) async-start(bf16[32,320,128]{2,1,0:T(8,128)(2,1)} %bitcast.35), calls=%async_computation.1 | async-start | bytes 5242880 | tf_op jit(solution)/shard_map/all_to_all | solution.py:351
  49.6 1.9 collective-permute-start.2
  51.5 4.6 %collective-permute-start.3 = (bf16[256,512]{1,0:T(8,128)(2,1)}, bf16[256,512]{1,0:T(8,128)(2,1)S(1)}, u32[]{:S(2)}, u32[]{:S(2)}) collective-permute-start(bf16[256,512]{1,0:T(8,128)(2,1)} %copy-done.8), channel_id=1, source_target_pairs={{0,14},{1,15},{2,0},{3,1},{4,2},{5,3},{6,4},{7,5},{8,6},{9,7},{10,... | collective-permute-start | bytes 786440 | tf_op jit(solution)/shard_map/ppermute | solution.py:278
  56.1 4.1 %collective-permute-done.2.refs_3_ = bf16[256,512]{1,0:T(8,128)(2,1)S(1)} collective-permute-done((bf16[256,512]{1,0:T(8,128)(2,1)S(1)}, bf16[256,512]{1,0:T(8,128)(2,1)S(1)}, u32[]{:S(2)}, u32[]{:S(2)}) %collective-permute-start.2) | collective-permute-done | bytes 262176 | tf_op jit(solution)/shard_map/ppermute | solution.py:278
  60.1 1.9 collective-permute-start.4
  62.1 4.6 %collective-permute-start.5 = (bf16[256,512]{1,0:T(8,128)(2,1)S(1)}, bf16[256,512]{1,0:T(8,128)(2,1)S(1)}, u32[]{:S(2)}, u32[]{:S(2)}) collective-permute-start(bf16[256,512]{1,0:T(8,128)(2,1)S(1)} %collective-permute-done.3.refs_0_), channel_id=1, source_target_pairs={{0,14},{1,15},{2,0},{3,1},{4,2},{5,3},{6,4},{7,5},{8,6},{9,7},{10,... | collective-permute-start | bytes 786440 | tf_op jit(solution)/shard_map/ppermute | solution.py:278
  66.7 3.2 %collective-permute-done.4.refs_1_ = bf16[256,512]{1,0:T(8,128)(2,1)S(1)} collective-permute-done((bf16[256,512]{1,0:T(8,128)(2,1)S(1)}, bf16[256,512]{1,0:T(8,128)(2,1)S(1)}, u32[]{:S(2)}, u32[]{:S(2)}) %collective-permute-start.4) | collective-permute-done | bytes 262176 | tf_op jit(solution)/shard_map/ppermute | solution.py:278
  69.8 0.7 slice.41
  70.5 1.9 collective-permute-start.6
  72.5 0.7 copy-done.5
  73.2 0.7 slice.42
  73.8 4.7 %collective-permute-start.7 = (bf16[128,512]{1,0:T(8,128)(2,1)}, bf16[128,512]{1,0:T(8,128)(2,1)}, u32[]{:S(2)}, u32[]{:S(2)}) collective-permute-start(bf16[128,512]{1,0:T(8,128)(2,1)} %slice.42), channel_id=1, source_target_pairs={{0,14},{1,15},{2,0},{3,1},{4,2},{5,3},{6,4},{7,5},{8,6},{9,7},{10,... | collective-permute-start | bytes 393224 | tf_op jit(solution)/shard_map/ppermute | solution.py:278
  78.5 2.2 join.2
  80.8 2.2 collective-permute-start.8
  83.0 0.6 copy-done.11
  83.6 2.3 %join.3 = bf16[1024,512]{1,0:T(8,128)(2,1)} custom-call(bf16[256,512]{1,0:T(8,128)(2,1)} %copy-done.9, bf16[256,512]{1,0:T(8,128)(2,1)} %copy-done.4, bf16[256,512]{1,0:T(8,128)(2,1)} %copy-done.5, bf16[128,512]{1,0:T(8,128)(2,1)} %copy-done.11, bf16[128,512]{1,0:T(8,128)(2,1)} %collective-permute-done.7.refs_4_), custom_call_target="tpu_custom_call" | custom-call | tf_op jit(solution)/shard_map/join/pallas_call | solution.py:225
  85.9 2.3 %collective-permute-start.9 = (bf16[4,256,512]{2,1,0:T(8,128)(2,1)}, bf16[4,256,512]{2,1,0:T(8,128)(2,1)}, u32[]{:S(2)}, u32[]{:S(2)}) collective-permute-start(bf16[4,256,512]{2,1,0:T(8,128)(2,1)} %bitcast.40), channel_id=1, source_target_pairs={{0,33},{1,32},{2,35},{3,34},{4,37},{5,36},{6,39},{7,38},{8,41},{9,... | collective-permute-start | bytes 3145736 | tf_op jit(solution)/shard_map/ppermute | solution.py:282
  88.2 5.0 %collective-permute-start.10 = (bf16[4,256,512]{2,1,0:T(8,128)(2,1)}, bf16[4,256,512]{2,1,0:T(8,128)(2,1)}, u32[]{:S(2)}, u32[]{:S(2)}) collective-permute-start(bf16[4,256,512]{2,1,0:T(8,128)(2,1)} %bitcast.38), channel_id=1, source_target_pairs={{0,16},{1,17},{2,18},{3,19},{4,20},{5,21},{6,22},{7,23},{8,24},{9,... | collective-permute-start | bytes 3145736 | tf_op jit(solution)/shard_map/ppermute | solution.py:282
  93.2 1.9 collective-permute-start.11
  95.1 21.8 %collective-permute-done.8.refs_2_ = bf16[4,256,512]{2,1,0:T(8,128)(2,1)} collective-permute-done((bf16[4,256,512]{2,1,0:T(8,128)(2,1)}, bf16[4,256,512]{2,1,0:T(8,128)(2,1)}, u32[]{:S(2)}, u32[]{:S(2)}) %collective-permute-start.8) | collective-permute-done | bytes 1048608 | tf_op jit(solution)/shard_map/ppermute | solution.py:282
  116.9 4.0 %collective-permute-start.12 = (bf16[4,256,512]{2,1,0:T(8,128)(2,1)}, bf16[4,256,512]{2,1,0:T(8,128)(2,1)}, u32[]{:S(2)}, u32[]{:S(2)}) collective-permute-start(bf16[4,256,512]{2,1,0:T(8,128)(2,1)} %collective-permute-done.8.refs_2_), channel_id=1, source_target_pairs={{0,16},{1,17},{2,18},{3,19},{4,20},{5,21},{6,22},{7,23},{8,24},{9,... | collective-permute-start | bytes 3145736 | tf_op jit(solution)/shard_map/ppermute | solution.py:282
  121.0 2.4 %collective-permute-start.13 = (bf16[4,256,512]{2,1,0:T(8,128)(2,1)}, bf16[4,256,512]{2,1,0:T(8,128)(2,1)}, u32[]{:S(2)}, u32[]{:S(2)}) collective-permute-start(bf16[4,256,512]{2,1,0:T(8,128)(2,1)} %collective-permute-done.9.refs_3_), channel_id=1, source_target_pairs={{0,16},{1,17},{2,18},{3,19},{4,20},{5,21},{6,22},{7,23},{8,24},{9,... | collective-permute-start | bytes 3145736 | tf_op jit(solution)/shard_map/ppermute | solution.py:282
  123.4 0.1 fusion.6
  123.5 1.9 collective-permute-start.14
  125.4 7.8 %collective-permute-done.14 = bf16[16,64,128]{2,1,0:T(8,128)(2,1)S(1)} collective-permute-done((bf16[16,64,128]{2,1,0:T(8,128)(2,1)S(1)}, bf16[16,64,128]{2,1,0:T(8,128)(2,1)S(1)}, u32[]{:S(2)}, u32[]{:S(2)}) %collective-permute-start.14) | collective-permute-done | bytes 262176 | tf_op jit(solution)/shard_map/ppermute | solution.py:340
  133.2 0.7 copy-done.6
  133.9 2.4 %collective-permute-start.15 = (bf16[16,64,128]{2,1,0:T(8,128)(2,1)S(1)}, bf16[16,64,128]{2,1,0:T(8,128)(2,1)}, u32[]{:S(2)}, u32[]{:S(2)}) collective-permute-start(bf16[16,64,128]{2,1,0:T(8,128)(2,1)S(1)} %get-tuple-element.23), channel_id=1, source_target_pairs={{1,0},{2,1},{3,2},{4,3},{5,4},{6,5},{7,6},{8,7},{9,8},{10,9},{11,1... | collective-permute-start | bytes 786440 | tf_op jit(solution)/shard_map/ppermute | solution.py:341
  136.4 0.2 convert_reduce_fusion.2
  136.7 0.6 reshape.206.pos_ref
  137.4 6.3 %collective-permute-done.15 = bf16[16,64,128]{2,1,0:T(8,128)(2,1)} collective-permute-done((bf16[16,64,128]{2,1,0:T(8,128)(2,1)S(1)}, bf16[16,64,128]{2,1,0:T(8,128)(2,1)}, u32[]{:S(2)}, u32[]{:S(2)}) %collective-permute-start.15) | collective-permute-done | bytes 262176 | tf_op jit(solution)/shard_map/ppermute | solution.py:341
  143.7 1.5 copy-done
  145.2 3.5 %place_blocks.1 = bf16[16,64,896]{2,1,0:T(8,128)(2,1)} custom-call(s32[112]{0:T(128)} %reshape.206.pos_ref, bf16[160,64,128]{2,1,0:T(8,128)(2,1)} %bitcast.34), custom_call_target="tpu_custom_call" | custom-call | tf_op jit(solution)/shard_map/place_blocks/pallas_call | solution.py:70
  148.8 9.6 %all-to-all-start.2 = ((bf16[16,64,896]{2,1,0:T(8,128)(2,1)}), bf16[16,64,896]{2,1,0:T(8,128)(2,1)S(1)}, u32[]{:S(2)}, u32[]{:S(2)}) async-start(bf16[16,64,896]{2,1,0:T(8,128)(2,1)} %place_blocks.1), calls=%async_computation.2 | async-start | bytes 3670016 | tf_op jit(solution)/shard_map/all_to_all | solution.py:367
  158.3 0.3 reduce-window.9
  158.7 0.1 slice_reduce_fusion
  158.9 0.4 convert_reduce_fusion
  159.3 0.2 compare_select_fusion
  159.5 0.8 pad_maximum_fusion.1.mask_ref
  160.3 1.2 pad_maximum_fusion
  161.4 6.9 %assemble.1 = (bf16[16,64,1024]{2,1,0:T(8,128)(2,1)}, bf16[16,64,1024]{2,1,0:T(8,128)(2,1)}, bf16[16,64,1024]{2,1,0:T(8,128)(2,1)}, bf16[16,64,1024]{2,1,0:T(8,128)(2,1)}) custom-call(s32[1]{0:T(128)} %bitcast.core_ref, bf16[4,256,512]{2,1,0:T(8,128)(2,1)} %bitcast.39, bf16[4,256,512]{2,1,0:T(8,128)(2,1)} %bitcast.42, ...), custom_call_target="tpu_custom_call" | custom-call | tf_op jit(solution)/shard_map/assemble/pallas_call | solution.py:262
  168.4 3.2 %fusion.2.qt_ref = bf16[1024,256]{1,0:T(8,128)(2,1)} fusion(bf16[1024,1024]{1,0:T(8,128)(2,1)} %bitcast.56, bf16[1024,256]{1,0:T(8,128)(2,1)S(1)} %bitcast.36), kind=kOutput, calls=%fused_computation.10 | convolution fusion | flops 537919488 | bytes 3145728 | tf_op jit(solution)/shard_map/dot_general | solution.py:380
  171.6 2.3 %convolution_convert_fusion.2.vt_ref = bf16[1024,512]{1,0:T(8,128)(2,1)} fusion(bf16[1024,1024]{1,0:T(8,128)(2,1)S(1)} %bitcast.55, bf16[1024,512]{1,0:T(8,128)(2,1)S(1)} %bitcast.46), kind=kOutput, calls=%fused_computation.4 | convolution fusion | flops 1074266112 | bytes 4194304 | tf_op jit(solution)/shard_map/dot_general | solution.py:383
  173.9 2.3 %convolution_convert_fusion.3.k_ref = bf16[512,1024]{1,0:T(8,128)(2,1)} fusion(bf16[1024,512]{1,0:T(8,128)(2,1)S(1)} %bitcast.47, bf16[1024,1024]{1,0:T(8,128)(2,1)S(1)} %bitcast.52), kind=kOutput, calls=%fused_computation.5 | convolution fusion | flops 1074266112 | bytes 4194304 | tf_op jit(solution)/shard_map/dot_general | solution.py:382
  176.2 9.4 %near_attention.1 = (f32[1024,256]{1,0:T(8,128)}, f32[8,2,8,256]{3,2,1,0:T(8,128)}, f32[8,2,8,256]{3,2,1,0:T(8,128)}) custom-call(bf16[1024,256]{1,0:T(8,128)(2,1)} %fusion.2.qt_ref, bf16[512,1024]{1,0:T(8,128)(2,1)} %convolution_convert_fusion.3.k_ref, bf16[1024,512]{1,0:T(8,128)(2,1)} %convolution_convert_fusion.2.vt_ref, ...), custom_call_target="tpu_custom_call" | custom-call | tf_op jit(solution)/shard_map/near_attention/pallas_call | solution.py:156
  185.7 15.1 %all-to-all-done.2 = bf16[16,64,896]{2,1,0:T(8,128)(2,1)S(1)} async-done(((bf16[16,64,896]{2,1,0:T(8,128)(2,1)}), bf16[16,64,896]{2,1,0:T(8,128)(2,1)S(1)}, u32[]{:S(2)}, u32[]{:S(2)}) %all-to-all-start.2) | async-done | bytes 1835040 | tf_op jit(solution)/shard_map/all_to_all | solution.py:367
  200.7 5.3 %convolution_convert_fusion.vt_ref = bf16[1024,896]{1,0:T(8,128)(2,1)} fusion(bf16[1024,1024]{1,0:T(8,128)(2,1)} %bitcast.54, bf16[1024,896]{1,0:T(8,128)(2,1)S(1)} %bitcast.44), kind=kOutput, calls=%fused_computation.1 | convolution fusion | flops 1879965696 | bytes 5767168 | tf_op jit(solution)/shard_map/dot_general | solution.py:386
  206.1 3.4 %convolution_convert_fusion.1.k_ref = bf16[896,1024]{1,0:T(8,128)(2,1)} fusion(bf16[1024,896]{1,0:T(8,128)(2,1)S(1)} %bitcast.45, bf16[1024,1024]{1,0:T(8,128)(2,1)S(1)} %bitcast.53), kind=kOutput, calls=%fused_computation.2 | convolution fusion | flops 1879965696 | bytes 5767168 | tf_op jit(solution)/shard_map/dot_general | solution.py:385
  209.4 10.3 %far_attention.1 = bf16[1024,256]{1,0:T(8,128)(2,1)} custom-call(bf16[1024,256]{1,0:T(8,128)(2,1)} %fusion.2.qt_ref, bf16[896,1024]{1,0:T(8,128)(2,1)} %convolution_convert_fusion.1.k_ref, bf16[1024,896]{1,0:T(8,128)(2,1)} %convolution_convert_fusion.vt_ref, f32[1024,256]{1,0:T(8,128)} %get-tuple-element.19.acc_ref, ...), custom_call_target="tpu_custom_call" | custom-call | tf_op jit(solution)/shard_map/far_attention/pallas_call | solution.py:169
  219.7 2.6 %fusion.3 = bf16[256,1024]{1,0:T(8,128)(2,1)} fusion(bf16[1024,256]{1,0:T(8,128)(2,1)} %far_attention.1, bf16[1024,1024]{1,0:T(8,128)(2,1)S(1)} %bitcast.43, f32[1024]{0:T(1024)S(1)} %copy-done.12), kind=kOutput, calls=%fused_computation.11 | convolution fusion | flops 537395200 | bytes 3149824 | tf_op jit(solution)/shard_map/dot_general | solution.py:388
  (61 shorter events, 0.6 us)
Async XLA Ops:
  0.0 18.5 %copy-start.13 = (s32[1024,3]{0,1:T(4,128)S(1)}, s32[1024,3]{0,1:T(4,128)}, u32[]{:S(2)}) copy-start(s32[1024,3]{0,1:T(4,128)} %param.16) | copy-start | bytes 36868
  0.0 19.1 %copy-start.14 = (s32[1024,3]{0,1:T(4,128)S(1)}, s32[1024,3]{0,1:T(4,128)}, u32[]{:S(2)}) copy-start(s32[1024,3]{0,1:T(4,128)} %param.17) | copy-start | bytes 36868
  2.4 27.7 %all-to-all-start = ((bf16[16,64,256]{2,1,0:T(8,128)(2,1)}), bf16[16,64,256]{2,1,0:T(8,128)(2,1)S(1)}, u32[]{:S(2)}, u32[]{:S(2)}) async-start(bf16[16,64,256]{2,1,0:T(8,128)(2,1)} %layer_norm.1), calls=%async_computation | async-start | bytes 1048576 | tf_op jit(solution)/shard_map/all_to_all | solution.py:332
  12.0 18.0 %collective-permute-start = (bf16[256,512]{1,0:T(8,128)(2,1)}, bf16[256,512]{1,0:T(8,128)(2,1)S(1)}, u32[]{:S(2)}, u32[]{:S(2)}) collective-permute-start(bf16[256,512]{1,0:T(8,128)(2,1)} %own_piece.1.refs_0_), channel_id=1, source_target_pairs={{0,2},{1,3},{2,4},{3,5},{4,6},{5,7},{6,8},{7,9},{8,10},{9,11},{10,... | collective-permute-start | bytes 786440 | tf_op jit(solution)/shard_map/ppermute | solution.py:278
  15.1 14.9 %collective-permute-start.1 = (bf16[256,512]{1,0:T(8,128)(2,1)}, bf16[256,512]{1,0:T(8,128)(2,1)S(1)}, u32[]{:S(2)}, u32[]{:S(2)}) collective-permute-start(bf16[256,512]{1,0:T(8,128)(2,1)} %own_piece.1.refs_0_), channel_id=1, source_target_pairs={{0,14},{1,15},{2,0},{3,1},{4,2},{5,3},{6,4},{7,5},{8,6},{9,7},{10,... | collective-permute-start | bytes 786440 | tf_op jit(solution)/shard_map/ppermute | solution.py:278
  30.1 26.0 %copy-start.7 = (bf16[256,512]{1,0:T(8,128)(2,1)}, bf16[256,512]{1,0:T(8,128)(2,1)S(1)}, u32[]{:S(2)}) copy-start(bf16[256,512]{1,0:T(8,128)(2,1)S(1)} %collective-permute-done.refs_1_) | copy-start | bytes 786436
  30.1 5.0 %copy-start.8 = (bf16[256,512]{1,0:T(8,128)(2,1)}, bf16[256,512]{1,0:T(8,128)(2,1)S(1)}, u32[]{:S(2)}) copy-start(bf16[256,512]{1,0:T(8,128)(2,1)S(1)} %collective-permute-done.1.refs_2_) | copy-start | bytes 786436
  30.1 0.8 copy-start.3
  35.1 108.6 %all-to-all-start.1 = ((bf16[32,320,128]{2,1,0:T(8,128)(2,1)}), bf16[32,320,128]{2,1,0:T(8,128)(2,1)S(1)}, u32[]{:S(2)}, u32[]{:S(2)}) async-start(bf16[32,320,128]{2,1,0:T(8,128)(2,1)} %bitcast.35), calls=%async_computation.1 | async-start | bytes 5242880 | tf_op jit(solution)/shard_map/all_to_all | solution.py:351
  49.6 10.6 %collective-permute-start.2 = (bf16[256,512]{1,0:T(8,128)(2,1)S(1)}, bf16[256,512]{1,0:T(8,128)(2,1)S(1)}, u32[]{:S(2)}, u32[]{:S(2)}) collective-permute-start(bf16[256,512]{1,0:T(8,128)(2,1)S(1)} %collective-permute-done.refs_1_), channel_id=1, source_target_pairs={{0,2},{1,3},{2,4},{3,5},{4,6},{5,7},{6,8},{7,9},{8,10},{9,11},{10,... | collective-permute-start | bytes 786440 | tf_op jit(solution)/shard_map/ppermute | solution.py:278
  51.5 10.6 %collective-permute-start.3 = (bf16[256,512]{1,0:T(8,128)(2,1)}, bf16[256,512]{1,0:T(8,128)(2,1)S(1)}, u32[]{:S(2)}, u32[]{:S(2)}) collective-permute-start(bf16[256,512]{1,0:T(8,128)(2,1)} %copy-done.8), channel_id=1, source_target_pairs={{0,14},{1,15},{2,0},{3,1},{4,2},{5,3},{6,4},{7,5},{8,6},{9,7},{10,... | collective-permute-start | bytes 786440 | tf_op jit(solution)/shard_map/ppermute | solution.py:278
  60.1 1.9 copy-start.10
  60.1 9.7 %collective-permute-start.4 = (bf16[256,512]{1,0:T(8,128)(2,1)S(1)}, bf16[256,512]{1,0:T(8,128)(2,1)S(1)}, u32[]{:S(2)}, u32[]{:S(2)}) collective-permute-start(bf16[256,512]{1,0:T(8,128)(2,1)S(1)} %collective-permute-done.2.refs_3_), channel_id=1, source_target_pairs={{0,2},{1,3},{2,4},{3,5},{4,6},{5,7},{6,8},{7,9},{8,10},{9,11},{10,... | collective-permute-start | bytes 786440 | tf_op jit(solution)/shard_map/ppermute | solution.py:278
  62.1 11.8 %copy-start.9 = (bf16[256,512]{1,0:T(8,128)(2,1)}, bf16[256,512]{1,0:T(8,128)(2,1)S(1)}, u32[]{:S(2)}) copy-start(bf16[256,512]{1,0:T(8,128)(2,1)S(1)} %collective-permute-done.3.refs_0_) | copy-start | bytes 786436
  62.1 10.4 %collective-permute-start.5 = (bf16[256,512]{1,0:T(8,128)(2,1)S(1)}, bf16[256,512]{1,0:T(8,128)(2,1)S(1)}, u32[]{:S(2)}, u32[]{:S(2)}) collective-permute-start(bf16[256,512]{1,0:T(8,128)(2,1)S(1)} %collective-permute-done.3.refs_0_), channel_id=1, source_target_pairs={{0,14},{1,15},{2,0},{3,1},{4,2},{5,3},{6,4},{7,5},{8,6},{9,7},{10,... | collective-permute-start | bytes 786440 | tf_op jit(solution)/shard_map/ppermute | solution.py:278
  69.8 13.1 %copy-start.4 = (bf16[256,512]{1,0:T(8,128)(2,1)}, bf16[256,512]{1,0:T(8,128)(2,1)S(1)}, u32[]{:S(2)}) copy-start(bf16[256,512]{1,0:T(8,128)(2,1)S(1)} %collective-permute-done.4.refs_1_) | copy-start | bytes 786436
  70.5 12.4 %collective-permute-start.6 = (bf16[128,512]{1,0:T(8,128)(2,1)}, bf16[128,512]{1,0:T(8,128)(2,1)S(1)}, u32[]{:S(2)}, u32[]{:S(2)}) collective-permute-start(bf16[128,512]{1,0:T(8,128)(2,1)} %slice.41), channel_id=1, source_target_pairs={{0,2},{1,3},{2,4},{3,5},{4,6},{5,7},{6,8},{7,9},{8,10},{9,11},{10,... | collective-permute-start | bytes 393224 | tf_op jit(solution)/shard_map/ppermute | solution.py:278
  72.5 0.7 copy-start.5
  73.8 49.5 %copy-start.1 = (bf16[16,64,256]{2,1,0:T(8,128)(2,1)S(1)}, bf16[16,64,256]{2,1,0:T(8,128)(2,1)}, u32[]{:S(2)}) copy-start(bf16[16,64,256]{2,1,0:T(8,128)(2,1)} %layer_norm.1) | copy-start | bytes 1572868
  73.8 9.1 %collective-permute-start.7 = (bf16[128,512]{1,0:T(8,128)(2,1)}, bf16[128,512]{1,0:T(8,128)(2,1)}, u32[]{:S(2)}, u32[]{:S(2)}) collective-permute-start(bf16[128,512]{1,0:T(8,128)(2,1)} %slice.42), channel_id=1, source_target_pairs={{0,14},{1,15},{2,0},{3,1},{4,2},{5,3},{6,4},{7,5},{8,6},{9,7},{10,... | collective-permute-start | bytes 393224 | tf_op jit(solution)/shard_map/ppermute | solution.py:278
  80.8 36.2 %collective-permute-start.8 = (bf16[4,256,512]{2,1,0:T(8,128)(2,1)}, bf16[4,256,512]{2,1,0:T(8,128)(2,1)}, u32[]{:S(2)}, u32[]{:S(2)}) collective-permute-start(bf16[4,256,512]{2,1,0:T(8,128)(2,1)} %bitcast.37), channel_id=1, source_target_pairs={{0,1},{1,0},{2,3},{3,2},{4,5},{5,4},{6,7},{7,6},{8,9},{9,8},{10,11... | collective-permute-start | bytes 3145736 | tf_op jit(solution)/shard_map/ppermute | solution.py:282
  83.0 0.6 copy-start.11
  85.9 35.1 %collective-permute-start.9 = (bf16[4,256,512]{2,1,0:T(8,128)(2,1)}, bf16[4,256,512]{2,1,0:T(8,128)(2,1)}, u32[]{:S(2)}, u32[]{:S(2)}) collective-permute-start(bf16[4,256,512]{2,1,0:T(8,128)(2,1)} %bitcast.40), channel_id=1, source_target_pairs={{0,33},{1,32},{2,35},{3,34},{4,37},{5,36},{6,39},{7,38},{8,41},{9,... | collective-permute-start | bytes 3145736 | tf_op jit(solution)/shard_map/ppermute | solution.py:282
  88.2 55.5 %collective-permute-start.10 = (bf16[4,256,512]{2,1,0:T(8,128)(2,1)}, bf16[4,256,512]{2,1,0:T(8,128)(2,1)}, u32[]{:S(2)}, u32[]{:S(2)}) collective-permute-start(bf16[4,256,512]{2,1,0:T(8,128)(2,1)} %bitcast.38), channel_id=1, source_target_pairs={{0,16},{1,17},{2,18},{3,19},{4,20},{5,21},{6,22},{7,23},{8,24},{9,... | collective-permute-start | bytes 3145736 | tf_op jit(solution)/shard_map/ppermute | solution.py:282
  93.2 50.5 %collective-permute-start.11 = (bf16[4,256,512]{2,1,0:T(8,128)(2,1)}, bf16[4,256,512]{2,1,0:T(8,128)(2,1)}, u32[]{:S(2)}, u32[]{:S(2)}) collective-permute-start(bf16[4,256,512]{2,1,0:T(8,128)(2,1)} %bitcast.41), channel_id=1, source_target_pairs={{0,16},{1,17},{2,18},{3,19},{4,20},{5,21},{6,22},{7,23},{8,24},{9,... | collective-permute-start | bytes 3145736 | tf_op jit(solution)/shard_map/ppermute | solution.py:282
  116.9 26.8 %collective-permute-start.12 = (bf16[4,256,512]{2,1,0:T(8,128)(2,1)}, bf16[4,256,512]{2,1,0:T(8,128)(2,1)}, u32[]{:S(2)}, u32[]{:S(2)}) collective-permute-start(bf16[4,256,512]{2,1,0:T(8,128)(2,1)} %collective-permute-done.8.refs_2_), channel_id=1, source_target_pairs={{0,16},{1,17},{2,18},{3,19},{4,20},{5,21},{6,22},{7,23},{8,24},{9,... | collective-permute-start | bytes 3145736 | tf_op jit(solution)/shard_map/ppermute | solution.py:282
  121.0 22.7 %collective-permute-start.13 = (bf16[4,256,512]{2,1,0:T(8,128)(2,1)}, bf16[4,256,512]{2,1,0:T(8,128)(2,1)}, u32[]{:S(2)}, u32[]{:S(2)}) collective-permute-start(bf16[4,256,512]{2,1,0:T(8,128)(2,1)} %collective-permute-done.9.refs_3_), channel_id=1, source_target_pairs={{0,16},{1,17},{2,18},{3,19},{4,20},{5,21},{6,22},{7,23},{8,24},{9,... | collective-permute-start | bytes 3145736 | tf_op jit(solution)/shard_map/ppermute | solution.py:282
  123.5 9.7 %collective-permute-start.14 = (bf16[16,64,128]{2,1,0:T(8,128)(2,1)S(1)}, bf16[16,64,128]{2,1,0:T(8,128)(2,1)S(1)}, u32[]{:S(2)}, u32[]{:S(2)}) collective-permute-start(bf16[16,64,128]{2,1,0:T(8,128)(2,1)S(1)} %get-tuple-element.24), channel_id=1, source_target_pairs={{0,1},{1,2},{2,3},{3,4},{4,5},{5,6},{6,7},{7,8},{8,9},{9,10},{10,1... | collective-permute-start | bytes 786440 | tf_op jit(solution)/shard_map/ppermute | solution.py:340
  133.2 0.7 copy-start.6
  133.9 9.8 %collective-permute-start.15 = (bf16[16,64,128]{2,1,0:T(8,128)(2,1)S(1)}, bf16[16,64,128]{2,1,0:T(8,128)(2,1)}, u32[]{:S(2)}, u32[]{:S(2)}) collective-permute-start(bf16[16,64,128]{2,1,0:T(8,128)(2,1)S(1)} %get-tuple-element.23), channel_id=1, source_target_pairs={{1,0},{2,1},{3,2},{4,3},{5,4},{6,5},{7,6},{8,7},{9,8},{10,9},{11,1... | collective-permute-start | bytes 786440 | tf_op jit(solution)/shard_map/ppermute | solution.py:341
  143.7 1.5 copy-start
  148.8 9.6 %copy-start.15 = (s32[1024]{0:T(1024)S(1)}, s32[1024]{0:T(1024)}, u32[]{:S(2)}) copy-start(s32[1024]{0:T(1024)} %param.15) | copy-start | bytes 12292
  148.8 52.0 %all-to-all-start.2 = ((bf16[16,64,896]{2,1,0:T(8,128)(2,1)}), bf16[16,64,896]{2,1,0:T(8,128)(2,1)S(1)}, u32[]{:S(2)}, u32[]{:S(2)}) async-start(bf16[16,64,896]{2,1,0:T(8,128)(2,1)} %place_blocks.1), calls=%async_computation.2 | async-start | bytes 3670016 | tf_op jit(solution)/shard_map/all_to_all | solution.py:367
  168.4 3.3 %copy-start.18 = (bf16[16,64,1024]{2,1,0:T(8,128)(2,1)S(1)}, bf16[16,64,1024]{2,1,0:T(8,128)(2,1)}, u32[]{:S(2)}) copy-start(bf16[16,64,1024]{2,1,0:T(8,128)(2,1)} %get-tuple-element.18) | copy-start | bytes 6291460
  171.6 2.3 %copy-start.16 = (bf16[16,64,1024]{2,1,0:T(8,128)(2,1)S(1)}, bf16[16,64,1024]{2,1,0:T(8,128)(2,1)}, u32[]{:S(2)}) copy-start(bf16[16,64,1024]{2,1,0:T(8,128)(2,1)} %get-tuple-element.17) | copy-start | bytes 6291460
  200.7 5.3 %copy-start.17 = (bf16[16,64,1024]{2,1,0:T(8,128)(2,1)S(1)}, bf16[16,64,1024]{2,1,0:T(8,128)(2,1)}, u32[]{:S(2)}) copy-start(bf16[16,64,1024]{2,1,0:T(8,128)(2,1)} %get-tuple-element.17) | copy-start | bytes 6291460
  209.4 10.3 %copy-start.2 = (bf16[16,64,1024]{2,1,0:T(8,128)(2,1)S(1)}, bf16[16,64,1024]{2,1,0:T(8,128)(2,1)}, u32[]{:S(2)}) copy-start(bf16[16,64,1024]{2,1,0:T(8,128)(2,1)} %get-tuple-element.22) | copy-start | bytes 6291460
  209.4 10.3 %copy-start.12 = (f32[1024]{0:T(1024)S(1)}, f32[1024]{0:T(1024)}, u32[]{:S(2)}) copy-start(f32[1024]{0:T(1024)} %param.14) | copy-start | bytes 12292

commit v5 on v4

--- a/solution.py
+++ b/solution.py
@@ -14,19 +14,25 @@
 TN = (((0,), (1,)), ((), ()))
 
 
-def ln_kernel(tok_ref, gain_ref, bias_ref, normt_ref):
+def ln_kernel(tok_ref, gain_ref, bias_ref, normt_ref, first_ref, last_ref):
     values = tok_ref[...].astype(jnp.float32)
     center = values - jnp.mean(values, axis=-1, keepdims=True)
     spread = jnp.mean(center * center, axis=-1, keepdims=True)
     normed = center * lax.rsqrt(spread + EPS) * gain_ref[...] + bias_ref[...]
-    normt_ref[...] = jnp.transpose(normed).astype(jnp.bfloat16).reshape(normt_ref.shape)
+    turned = jnp.transpose(normed).astype(jnp.bfloat16).reshape(normt_ref.shape)
+    normt_ref[...] = turned
+    first_ref[...] = turned[:, :, :BLK]
+    last_ref[...] = turned[:, :, turned.shape[2] - BLK :]
 
 
 def layer_norm(tokens, gain, bias, heads):
     rows, width = tokens.shape
     return pl.pallas_call(
         ln_kernel,
-        out_shape=jax.ShapeDtypeStruct((heads, width // heads, rows), jnp.bfloat16),
+        out_shape=tuple(
+            jax.ShapeDtypeStruct((heads, width // heads, cols), jnp.bfloat16)
+            for cols in (rows, BLK, BLK)
+        ),
         name="layer_norm",
     )(tokens, gain.reshape(1, width), bias.reshape(1, width))
 
@@ -235,15 +241,15 @@
 def assemble_kernel(core_ref, *refs):
     sems = refs[-1]
     outs, parts = refs[-5:-1], refs[:-5]
-    hd, width = outs[0].shape[1], outs[0].shape[2]
+    heads, hd, width = outs[0].shape
     cols = width // 2
-    half = len(parts) // 2
-    copies = []
+    copies, head = [], 0
     for n, part in enumerate(parts):
-        side = core_ref[0] if n < half else 1 - core_ref[0]
+        side = core_ref[0] if head < heads else 1 - core_ref[0]
         into_cols = pl.ds(pl.multiple_of(side * cols, cols), cols)
         count = part.shape[0]
-        into_heads = pl.ds((n % half) * count, count)
+        into_heads = pl.ds(head % heads, count)
+        head += count
         for k, out in enumerate(outs):
             copies.append(
                 pltpu.make_async_copy(
@@ -255,9 +261,9 @@
     run_copies(copies)
 
 
-def assemble(core, parts, heads):
-    count, rows, cols = parts[0].shape
-    hd = rows // 4
+def assemble(core, parts, heads, hd):
+    cols = parts[0].shape[1]
+    parts = [part.reshape(-1, 4 * hd, cols) for part in parts]
     one = jax.ShapeDtypeStruct((heads, hd, 2 * cols), jnp.bfloat16)
     return pl.pallas_call(
         assemble_kernel,
@@ -328,17 +334,17 @@
     core = (ctx_index % 2).astype(jnp.int32).reshape(1)
     place = ctx_index * heads + head_index
 
-    normed_t = layer_norm(tokens, ln_gain, ln_bias, heads)
+    normed_t, first, last = layer_norm(tokens, ln_gain, ln_bias, heads)
     cells = lax.all_to_all(normed_t, "head", split_axis=0, concat_axis=0, tiled=True)
 
     own = own_piece(core, wt, out_weight)
-    u1, d1 = shift(own, 2, heads), shift(own, -2, heads)
+    beside = swap(own, 1, devices)
 
     both = ("ctx", "head")
     right = [(i, i + 1) for i in range(devices - 1)]
     left = [(i + 1, i) for i in range(devices - 1)]
-    before = lax.ppermute(normed_t[:, :, rows - BLK :], both, right)
-    after = lax.ppermute(normed_t[:, :, :BLK], both, left)
+    before = lax.ppermute(last, both, right)
+    after = lax.ppermute(first, both, left)
 
     pair_count = (heads * rows // BLK) * RAND
     order = jnp.arange(pair_count, dtype=jnp.int32)
@@ -346,24 +352,20 @@
     send, take = exchange_plan(
         pairs_dev, pairs_off, ctx_count, ctx_index, lower, pair_count // heads
     )
-    outgoing = pick_blocks(tied(send, u1, d1), cells)
+    outgoing = pick_blocks(tied(send, beside, before, after), cells)
     outgoing = outgoing.reshape(ctx_count, SLOTS * hd, BLK)
     slots = lax.all_to_all(outgoing, "ctx", split_axis=0, concat_axis=0, tiled=True)
     slots = slots.reshape(ctx_count * SLOTS, hd, BLK)
 
-    mid = own.shape[0] // 2
+    mid = own.shape[0]
+    two = join(own, beside)
+    u1, d1 = shift(two, 2, heads), shift(two, -2, heads)
     u2, d2 = shift(u1, 2, heads), shift(d1, -2, heads)
     u3, d3 = shift(u2, 2, heads), shift(d2, -2, heads)
     u4, d4 = shift(u3[:mid], 2, heads), shift(d3[mid:], -2, heads)
-    shape = (heads // 4,) + own.shape
-    a = join(own, u1, d1, u2).reshape(shape)
-    b = join(d2, u3, d3, u4, d4).reshape(shape)
-    c = swap(a, 1, devices)
-    d = swap(b, 2 * heads + 1, devices)
-
-    mine = [a, b, c, d]
-    other = [swap(part, heads, devices) for part in mine]
-    placed = place_blocks(tied(take, before, after, *other), slots, heads)
+    mine = [two, u1, d1, u2, d2, u3, d3, u4, d4]
+    other = [swap(join(*part), heads, devices) for part in (mine[:4], mine[4:])]
+    placed = place_blocks(tied(take, *other), slots, heads)
     far = lax.all_to_all(placed, "head", split_axis=0, concat_axis=0, tiled=True)
     far = far.reshape(width, far.shape[2])
 
@@ -374,7 +376,7 @@
 
     f32 = jnp.float32
     bf16 = jnp.bfloat16
-    weights = assemble(core, mine + other, heads)
+    weights = assemble(core, mine + other, heads, hd)
     w_q, w_k, w_v, w_o = (w.reshape(width, width) for w in weights)
     own_t = normed_t.reshape(width, rows)
     qt = jnp.dot(w_q, own_t, preferred_element_type=f32).astype(bf16)

time: 225 us -> 212 us (0.942)
  starting transfers between devices: 80.3 us -> 71.6 us
  waiting for transfers between devices: 67.2 us -> 58.9 us
  Pallas kernels: 42.8 us -> 46.3 us
    ppermute x8, waiting for transfers between devices: 16.2 us -> 26.6 us  [shift(): return lax.ppermute(value, 'head', pairs)]
    ppermute x6 -> x3, waiting for transfers between devices: 21.8 us -> 12.1 us  [swap(): lax.ppermute(value, ('ctx', 'head'), [(i, i ^ bits) for i in range(device...]
    ppermute x2, waiting for transfers between devices: 14.1 us -> 5.62 us  [the longest x1 5.62 us: per_device(): before = lax.ppermute(last, both, right)]
    ppermute x6 -> x3, starting transfers between devices: 17.8 us -> 9.38 us  [swap(): lax.ppermute(value, ('ctx', 'head'), [(i, i ^ bits) for i in range(device...]
    pallas_call x2 -> x3, Pallas kernels: 4.45 us -> 7.63 us  [join(): pl.pallas_call(join_kernel, out_shape=jax.ShapeDtypeStruct((rows,) + part...]
    unnamed x41 -> x45, local copies, waits for them, and re-layouts: 4.93 us -> 4.39 us
  transfers between devices with their start and end apart: 19 -> 16, of which waited for: 7 -> 7; matrix products, arithmetic and copies ran while one was open for 7% -> 8% of each run, Pallas kernels for 10% -> 12%
where the time goes in v5:
time: 212 us; the launch traced here: 208 us
  starting transfers between devices  71.6 us (34%)
  waiting for transfers between devices  58.9 us (28%)
  Pallas kernels  46.3 us (22%)
  matrix products  19.1 us (9%)
  local copies, waits for them, and re-layouts  8.04 us (4%)
  other arithmetic  3.85 us (2%)
    ppermute x8, waiting for transfers between devices, shift(): return lax.ppermute(value, 'head', pairs)  26.6 us
    ppermute x8, starting transfers between devices, shift(): return lax.ppermute(value, 'head', pairs)  25.9 us
    all_to_all x1, starting transfers between devices, per_device(): lax.all_to_all(outgoing, 'ctx', split_axis=0, concat_axis=0, tiled=True)  14.7 us
    all_to_all x1, waiting for transfers between devices, per_device(): lax.all_to_all(placed, 'head', split_axis=0, concat_axis=0, tiled=True)  14.5 us
    ppermute x3, waiting for transfers between devices, swap(): lax.ppermute(value, ('ctx', 'head'), [(i, i ^ bits) for i in range(device...  12.1 us
    pallas_call x1, Pallas kernels, far_attention(): pl.pallas_call(far_kernel, out_shape=jax.ShapeDtypeStruct((width, rows),...  10.3 us
    pallas_call x1, Pallas kernels, near_attention(): pl.pallas_call(near_kernel, out_shape=(jax.ShapeDtypeStruct((width, rows)...  9.44 us
    ppermute x3, starting transfers between devices, swap(): lax.ppermute(value, ('ctx', 'head'), [(i, i ^ bits) for i in range(device...  9.38 us
  transfers between devices with their start and end apart: 16, of which 7 were waited for; matrix products, arithmetic and copies ran while one was open for 8% of the time, Pallas kernels for 12%

profile of v5, /device:TPU:7, one launch (start us, length us, event | category | flops | bytes accessed | tf_op | source)
XLA Modules:
  0.0 208.2 jit_solution(1226324195732257255)
XLA Ops:
  0.0 2.5 %layer_norm.1 = (bf16[16,64,256]{2,1,0:T(8,128)(2,1)}, bf16[16,64,128]{2,1,0:T(8,128)(2,1)}, bf16[16,64,128]{2,1,0:T(8,128)(2,1)}) custom-call(bf16[256,1024]{1,0:T(8,128)(2,1)} %tok_ref.1, f32[1,1024]{1,0:T(1,128)} %bitcast.60, f32[1,1024]{1,0:T(1,128)} %bitcast.61), custom_call_target="tpu_custom_call" | custom-call | tf_op jit(solution)/shard_map/layer_norm/pallas_call | solution.py:30
  2.5 8.0 %all-to-all-start = ((bf16[16,64,256]{2,1,0:T(8,128)(2,1)}), bf16[16,64,256]{2,1,0:T(8,128)(2,1)S(1)}, u32[]{:S(2)}, u32[]{:S(2)}) async-start(bf16[16,64,256]{2,1,0:T(8,128)(2,1)} %get-tuple-element.18), calls=%async_computation | async-start | bytes 1048576 | tf_op jit(solution)/shard_map/all_to_all | solution.py:338
  10.5 1.7 own_piece.1.refs_0_
  12.1 2.0 collective-permute-start
  14.2 4.2 %collective-permute-start.11 = (bf16[16,64,128]{2,1,0:T(8,128)(2,1)}, bf16[16,64,128]{2,1,0:T(8,128)(2,1)S(1)}, u32[]{:S(2)}, u32[]{:S(2)}) collective-permute-start(bf16[16,64,128]{2,1,0:T(8,128)(2,1)} %get-tuple-element.20), channel_id=1, source_target_pairs={{0,1},{1,2},{2,3},{3,4},{4,5},{5,6},{6,7},{7,8},{8,9},{9,10},{10,1... | collective-permute-start | bytes 786440 | tf_op jit(solution)/shard_map/ppermute | solution.py:346
  18.3 1.9 collective-permute-start.12
  20.3 0.2 copy.12
  20.5 0.3 reshape.241
  20.8 0.2 copy.13
  21.1 0.3 broadcast_in_dim.28
  21.3 0.6 convert_reduce_fusion.1
  22.0 0.1 select_reduce_fusion
  22.1 0.1 copy.15
  22.2 0.6 reshape.243.ids_ref
  22.8 8.7 %collective-permute-done.refs_1_ = bf16[256,512]{1,0:T(8,128)(2,1)S(1)} collective-permute-done((bf16[256,512]{1,0:T(8,128)(2,1)}, bf16[256,512]{1,0:T(8,128)(2,1)S(1)}, u32[]{:S(2)}, u32[]{:S(2)}) %collective-permute-start) | collective-permute-done | bytes 262176 | tf_op jit(solution)/shard_map/ppermute | solution.py:288
  31.5 5.6 %collective-permute-done.11 = bf16[16,64,128]{2,1,0:T(8,128)(2,1)S(1)} collective-permute-done((bf16[16,64,128]{2,1,0:T(8,128)(2,1)}, bf16[16,64,128]{2,1,0:T(8,128)(2,1)S(1)}, u32[]{:S(2)}, u32[]{:S(2)}) %collective-permute-start.11) | collective-permute-done | bytes 262176 | tf_op jit(solution)/shard_map/ppermute | solution.py:346
  37.2 0.8 copy-done.5
  38.0 4.2 %pick_blocks.1 = bf16[160,64,128]{2,1,0:T(8,128)(2,1)} custom-call(s32[160]{0:T(256)} %reshape.243.ids_ref, bf16[16,64,256]{2,1,0:T(8,128)(2,1)} %copy-done.5), custom_call_target="tpu_custom_call" | custom-call | tf_op jit(solution)/shard_map/pick_blocks/pallas_call | solution.py:51
  42.1 14.7 %all-to-all-start.1 = ((bf16[32,320,128]{2,1,0:T(8,128)(2,1)}), bf16[32,320,128]{2,1,0:T(8,128)(2,1)S(1)}, u32[]{:S(2)}, u32[]{:S(2)}) async-start(bf16[32,320,128]{2,1,0:T(8,128)(2,1)} %bitcast.44), calls=%async_computation.1 | async-start | bytes 5242880 | tf_op jit(solution)/shard_map/all_to_all | solution.py:357
  56.8 1.8 join.3.refs_0_
  58.7 2.9 %collective-permute-start.1 = (bf16[512,512]{1,0:T(8,128)(2,1)}, bf16[512,512]{1,0:T(8,128)(2,1)S(1)}, u32[]{:S(2)}, u32[]{:S(2)}) collective-permute-start(bf16[512,512]{1,0:T(8,128)(2,1)} %join.3.refs_0_), channel_id=1, source_target_pairs={{0,2},{1,3},{2,4},{3,5},{4,6},{5,7},{6,8},{7,9},{8,10},{9,11},{10,... | collective-permute-start | bytes 1572872 | tf_op jit(solution)/shard_map/ppermute | solution.py:284
  61.6 3.6 %collective-permute-start.2 = (bf16[512,512]{1,0:T(8,128)(2,1)}, bf16[512,512]{1,0:T(8,128)(2,1)S(1)}, u32[]{:S(2)}, u32[]{:S(2)}) collective-permute-start(bf16[512,512]{1,0:T(8,128)(2,1)} %join.3.refs_0_), channel_id=1, source_target_pairs={{0,14},{1,15},{2,0},{3,1},{4,2},{5,3},{6,4},{7,5},{8,6},{9,7},{10,... | collective-permute-start | bytes 1572872 | tf_op jit(solution)/shard_map/ppermute | solution.py:284
  65.2 9.9 %collective-permute-done.1.refs_1_ = bf16[512,512]{1,0:T(8,128)(2,1)S(1)} collective-permute-done((bf16[512,512]{1,0:T(8,128)(2,1)}, bf16[512,512]{1,0:T(8,128)(2,1)S(1)}, u32[]{:S(2)}, u32[]{:S(2)}) %collective-permute-start.1) | collective-permute-done | bytes 524320 | tf_op jit(solution)/shard_map/ppermute | solution.py:284
  75.1 1.9 collective-permute-start.3
  77.0 4.6 %collective-permute-start.4 = (bf16[512,512]{1,0:T(8,128)(2,1)S(1)}, bf16[512,512]{1,0:T(8,128)(2,1)S(1)}, u32[]{:S(2)}, u32[]{:S(2)}) collective-permute-start(bf16[512,512]{1,0:T(8,128)(2,1)S(1)} %collective-permute-done.2.refs_2_), channel_id=1, source_target_pairs={{0,14},{1,15},{2,0},{3,1},{4,2},{5,3},{6,4},{7,5},{8,6},{9,7},{10,... | collective-permute-start | bytes 1572872 | tf_op jit(solution)/shard_map/ppermute | solution.py:284
  81.6 8.8 %collective-permute-done.3.refs_3_ = bf16[512,512]{1,0:T(8,128)(2,1)S(1)} collective-permute-done((bf16[512,512]{1,0:T(8,128)(2,1)S(1)}, bf16[512,512]{1,0:T(8,128)(2,1)S(1)}, u32[]{:S(2)}, u32[]{:S(2)}) %collective-permute-start.3) | collective-permute-done | bytes 524320 | tf_op jit(solution)/shard_map/ppermute | solution.py:284
  90.4 1.9 collective-permute-start.5
  92.4 4.6 %collective-permute-start.6 = (bf16[512,512]{1,0:T(8,128)(2,1)S(1)}, bf16[512,512]{1,0:T(8,128)(2,1)S(1)}, u32[]{:S(2)}, u32[]{:S(2)}) collective-permute-start(bf16[512,512]{1,0:T(8,128)(2,1)S(1)} %collective-permute-done.4.refs_0_), channel_id=1, source_target_pairs={{0,14},{1,15},{2,0},{3,1},{4,2},{5,3},{6,4},{7,5},{8,6},{9,7},{10,... | collective-permute-start | bytes 1572872 | tf_op jit(solution)/shard_map/ppermute | solution.py:284
  97.0 7.9 %collective-permute-done.5.refs_1_ = bf16[512,512]{1,0:T(8,128)(2,1)S(1)} collective-permute-done((bf16[512,512]{1,0:T(8,128)(2,1)S(1)}, bf16[512,512]{1,0:T(8,128)(2,1)S(1)}, u32[]{:S(2)}, u32[]{:S(2)}) %collective-permute-start.5) | collective-permute-done | bytes 524320 | tf_op jit(solution)/shard_map/ppermute | solution.py:284
  104.9 0.8 slice.33
  105.7 1.9 collective-permute-start.7
  107.6 0.8 copy-done.2
  108.4 0.7 slice.34
  109.1 4.6 %collective-permute-start.8 = (bf16[256,512]{1,0:T(8,128)(2,1)}, bf16[256,512]{1,0:T(8,128)(2,1)}, u32[]{:S(2)}, u32[]{:S(2)}) collective-permute-start(bf16[256,512]{1,0:T(8,128)(2,1)} %slice.34), channel_id=1, source_target_pairs={{0,14},{1,15},{2,0},{3,1},{4,2},{5,3},{6,4},{7,5},{8,6},{9,7},{10,... | collective-permute-start | bytes 786440 | tf_op jit(solution)/shard_map/ppermute | solution.py:284
  113.7 2.9 %join.4 = bf16[2048,512]{1,0:T(8,128)(2,1)} custom-call(bf16[512,512]{1,0:T(8,128)(2,1)} %join.3.refs_0_, bf16[512,512]{1,0:T(8,128)(2,1)} %copy-done.6, bf16[512,512]{1,0:T(8,128)(2,1)} %copy-done.7, bf16[512,512]{1,0:T(8,128)(2,1)} %copy-done.8), custom_call_target="tpu_custom_call" | custom-call | tf_op jit(solution)/shard_map/join/pallas_call | solution.py:231
  116.7 5.4 %collective-permute-start.9 = (bf16[2048,512]{1,0:T(8,128)(2,1)}, bf16[2048,512]{1,0:T(8,128)(2,1)}, u32[]{:S(2)}, u32[]{:S(2)}) collective-permute-start(bf16[2048,512]{1,0:T(8,128)(2,1)} %join.4), channel_id=1, source_target_pairs={{0,16},{1,17},{2,18},{3,19},{4,20},{5,21},{6,22},{7,23},{8,24},{9,... | collective-permute-start | bytes 6291464 | tf_op jit(solution)/shard_map/ppermute | solution.py:288
  122.1 0.7 copy-done.10
  122.8 2.9 %join.5 = bf16[2048,512]{1,0:T(8,128)(2,1)} custom-call(bf16[512,512]{1,0:T(8,128)(2,1)} %copy-done.9, bf16[512,512]{1,0:T(8,128)(2,1)} %copy-done.1, bf16[512,512]{1,0:T(8,128)(2,1)} %copy-done.2, bf16[256,512]{1,0:T(8,128)(2,1)} %copy-done.10, bf16[256,512]{1,0:T(8,128)(2,1)} %collective-permute-done.8.refs_4_), custom_call_target="tpu_custom_call" | custom-call | tf_op jit(solution)/shard_map/join/pallas_call | solution.py:231
  125.7 1.9 collective-permute-start.10
  127.6 0.2 convert_reduce_fusion.2
  127.8 0.1 reduce_sum.39
  127.9 0.1 mul.26
  128.0 0.6 reshape.242.pos_ref
  128.6 3.4 %collective-permute-done.10 = bf16[2048,512]{1,0:T(8,128)(2,1)} collective-permute-done((bf16[2048,512]{1,0:T(8,128)(2,1)}, bf16[2048,512]{1,0:T(8,128)(2,1)}, u32[]{:S(2)}, u32[]{:S(2)}) %collective-permute-start.10) | collective-permute-done | bytes 2097184 | tf_op jit(solution)/shard_map/ppermute | solution.py:288
  132.1 1.5 copy-done
  133.6 3.5 %place_blocks.1 = bf16[16,64,896]{2,1,0:T(8,128)(2,1)} custom-call(s32[112]{0:T(128)} %reshape.242.pos_ref, bf16[160,64,128]{2,1,0:T(8,128)(2,1)} %bitcast.43), custom_call_target="tpu_custom_call" | custom-call | tf_op jit(solution)/shard_map/place_blocks/pallas_call | solution.py:76
  137.0 7.5 %all-to-all-start.2 = ((bf16[16,64,896]{2,1,0:T(8,128)(2,1)}), bf16[16,64,896]{2,1,0:T(8,128)(2,1)S(1)}, u32[]{:S(2)}, u32[]{:S(2)}) async-start(bf16[16,64,896]{2,1,0:T(8,128)(2,1)} %place_blocks.1), calls=%async_computation.2 | async-start | bytes 3670016 | tf_op jit(solution)/shard_map/all_to_all | solution.py:369
  144.5 0.3 reduce-window.9
  144.8 0.1 slice.27
  144.9 0.1 slice_reduce_fusion
  145.1 0.4 convert_reduce_fusion
  145.5 0.2 compare_select_fusion
  145.7 0.8 pad_maximum_fusion.1.mask_ref
  146.5 1.2 pad_maximum_fusion
  147.6 7.3 %assemble.1 = (bf16[16,64,1024]{2,1,0:T(8,128)(2,1)}, bf16[16,64,1024]{2,1,0:T(8,128)(2,1)}, bf16[16,64,1024]{2,1,0:T(8,128)(2,1)}, bf16[16,64,1024]{2,1,0:T(8,128)(2,1)}) custom-call(s32[1]{0:T(128)} %bitcast.core_ref, bf16[2,256,512]{2,1,0:T(8,128)(2,1)} %bitcast.45, bf16[2,256,512]{2,1,0:T(8,128)(2,1)} %bitcast.50, bf16[2,256,512]{2,1,0:T(8,128)(2,1)} %bitcast.51, ...), custom_call_target="tpu_custom_call" | custom-call | tf_op jit(solution)/shard_map/assemble/pallas_call | solution.py:268
  154.9 3.2 %fusion.2.qt_ref = bf16[1024,256]{1,0:T(8,128)(2,1)} fusion(bf16[1024,1024]{1,0:T(8,128)(2,1)} %bitcast.67, bf16[1024,256]{1,0:T(8,128)(2,1)S(1)} %bitcast.49), kind=kOutput, calls=%fused_computation.10 | convolution fusion | flops 537919488 | bytes 3145728 | tf_op jit(solution)/shard_map/dot_general | solution.py:382
  158.2 2.3 %convolution_convert_fusion.2.vt_ref = bf16[1024,512]{1,0:T(8,128)(2,1)} fusion(bf16[1024,1024]{1,0:T(8,128)(2,1)S(1)} %bitcast.66, bf16[1024,512]{1,0:T(8,128)(2,1)S(1)} %bitcast.57), kind=kOutput, calls=%fused_computation.4 | convolution fusion | flops 1074266112 | bytes 4194304 | tf_op jit(solution)/shard_map/dot_general | solution.py:385
  160.5 2.3 %convolution_convert_fusion.3.k_ref = bf16[512,1024]{1,0:T(8,128)(2,1)} fusion(bf16[1024,512]{1,0:T(8,128)(2,1)S(1)} %bitcast.58, bf16[1024,1024]{1,0:T(8,128)(2,1)S(1)} %bitcast.63), kind=kOutput, calls=%fused_computation.5 | convolution fusion | flops 1074266112 | bytes 4194304 | tf_op jit(solution)/shard_map/dot_general | solution.py:384
  162.7 9.4 %near_attention.1 = (f32[1024,256]{1,0:T(8,128)}, f32[8,2,8,256]{3,2,1,0:T(8,128)}, f32[8,2,8,256]{3,2,1,0:T(8,128)}) custom-call(bf16[1024,256]{1,0:T(8,128)(2,1)} %fusion.2.qt_ref, bf16[512,1024]{1,0:T(8,128)(2,1)} %convolution_convert_fusion.3.k_ref, bf16[1024,512]{1,0:T(8,128)(2,1)} %convolution_convert_fusion.2.vt_ref, ...), custom_call_target="tpu_custom_call" | custom-call | tf_op jit(solution)/shard_map/near_attention/pallas_call | solution.py:162
  172.2 14.5 %all-to-all-done.2 = bf16[16,64,896]{2,1,0:T(8,128)(2,1)S(1)} async-done(((bf16[16,64,896]{2,1,0:T(8,128)(2,1)}), bf16[16,64,896]{2,1,0:T(8,128)(2,1)S(1)}, u32[]{:S(2)}, u32[]{:S(2)}) %all-to-all-start.2) | async-done | bytes 1835040 | tf_op jit(solution)/shard_map/all_to_all | solution.py:369
  186.6 5.3 %convolution_convert_fusion.vt_ref = bf16[1024,896]{1,0:T(8,128)(2,1)} fusion(bf16[1024,1024]{1,0:T(8,128)(2,1)} %bitcast.65, bf16[1024,896]{1,0:T(8,128)(2,1)S(1)} %bitcast.54), kind=kOutput, calls=%fused_computation.1 | convolution fusion | flops 1879965696 | bytes 5767168 | tf_op jit(solution)/shard_map/dot_general | solution.py:388
  191.9 3.4 %convolution_convert_fusion.1.k_ref = bf16[896,1024]{1,0:T(8,128)(2,1)} fusion(bf16[1024,896]{1,0:T(8,128)(2,1)S(1)} %bitcast.55, bf16[1024,1024]{1,0:T(8,128)(2,1)S(1)} %bitcast.64), kind=kOutput, calls=%fused_computation.2 | convolution fusion | flops 1879965696 | bytes 5767168 | tf_op jit(solution)/shard_map/dot_general | solution.py:387
  195.3 10.3 %far_attention.1 = bf16[1024,256]{1,0:T(8,128)(2,1)} custom-call(bf16[1024,256]{1,0:T(8,128)(2,1)} %fusion.2.qt_ref, bf16[896,1024]{1,0:T(8,128)(2,1)} %convolution_convert_fusion.1.k_ref, bf16[1024,896]{1,0:T(8,128)(2,1)} %convolution_convert_fusion.vt_ref, f32[1024,256]{1,0:T(8,128)} %get-tuple-element.25.acc_ref, ...), custom_call_target="tpu_custom_call" | custom-call | tf_op jit(solution)/shard_map/far_attention/pallas_call | solution.py:175
  205.6 2.6 %fusion.3 = bf16[256,1024]{1,0:T(8,128)(2,1)} fusion(bf16[1024,256]{1,0:T(8,128)(2,1)} %far_attention.1, bf16[1024,1024]{1,0:T(8,128)(2,1)S(1)} %bitcast.48, f32[1024]{0:T(1024)S(1)} %copy-done.14), kind=kOutput, calls=%fused_computation.11 | convolution fusion | flops 537395200 | bytes 3149824 | tf_op jit(solution)/shard_map/dot_general | solution.py:390
  (59 shorter events, 0.3 us)
Async XLA Ops:
  0.0 20.3 %copy-start.15 = (s32[1024,3]{0,1:T(4,128)S(1)}, s32[1024,3]{0,1:T(4,128)}, u32[]{:S(2)}) copy-start(s32[1024,3]{0,1:T(4,128)} %param.16) | copy-start | bytes 36868
  0.0 20.8 %copy-start.16 = (s32[1024,3]{0,1:T(4,128)S(1)}, s32[1024,3]{0,1:T(4,128)}, u32[]{:S(2)}) copy-start(s32[1024,3]{0,1:T(4,128)} %param.17) | copy-start | bytes 36868
  2.5 34.7 %all-to-all-start = ((bf16[16,64,256]{2,1,0:T(8,128)(2,1)}), bf16[16,64,256]{2,1,0:T(8,128)(2,1)S(1)}, u32[]{:S(2)}, u32[]{:S(2)}) async-start(bf16[16,64,256]{2,1,0:T(8,128)(2,1)} %get-tuple-element.18), calls=%async_computation | async-start | bytes 1048576 | tf_op jit(solution)/shard_map/all_to_all | solution.py:338
  12.1 19.4 %collective-permute-start = (bf16[256,512]{1,0:T(8,128)(2,1)}, bf16[256,512]{1,0:T(8,128)(2,1)S(1)}, u32[]{:S(2)}, u32[]{:S(2)}) collective-permute-start(bf16[256,512]{1,0:T(8,128)(2,1)} %own_piece.1.refs_0_), channel_id=1, source_target_pairs={{0,1},{1,0},{2,3},{3,2},{4,5},{5,4},{6,7},{7,6},{8,9},{9,8},{10,11... | collective-permute-start | bytes 786440 | tf_op jit(solution)/shard_map/ppermute | solution.py:288
  14.2 22.9 %collective-permute-start.11 = (bf16[16,64,128]{2,1,0:T(8,128)(2,1)}, bf16[16,64,128]{2,1,0:T(8,128)(2,1)S(1)}, u32[]{:S(2)}, u32[]{:S(2)}) collective-permute-start(bf16[16,64,128]{2,1,0:T(8,128)(2,1)} %get-tuple-element.20), channel_id=1, source_target_pairs={{0,1},{1,2},{2,3},{3,4},{4,5},{5,6},{6,7},{7,8},{8,9},{9,10},{10,1... | collective-permute-start | bytes 786440 | tf_op jit(solution)/shard_map/ppermute | solution.py:346
  18.3 18.8 %collective-permute-start.12 = (bf16[16,64,128]{2,1,0:T(8,128)(2,1)}, bf16[16,64,128]{2,1,0:T(8,128)(2,1)S(1)}, u32[]{:S(2)}, u32[]{:S(2)}) collective-permute-start(bf16[16,64,128]{2,1,0:T(8,128)(2,1)} %get-tuple-element.21), channel_id=1, source_target_pairs={{1,0},{2,1},{3,2},{4,3},{5,4},{6,5},{7,6},{8,7},{9,8},{10,9},{11,1... | collective-permute-start | bytes 786440 | tf_op jit(solution)/shard_map/ppermute | solution.py:347
  31.5 25.3 %copy-start.11 = (bf16[256,512]{1,0:T(8,128)(2,1)}, bf16[256,512]{1,0:T(8,128)(2,1)S(1)}, u32[]{:S(2)}) copy-start(bf16[256,512]{1,0:T(8,128)(2,1)S(1)} %collective-permute-done.refs_1_) | copy-start | bytes 786436
  37.1 5.0 %copy-start.12 = (bf16[16,64,128]{2,1,0:T(8,128)(2,1)}, bf16[16,64,128]{2,1,0:T(8,128)(2,1)S(1)}, u32[]{:S(2)}) copy-start(bf16[16,64,128]{2,1,0:T(8,128)(2,1)S(1)} %collective-permute-done.11) | copy-start | bytes 786436
  37.1 5.0 %copy-start.13 = (bf16[16,64,128]{2,1,0:T(8,128)(2,1)}, bf16[16,64,128]{2,1,0:T(8,128)(2,1)S(1)}, u32[]{:S(2)}) copy-start(bf16[16,64,128]{2,1,0:T(8,128)(2,1)S(1)} %collective-permute-done.12) | copy-start | bytes 786436
  37.1 0.8 copy-start.5
  42.1 89.9 %all-to-all-start.1 = ((bf16[32,320,128]{2,1,0:T(8,128)(2,1)}), bf16[32,320,128]{2,1,0:T(8,128)(2,1)S(1)}, u32[]{:S(2)}, u32[]{:S(2)}) async-start(bf16[32,320,128]{2,1,0:T(8,128)(2,1)} %bitcast.44), calls=%async_computation.1 | async-start | bytes 5242880 | tf_op jit(solution)/shard_map/all_to_all | solution.py:357
  58.7 16.4 %collective-permute-start.1 = (bf16[512,512]{1,0:T(8,128)(2,1)}, bf16[512,512]{1,0:T(8,128)(2,1)S(1)}, u32[]{:S(2)}, u32[]{:S(2)}) collective-permute-start(bf16[512,512]{1,0:T(8,128)(2,1)} %join.3.refs_0_), channel_id=1, source_target_pairs={{0,2},{1,3},{2,4},{3,5},{4,6},{5,7},{6,8},{7,9},{8,10},{9,11},{10,... | collective-permute-start | bytes 1572872 | tf_op jit(solution)/shard_map/ppermute | solution.py:284
  61.6 15.4 %collective-permute-start.2 = (bf16[512,512]{1,0:T(8,128)(2,1)}, bf16[512,512]{1,0:T(8,128)(2,1)S(1)}, u32[]{:S(2)}, u32[]{:S(2)}) collective-permute-start(bf16[512,512]{1,0:T(8,128)(2,1)} %join.3.refs_0_), channel_id=1, source_target_pairs={{0,14},{1,15},{2,0},{3,1},{4,2},{5,3},{6,4},{7,5},{8,6},{9,7},{10,... | collective-permute-start | bytes 1572872 | tf_op jit(solution)/shard_map/ppermute | solution.py:284
  75.1 17.3 %copy-start.6 = (bf16[512,512]{1,0:T(8,128)(2,1)}, bf16[512,512]{1,0:T(8,128)(2,1)S(1)}, u32[]{:S(2)}) copy-start(bf16[512,512]{1,0:T(8,128)(2,1)S(1)} %collective-permute-done.1.refs_1_) | copy-start | bytes 1572868
  75.1 15.3 %collective-permute-start.3 = (bf16[512,512]{1,0:T(8,128)(2,1)S(1)}, bf16[512,512]{1,0:T(8,128)(2,1)S(1)}, u32[]{:S(2)}, u32[]{:S(2)}) collective-permute-start(bf16[512,512]{1,0:T(8,128)(2,1)S(1)} %collective-permute-done.1.refs_1_), channel_id=1, source_target_pairs={{0,2},{1,3},{2,4},{3,5},{4,6},{5,7},{6,8},{7,9},{8,10},{9,11},{10,... | collective-permute-start | bytes 1572872 | tf_op jit(solution)/shard_map/ppermute | solution.py:284
  77.0 19.9 %copy-start.7 = (bf16[512,512]{1,0:T(8,128)(2,1)}, bf16[512,512]{1,0:T(8,128)(2,1)S(1)}, u32[]{:S(2)}) copy-start(bf16[512,512]{1,0:T(8,128)(2,1)S(1)} %collective-permute-done.2.refs_2_) | copy-start | bytes 1572868
  77.0 15.3 %collective-permute-start.4 = (bf16[512,512]{1,0:T(8,128)(2,1)S(1)}, bf16[512,512]{1,0:T(8,128)(2,1)S(1)}, u32[]{:S(2)}, u32[]{:S(2)}) collective-permute-start(bf16[512,512]{1,0:T(8,128)(2,1)S(1)} %collective-permute-done.2.refs_2_), channel_id=1, source_target_pairs={{0,14},{1,15},{2,0},{3,1},{4,2},{5,3},{6,4},{7,5},{8,6},{9,7},{10,... | collective-permute-start | bytes 1572872 | tf_op jit(solution)/shard_map/ppermute | solution.py:284
  90.4 6.5 %copy-start.8 = (bf16[512,512]{1,0:T(8,128)(2,1)}, bf16[512,512]{1,0:T(8,128)(2,1)S(1)}, u32[]{:S(2)}) copy-start(bf16[512,512]{1,0:T(8,128)(2,1)S(1)} %collective-permute-done.3.refs_3_) | copy-start | bytes 1572868
  90.4 14.5 %collective-permute-start.5 = (bf16[512,512]{1,0:T(8,128)(2,1)S(1)}, bf16[512,512]{1,0:T(8,128)(2,1)S(1)}, u32[]{:S(2)}, u32[]{:S(2)}) collective-permute-start(bf16[512,512]{1,0:T(8,128)(2,1)S(1)} %collective-permute-done.3.refs_3_), channel_id=1, source_target_pairs={{0,2},{1,3},{2,4},{3,5},{4,6},{5,7},{6,8},{7,9},{8,10},{9,11},{10,... | collective-permute-start | bytes 1572872 | tf_op jit(solution)/shard_map/ppermute | solution.py:284
  92.4 16.8 %copy-start.9 = (bf16[512,512]{1,0:T(8,128)(2,1)}, bf16[512,512]{1,0:T(8,128)(2,1)S(1)}, u32[]{:S(2)}) copy-start(bf16[512,512]{1,0:T(8,128)(2,1)S(1)} %collective-permute-done.4.refs_0_) | copy-start | bytes 1572868
  92.4 15.2 %collective-permute-start.6 = (bf16[512,512]{1,0:T(8,128)(2,1)S(1)}, bf16[512,512]{1,0:T(8,128)(2,1)S(1)}, u32[]{:S(2)}, u32[]{:S(2)}) collective-permute-start(bf16[512,512]{1,0:T(8,128)(2,1)S(1)} %collective-permute-done.4.refs_0_), channel_id=1, source_target_pairs={{0,14},{1,15},{2,0},{3,1},{4,2},{5,3},{6,4},{7,5},{8,6},{9,7},{10,... | collective-permute-start | bytes 1572872 | tf_op jit(solution)/shard_map/ppermute | solution.py:284
  104.9 11.7 %copy-start.1 = (bf16[512,512]{1,0:T(8,128)(2,1)}, bf16[512,512]{1,0:T(8,128)(2,1)S(1)}, u32[]{:S(2)}) copy-start(bf16[512,512]{1,0:T(8,128)(2,1)S(1)} %collective-permute-done.5.refs_1_) | copy-start | bytes 1572868
  105.7 16.4 %collective-permute-start.7 = (bf16[256,512]{1,0:T(8,128)(2,1)}, bf16[256,512]{1,0:T(8,128)(2,1)S(1)}, u32[]{:S(2)}, u32[]{:S(2)}) collective-permute-start(bf16[256,512]{1,0:T(8,128)(2,1)} %slice.33), channel_id=1, source_target_pairs={{0,2},{1,3},{2,4},{3,5},{4,6},{5,7},{6,8},{7,9},{8,10},{9,11},{10,... | collective-permute-start | bytes 786440 | tf_op jit(solution)/shard_map/ppermute | solution.py:284
  107.6 0.8 copy-start.2
  109.1 13.0 %collective-permute-start.8 = (bf16[256,512]{1,0:T(8,128)(2,1)}, bf16[256,512]{1,0:T(8,128)(2,1)}, u32[]{:S(2)}, u32[]{:S(2)}) collective-permute-start(bf16[256,512]{1,0:T(8,128)(2,1)} %slice.34), channel_id=1, source_target_pairs={{0,14},{1,15},{2,0},{3,1},{4,2},{5,3},{6,4},{7,5},{8,6},{9,7},{10,... | collective-permute-start | bytes 786440 | tf_op jit(solution)/shard_map/ppermute | solution.py:284
  116.7 12.0 %collective-permute-start.9 = (bf16[2048,512]{1,0:T(8,128)(2,1)}, bf16[2048,512]{1,0:T(8,128)(2,1)}, u32[]{:S(2)}, u32[]{:S(2)}) collective-permute-start(bf16[2048,512]{1,0:T(8,128)(2,1)} %join.4), channel_id=1, source_target_pairs={{0,16},{1,17},{2,18},{3,19},{4,20},{5,21},{6,22},{7,23},{8,24},{9,... | collective-permute-start | bytes 6291464 | tf_op jit(solution)/shard_map/ppermute | solution.py:288
  122.1 0.7 copy-start.10
  125.7 6.4 %collective-permute-start.10 = (bf16[2048,512]{1,0:T(8,128)(2,1)}, bf16[2048,512]{1,0:T(8,128)(2,1)}, u32[]{:S(2)}, u32[]{:S(2)}) collective-permute-start(bf16[2048,512]{1,0:T(8,128)(2,1)} %join.5), channel_id=1, source_target_pairs={{0,16},{1,17},{2,18},{3,19},{4,20},{5,21},{6,22},{7,23},{8,24},{9,... | collective-permute-start | bytes 6291464 | tf_op jit(solution)/shard_map/ppermute | solution.py:288
  132.1 1.5 copy-start
  137.0 7.5 %copy-start.17 = (s32[1024]{0:T(1024)S(1)}, s32[1024]{0:T(1024)}, u32[]{:S(2)}) copy-start(s32[1024]{0:T(1024)} %param.15) | copy-start | bytes 12292
  137.0 9.4 %copy-start.4 = (bf16[16,64,256]{2,1,0:T(8,128)(2,1)S(1)}, bf16[16,64,256]{2,1,0:T(8,128)(2,1)}, u32[]{:S(2)}) copy-start(bf16[16,64,256]{2,1,0:T(8,128)(2,1)} %get-tuple-element.18) | copy-start | bytes 1572868
  137.0 49.6 %all-to-all-start.2 = ((bf16[16,64,896]{2,1,0:T(8,128)(2,1)}), bf16[16,64,896]{2,1,0:T(8,128)(2,1)S(1)}, u32[]{:S(2)}, u32[]{:S(2)}) async-start(bf16[16,64,896]{2,1,0:T(8,128)(2,1)} %place_blocks.1), calls=%async_computation.2 | async-start | bytes 3670016 | tf_op jit(solution)/shard_map/all_to_all | solution.py:369
  154.9 3.3 %copy-start.20 = (bf16[16,64,1024]{2,1,0:T(8,128)(2,1)S(1)}, bf16[16,64,1024]{2,1,0:T(8,128)(2,1)}, u32[]{:S(2)}) copy-start(bf16[16,64,1024]{2,1,0:T(8,128)(2,1)} %get-tuple-element.24) | copy-start | bytes 6291460
  158.2 2.3 %copy-start.18 = (bf16[16,64,1024]{2,1,0:T(8,128)(2,1)S(1)}, bf16[16,64,1024]{2,1,0:T(8,128)(2,1)}, u32[]{:S(2)}) copy-start(bf16[16,64,1024]{2,1,0:T(8,128)(2,1)} %get-tuple-element.23) | copy-start | bytes 6291460
  186.6 5.3 %copy-start.19 = (bf16[16,64,1024]{2,1,0:T(8,128)(2,1)S(1)}, bf16[16,64,1024]{2,1,0:T(8,128)(2,1)}, u32[]{:S(2)}) copy-start(bf16[16,64,1024]{2,1,0:T(8,128)(2,1)} %get-tuple-element.23) | copy-start | bytes 6291460
  195.3 10.3 %copy-start.3 = (bf16[16,64,1024]{2,1,0:T(8,128)(2,1)S(1)}, bf16[16,64,1024]{2,1,0:T(8,128)(2,1)}, u32[]{:S(2)}) copy-start(bf16[16,64,1024]{2,1,0:T(8,128)(2,1)} %get-tuple-element.28) | copy-start | bytes 6291460
  195.3 10.3 %copy-start.14 = (f32[1024]{0:T(1024)S(1)}, f32[1024]{0:T(1024)}, u32[]{:S(2)}) copy-start(f32[1024]{0:T(1024)} %param.14) | copy-start | bytes 12292

commit v6 on v5

--- a/solution.py
+++ b/solution.py
@@ -216,28 +216,6 @@
     )(core, wt, out_w)
 
 
-def join_kernel(*refs):
-    parts, out_ref, sems = refs[:-2], refs[-2], refs[-1]
-    copies, row = [], 0
-    for n, part in enumerate(parts):
-        into = out_ref.at[pl.ds(row, part.shape[0])]
-        copies.append(pltpu.make_async_copy(part, into, sems.at[n]))
-        row += part.shape[0]
-    run_copies(copies)
-
-
-def join(*parts):
-    rows = sum(part.shape[0] for part in parts)
-    return pl.pallas_call(
-        join_kernel,
-        out_shape=jax.ShapeDtypeStruct((rows,) + parts[0].shape[1:], jnp.bfloat16),
-        in_specs=any_specs(len(parts)),
-        out_specs=pl.BlockSpec(memory_space=pltpu.VMEM),
-        scratch_shapes=[pltpu.SemaphoreType.DMA((len(parts),))],
-        name="join",
-    )(*parts)
-
-
 def assemble_kernel(core_ref, *refs):
     sems = refs[-1]
     outs, parts = refs[-5:-1], refs[:-5]
@@ -262,8 +240,7 @@
 
 
 def assemble(core, parts, heads, hd):
-    cols = parts[0].shape[1]
-    parts = [part.reshape(-1, 4 * hd, cols) for part in parts]
+    cols = parts[0].shape[2]
     one = jax.ShapeDtypeStruct((heads, hd, 2 * cols), jnp.bfloat16)
     return pl.pallas_call(
         assemble_kernel,
@@ -277,11 +254,6 @@
 
 def tied(value, *others):
     return lax.optimization_barrier((value,) + others)[0]
-
-
-def shift(value, by, heads):
-    pairs = [(i, (i + by) % heads) for i in range(heads)]
-    return lax.ppermute(value, "head", pairs)
 
 
 def swap(value, bits, devices):
@@ -338,7 +310,8 @@
     cells = lax.all_to_all(normed_t, "head", split_axis=0, concat_axis=0, tiled=True)
 
     own = own_piece(core, wt, out_weight)
-    beside = swap(own, 1, devices)
+    along_y = [list(range(first_x, heads, 2)) for first_x in range(2)]
+    column = lax.all_gather(own, "head", axis_index_groups=along_y)
 
     both = ("ctx", "head")
     right = [(i, i + 1) for i in range(devices - 1)]
@@ -352,20 +325,19 @@
     send, take = exchange_plan(
         pairs_dev, pairs_off, ctx_count, ctx_index, lower, pair_count // heads
     )
-    outgoing = pick_blocks(tied(send, beside, before, after), cells)
+    outgoing = pick_blocks(tied(send, before, after), cells)
     outgoing = outgoing.reshape(ctx_count, SLOTS * hd, BLK)
     slots = lax.all_to_all(outgoing, "ctx", split_axis=0, concat_axis=0, tiled=True)
     slots = slots.reshape(ctx_count * SLOTS, hd, BLK)
 
-    mid = own.shape[0]
-    two = join(own, beside)
-    u1, d1 = shift(two, 2, heads), shift(two, -2, heads)
-    u2, d2 = shift(u1, 2, heads), shift(d1, -2, heads)
-    u3, d3 = shift(u2, 2, heads), shift(d2, -2, heads)
-    u4, d4 = shift(u3[:mid], 2, heads), shift(d3[mid:], -2, heads)
-    mine = [two, u1, d1, u2, d2, u3, d3, u4, d4]
-    other = [swap(join(*part), heads, devices) for part in (mine[:4], mine[4:])]
-    placed = place_blocks(tied(take, *other), slots, heads)
+    half = column.shape[0] // 2
+    mine = [
+        column,
+        swap(column[:half], 1, devices),
+        swap(column[half:], 2 * heads + 1, devices),
+    ]
+    other = [swap(part, heads, devices) for part in mine]
+    placed = place_blocks(tied(take, mine[1], mine[2], other[0]), slots, heads)
     far = lax.all_to_all(placed, "head", split_axis=0, concat_axis=0, tiled=True)
     far = far.reshape(width, far.shape[2])
 

time: 212 us -> 207 us (0.976)
  the two profiles are of different devices: /device:TPU:7 before, /device:TPU:4 now
where the time goes in v6:
time: 207 us; the launch traced here: 206 us
  waiting for transfers between devices  71 us (34%)
  starting transfers between devices  49.8 us (24%)
  Pallas kernels  38.3 us (19%)
  matrix products  19 us (9%)
  between operations  13.7 us (7%)
  local copies, waits for them, and re-layouts  9.22 us (4%)
  other arithmetic  4.91 us (2%)
    ppermute x5, waiting for transfers between devices, swap(): lax.ppermute(value, ('ctx', 'head'), [(i, i ^ bits) for i in range(device...  39 us
    all_to_all x1, starting transfers between devices, per_device(): lax.all_to_all(outgoing, 'ctx', split_axis=0, concat_axis=0, tiled=True)  13.4 us
    all_to_all x1, waiting for transfers between devices, per_device(): lax.all_to_all(placed, 'head', split_axis=0, concat_axis=0, tiled=True)  11.5 us
    ppermute x5, starting transfers between devices, swap(): lax.ppermute(value, ('ctx', 'head'), [(i, i ^ bits) for i in range(device...  11.4 us
    all_gather x1, waiting for transfers between devices, per_device(): column = lax.all_gather(own, 'head', axis_index_groups=along_y)  10.9 us
    pallas_call x1, Pallas kernels, far_attention(): pl.pallas_call(far_kernel, out_shape=jax.ShapeDtypeStruct((width, rows),...  10.3 us
    pallas_call x1, Pallas kernels, near_attention(): pl.pallas_call(near_kernel, out_shape=(jax.ShapeDtypeStruct((width, rows)...  9.46 us
    all_to_all x1, starting transfers between devices, per_device(): lax.all_to_all(placed, 'head', split_axis=0, concat_axis=0, tiled=True)  9.23 us
  transfers between devices with their start and end apart: 11, of which 7 were waited for; matrix products, arithmetic and copies ran while one was open for 9% of the time, Pallas kernels for 11%

profile of v6, /device:TPU:4, one launch (start us, length us, event | category | flops | bytes accessed | tf_op | source)
XLA Modules:
  0.0 205.9 jit_solution(3229880104510959154)
XLA Ops:
  6.5 2.5 %layer_norm.1 = (bf16[16,64,256]{2,1,0:T(8,128)(2,1)}, bf16[16,64,128]{2,1,0:T(8,128)(2,1)}, bf16[16,64,128]{2,1,0:T(8,128)(2,1)}) custom-call(bf16[256,1024]{1,0:T(8,128)(2,1)} %tok_ref.1, f32[1,1024]{1,0:T(1,128)} %bitcast.46, f32[1,1024]{1,0:T(1,128)} %bitcast.47), custom_call_target="tpu_custom_call" | custom-call | tf_op jit(solution)/shard_map/layer_norm/pallas_call | solution.py:30
  9.0 8.0 %all-to-all-start = ((bf16[16,64,256]{2,1,0:T(8,128)(2,1)}), bf16[16,64,256]{2,1,0:T(8,128)(2,1)S(1)}, u32[]{:S(2)}, u32[]{:S(2)}) async-start(bf16[16,64,256]{2,1,0:T(8,128)(2,1)} %get-tuple-element.18), calls=%async_computation | async-start | bytes 1048576 | tf_op jit(solution)/shard_map/all_to_all | solution.py:310
  17.0 0.0 all-gather.3.cloned.1.call-start
  17.1 1.7 own_piece.1
  18.7 0.0 all-gather.3.cloned.1.call-update
  18.8 0.0 copy-done.16
  18.8 3.8 %collective-permute-start.5 = (bf16[16,64,128]{2,1,0:T(8,128)(2,1)S(1)}, bf16[16,64,128]{2,1,0:T(8,128)(2,1)S(1)}, u32[]{:S(2)}, u32[]{:S(2)}) collective-permute-start(bf16[16,64,128]{2,1,0:T(8,128)(2,1)S(1)} %copy-done.16), channel_id=1, source_target_pairs={{0,1},{1,2},{2,3},{3,4},{4,5},{5,6},{6,7},{7,8},{8,9},{9,10},{10,1... | collective-permute-start | bytes 786440 | tf_op jit(solution)/shard_map/ppermute | solution.py:319
  22.6 3.8 %collective-permute-start.6 = (bf16[16,64,128]{2,1,0:T(8,128)(2,1)S(1)}, bf16[16,64,128]{2,1,0:T(8,128)(2,1)S(1)}, u32[]{:S(2)}, u32[]{:S(2)}) collective-permute-start(bf16[16,64,128]{2,1,0:T(8,128)(2,1)S(1)} %copy-done.15), channel_id=1, source_target_pairs={{1,0},{2,1},{3,2},{4,3},{5,4},{6,5},{7,6},{8,7},{9,8},{10,9},{11,1... | collective-permute-start | bytes 786440 | tf_op jit(solution)/shard_map/ppermute | solution.py:320
  26.5 0.2 copy.12
  26.7 0.3 reshape.197
  27.0 0.2 copy.13
  27.3 0.3 broadcast_in_dim.28
  27.5 0.6 convert_reduce_fusion.1
  28.2 0.1 select_reduce_fusion
  28.3 0.1 copy.15
  28.4 0.7 reshape.199.ids_ref
  29.1 8.7 %collective-permute-done.5 = bf16[16,64,128]{2,1,0:T(8,128)(2,1)S(1)} collective-permute-done((bf16[16,64,128]{2,1,0:T(8,128)(2,1)S(1)}, bf16[16,64,128]{2,1,0:T(8,128)(2,1)S(1)}, u32[]{:S(2)}, u32[]{:S(2)}) %collective-permute-start.5) | collective-permute-done | bytes 262176 | tf_op jit(solution)/shard_map/ppermute | solution.py:319
  37.8 0.8 collective-permute-done.6
  38.6 0.0 all-to-all-done.cells_ref
  38.6 0.8 copy-done.3
  39.4 4.2 %pick_blocks.1 = bf16[160,64,128]{2,1,0:T(8,128)(2,1)} custom-call(s32[160]{0:T(256)} %reshape.199.ids_ref, bf16[16,64,256]{2,1,0:T(8,128)(2,1)} %copy-done.3), custom_call_target="tpu_custom_call" | custom-call | tf_op jit(solution)/shard_map/pick_blocks/pallas_call | solution.py:51
  43.6 13.4 %all-to-all-start.1 = ((bf16[32,320,128]{2,1,0:T(8,128)(2,1)}), bf16[32,320,128]{2,1,0:T(8,128)(2,1)S(1)}, u32[]{:S(2)}, u32[]{:S(2)}) async-start(bf16[32,320,128]{2,1,0:T(8,128)(2,1)} %bitcast.36), calls=%async_computation.1 | async-start | bytes 5242880 | tf_op jit(solution)/shard_map/all_to_all | solution.py:330
  57.0 10.9 %all-gather.3.cloned.1.call-done = bf16[2048,512]{1,0:T(8,128)(2,1)} async-done(((bf16[256,512]{1,0:T(8,128)(2,1)}), bf16[2048,512]{1,0:T(8,128)(2,1)}) %all-gather.3.cloned.1.call-update) | async-done | bytes 2097168 | tf_op jit(solution)/shard_map/all_gather | solution.py:314
  67.9 1.9 collective-permute-start.2
  69.8 3.1 %fusion.6 = (bf16[1024,512]{1,0:T(8,128)(2,1)}, bf16[1024,512]{1,0:T(8,128)(2,1)}) fusion(bf16[2048,512]{1,0:T(8,128)(2,1)} %all-gather.3.cloned.1.call-done), kind=kLoop, calls=%fused_computation.29 | loop fusion | bytes 4194304 | tf_op jit(solution)/shard_map/slice | solution.py:337
  72.9 3.1 %collective-permute-start = (bf16[4,256,512]{2,1,0:T(8,128)(2,1)}, bf16[4,256,512]{2,1,0:T(8,128)(2,1)}, u32[]{:S(2)}, u32[]{:S(2)}) collective-permute-start(bf16[4,256,512]{2,1,0:T(8,128)(2,1)} %bitcast.4), channel_id=1, source_target_pairs={{0,1},{1,0},{2,3},{3,2},{4,5},{5,4},{6,7},{7,6},{8,9},{9,8},{10,11... | collective-permute-start | bytes 3145736 | tf_op jit(solution)/shard_map/ppermute | solution.py:260
  76.0 1.9 collective-permute-start.1
  77.9 0.2 convert_reduce_fusion.2
  78.1 0.1 reduce_sum.39
  78.2 0.1 mul.26
  78.3 0.6 reshape.198.pos_ref
  78.9 38.7 %collective-permute-done.refs_1_ = bf16[4,256,512]{2,1,0:T(8,128)(2,1)} collective-permute-done((bf16[4,256,512]{2,1,0:T(8,128)(2,1)}, bf16[4,256,512]{2,1,0:T(8,128)(2,1)}, u32[]{:S(2)}, u32[]{:S(2)}) %collective-permute-start) | collective-permute-done | bytes 1048608 | tf_op jit(solution)/shard_map/ppermute | solution.py:260
  117.6 0.3 collective-permute-done.1.refs_2_
  117.9 0.0 collective-permute-done.2.refs_3_
  117.9 0.2 all-to-all-done.1
  118.1 1.5 copy-done
  119.6 3.5 %place_blocks.1 = bf16[16,64,896]{2,1,0:T(8,128)(2,1)} custom-call(s32[112]{0:T(128)} %reshape.198.pos_ref, bf16[160,64,128]{2,1,0:T(8,128)(2,1)} %bitcast.35), custom_call_target="tpu_custom_call" | custom-call | tf_op jit(solution)/shard_map/place_blocks/pallas_call | solution.py:76
  123.1 9.2 %all-to-all-start.2 = ((bf16[16,64,896]{2,1,0:T(8,128)(2,1)}), bf16[16,64,896]{2,1,0:T(8,128)(2,1)S(1)}, u32[]{:S(2)}, u32[]{:S(2)}) async-start(bf16[16,64,896]{2,1,0:T(8,128)(2,1)} %place_blocks.1), calls=%async_computation.2 | async-start | bytes 3670016 | tf_op jit(solution)/shard_map/all_to_all | solution.py:341
  132.3 0.0 copy-done.11
  132.3 0.3 reduce-window.9
  132.6 0.1 slice.27
  132.7 0.1 slice_reduce_fusion
  132.8 0.1 add_bitcast_fusion
  132.9 0.4 convert_reduce_fusion
  133.3 1.9 collective-permute-start.3
  135.2 2.6 %collective-permute-start.4 = (bf16[4,256,512]{2,1,0:T(8,128)(2,1)}, bf16[4,256,512]{2,1,0:T(8,128)(2,1)}, u32[]{:S(2)}, u32[]{:S(2)}) collective-permute-start(bf16[4,256,512]{2,1,0:T(8,128)(2,1)} %collective-permute-done.1.refs_2_), channel_id=1, source_target_pairs={{0,16},{1,17},{2,18},{3,19},{4,20},{5,21},{6,22},{7,23},{8,24},{9,... | collective-permute-start | bytes 3145736 | tf_op jit(solution)/shard_map/ppermute | solution.py:260
  137.8 0.2 compare_select_fusion
  138.0 0.8 pad_maximum_fusion.1.mask_ref
  138.8 2.2 %pad_maximum_fusion = bf16[16,64,512]{2,1,0:T(8,128)(2,1)} fusion(bf16[16,64,128]{2,1,0:T(8,128)(2,1)} %copy-done.7, bf16[16,64,256]{2,1,0:T(8,128)(2,1)S(1)} %copy-done.2, bf16[16,64,128]{2,1,0:T(8,128)(2,1)} %copy-done.6), kind=kLoop, calls=%fused_computation.12 | loop fusion | flops 3145728 | bytes 2097152 | tf_op jit(solution)/shard_map/concatenate | solution.py:344
  141.0 0.0 collective-permute-done.3.refs_4_
  141.0 0.0 collective-permute-done.4.refs_5_
  141.0 1.0 copy-done.4
  142.0 6.8 %assemble.1 = (bf16[16,64,1024]{2,1,0:T(8,128)(2,1)}, bf16[16,64,1024]{2,1,0:T(8,128)(2,1)}, bf16[16,64,1024]{2,1,0:T(8,128)(2,1)}, bf16[16,64,1024]{2,1,0:T(8,128)(2,1)}) custom-call(s32[1]{0:T(128)} %bitcast.core_ref, bf16[8,256,512]{2,1,0:T(8,128)(2,1)} %bitcast.38, bf16[4,256,512]{2,1,0:T(8,128)(2,1)} %collective-permute-done.refs_1_, ...), custom_call_target="tpu_custom_call" | custom-call | tf_op jit(solution)/shard_map/assemble/pallas_call | solution.py:245
  148.8 0.0 copy-start.5
  148.8 0.0 copy-start.14
  148.9 3.2 %fusion.2.qt_ref = bf16[1024,256]{1,0:T(8,128)(2,1)} fusion(bf16[1024,1024]{1,0:T(8,128)(2,1)} %bitcast.53, bf16[1024,256]{1,0:T(8,128)(2,1)S(1)} %bitcast.40), kind=kOutput, calls=%fused_computation.10 | convolution fusion | flops 537919488 | bytes 3145728 | tf_op jit(solution)/shard_map/dot_general | solution.py:354
  152.1 2.2 %convolution_convert_fusion.2.vt_ref = bf16[1024,512]{1,0:T(8,128)(2,1)} fusion(bf16[1024,1024]{1,0:T(8,128)(2,1)S(1)} %bitcast.52, bf16[1024,512]{1,0:T(8,128)(2,1)S(1)} %bitcast.43), kind=kOutput, calls=%fused_computation.4 | convolution fusion | flops 1074266112 | bytes 4194304 | tf_op jit(solution)/shard_map/dot_general | solution.py:357
  154.4 2.3 %convolution_convert_fusion.3.k_ref = bf16[512,1024]{1,0:T(8,128)(2,1)} fusion(bf16[1024,512]{1,0:T(8,128)(2,1)S(1)} %bitcast.44, bf16[1024,1024]{1,0:T(8,128)(2,1)S(1)} %bitcast.49), kind=kOutput, calls=%fused_computation.5 | convolution fusion | flops 1074266112 | bytes 4194304 | tf_op jit(solution)/shard_map/dot_general | solution.py:356
  156.7 9.5 %near_attention.1 = (f32[1024,256]{1,0:T(8,128)}, f32[8,2,8,256]{3,2,1,0:T(8,128)}, f32[8,2,8,256]{3,2,1,0:T(8,128)}) custom-call(bf16[1024,256]{1,0:T(8,128)(2,1)} %fusion.2.qt_ref, bf16[512,1024]{1,0:T(8,128)(2,1)} %convolution_convert_fusion.3.k_ref, bf16[1024,512]{1,0:T(8,128)(2,1)} %convolution_convert_fusion.2.vt_ref, ...), custom_call_target="tpu_custom_call" | custom-call | tf_op jit(solution)/shard_map/near_attention/pallas_call | solution.py:162
  166.1 11.5 %all-to-all-done.2 = bf16[16,64,896]{2,1,0:T(8,128)(2,1)S(1)} async-done(((bf16[16,64,896]{2,1,0:T(8,128)(2,1)}), bf16[16,64,896]{2,1,0:T(8,128)(2,1)S(1)}, u32[]{:S(2)}, u32[]{:S(2)}) %all-to-all-start.2) | async-done | bytes 1835040 | tf_op jit(solution)/shard_map/all_to_all | solution.py:341
  177.6 5.3 %convolution_convert_fusion.vt_ref = bf16[1024,896]{1,0:T(8,128)(2,1)} fusion(bf16[1024,1024]{1,0:T(8,128)(2,1)} %bitcast.51, bf16[1024,896]{1,0:T(8,128)(2,1)S(1)} %bitcast.41), kind=kOutput, calls=%fused_computation.1 | convolution fusion | flops 1879965696 | bytes 5767168 | tf_op jit(solution)/shard_map/dot_general | solution.py:360
  182.9 3.4 %convolution_convert_fusion.1.k_ref = bf16[896,1024]{1,0:T(8,128)(2,1)} fusion(bf16[1024,896]{1,0:T(8,128)(2,1)S(1)} %bitcast.42, bf16[1024,1024]{1,0:T(8,128)(2,1)S(1)} %bitcast.50), kind=kOutput, calls=%fused_computation.2 | convolution fusion | flops 1879965696 | bytes 5767168 | tf_op jit(solution)/shard_map/dot_general | solution.py:359
  186.2 10.3 %far_attention.1 = bf16[1024,256]{1,0:T(8,128)(2,1)} custom-call(bf16[1024,256]{1,0:T(8,128)(2,1)} %fusion.2.qt_ref, bf16[896,1024]{1,0:T(8,128)(2,1)} %convolution_convert_fusion.1.k_ref, bf16[1024,896]{1,0:T(8,128)(2,1)} %convolution_convert_fusion.vt_ref, f32[1024,256]{1,0:T(8,128)} %get-tuple-element.25.acc_ref, ...), custom_call_target="tpu_custom_call" | custom-call | tf_op jit(solution)/shard_map/far_attention/pallas_call | solution.py:175
  196.5 2.6 %fusion.3 = bf16[256,1024]{1,0:T(8,128)(2,1)} fusion(bf16[1024,256]{1,0:T(8,128)(2,1)} %far_attention.1, bf16[1024,1024]{1,0:T(8,128)(2,1)S(1)} %bitcast.39, f32[1024]{0:T(1024)S(1)} %copy-done.8), kind=kOutput, calls=%fused_computation.11 | convolution fusion | flops 537395200 | bytes 3149824 | tf_op jit(solution)/shard_map/dot_general | solution.py:362
  (38 shorter events, 0.2 us)
Async XLA Ops:
  6.5 19.9 %copy-start.9 = (s32[1024,3]{0,1:T(4,128)S(1)}, s32[1024,3]{0,1:T(4,128)}, u32[]{:S(2)}) copy-start(s32[1024,3]{0,1:T(4,128)} %param.16) | copy-start | bytes 36868
  6.5 20.5 %copy-start.10 = (s32[1024,3]{0,1:T(4,128)S(1)}, s32[1024,3]{0,1:T(4,128)}, u32[]{:S(2)}) copy-start(s32[1024,3]{0,1:T(4,128)} %param.17) | copy-start | bytes 36868
  9.0 9.7 %copy-start.16 = (bf16[16,64,128]{2,1,0:T(8,128)(2,1)S(1)}, bf16[16,64,128]{2,1,0:T(8,128)(2,1)}, u32[]{:S(2)}) copy-start(bf16[16,64,128]{2,1,0:T(8,128)(2,1)} %get-tuple-element.20) | copy-start | bytes 786436
  9.0 13.6 %copy-start.15 = (bf16[16,64,128]{2,1,0:T(8,128)(2,1)S(1)}, bf16[16,64,128]{2,1,0:T(8,128)(2,1)}, u32[]{:S(2)}) copy-start(bf16[16,64,128]{2,1,0:T(8,128)(2,1)} %get-tuple-element.21) | copy-start | bytes 786436
  9.0 29.5 %all-to-all-start = ((bf16[16,64,256]{2,1,0:T(8,128)(2,1)}), bf16[16,64,256]{2,1,0:T(8,128)(2,1)S(1)}, u32[]{:S(2)}, u32[]{:S(2)}) async-start(bf16[16,64,256]{2,1,0:T(8,128)(2,1)} %get-tuple-element.18), calls=%async_computation | async-start | bytes 1048576 | tf_op jit(solution)/shard_map/all_to_all | solution.py:310
  17.0 50.9 %all-gather.3.cloned.1.call-start = ((), (), s32[]{:S(2)}) async-start(), calls=%async_computation.3 | async-start | bytes 2359296 | tf_op jit(solution)/shard_map/all_gather | solution.py:314
  18.8 19.0 %collective-permute-start.5 = (bf16[16,64,128]{2,1,0:T(8,128)(2,1)S(1)}, bf16[16,64,128]{2,1,0:T(8,128)(2,1)S(1)}, u32[]{:S(2)}, u32[]{:S(2)}) collective-permute-start(bf16[16,64,128]{2,1,0:T(8,128)(2,1)S(1)} %copy-done.16), channel_id=1, source_target_pairs={{0,1},{1,2},{2,3},{3,4},{4,5},{5,6},{6,7},{7,8},{8,9},{9,10},{10,1... | collective-permute-start | bytes 786440 | tf_op jit(solution)/shard_map/ppermute | solution.py:319
  22.6 15.9 %collective-permute-start.6 = (bf16[16,64,128]{2,1,0:T(8,128)(2,1)S(1)}, bf16[16,64,128]{2,1,0:T(8,128)(2,1)S(1)}, u32[]{:S(2)}, u32[]{:S(2)}) collective-permute-start(bf16[16,64,128]{2,1,0:T(8,128)(2,1)S(1)} %copy-done.15), channel_id=1, source_target_pairs={{1,0},{2,1},{3,2},{4,3},{5,4},{6,5},{7,6},{8,7},{9,8},{10,9},{11,1... | collective-permute-start | bytes 786440 | tf_op jit(solution)/shard_map/ppermute | solution.py:320
  37.8 5.8 %copy-start.6 = (bf16[16,64,128]{2,1,0:T(8,128)(2,1)}, bf16[16,64,128]{2,1,0:T(8,128)(2,1)S(1)}, u32[]{:S(2)}) copy-start(bf16[16,64,128]{2,1,0:T(8,128)(2,1)S(1)} %collective-permute-done.5) | copy-start | bytes 786436
  38.6 5.0 %copy-start.7 = (bf16[16,64,128]{2,1,0:T(8,128)(2,1)}, bf16[16,64,128]{2,1,0:T(8,128)(2,1)S(1)}, u32[]{:S(2)}) copy-start(bf16[16,64,128]{2,1,0:T(8,128)(2,1)S(1)} %collective-permute-done.6) | copy-start | bytes 786436
  38.6 0.8 copy-start.3
  43.6 74.5 %all-to-all-start.1 = ((bf16[32,320,128]{2,1,0:T(8,128)(2,1)}), bf16[32,320,128]{2,1,0:T(8,128)(2,1)S(1)}, u32[]{:S(2)}, u32[]{:S(2)}) async-start(bf16[32,320,128]{2,1,0:T(8,128)(2,1)} %bitcast.36), calls=%async_computation.1 | async-start | bytes 5242880 | tf_op jit(solution)/shard_map/all_to_all | solution.py:330
  67.9 50.0 %collective-permute-start.2 = (bf16[8,256,512]{2,1,0:T(8,128)(2,1)}, bf16[8,256,512]{2,1,0:T(8,128)(2,1)}, u32[]{:S(2)}, u32[]{:S(2)}) collective-permute-start(bf16[8,256,512]{2,1,0:T(8,128)(2,1)} %bitcast.37), channel_id=1, source_target_pairs={{0,16},{1,17},{2,18},{3,19},{4,20},{5,21},{6,22},{7,23},{8,24},{9,... | collective-permute-start | bytes 6291464 | tf_op jit(solution)/shard_map/ppermute | solution.py:260
  72.9 44.7 %collective-permute-start = (bf16[4,256,512]{2,1,0:T(8,128)(2,1)}, bf16[4,256,512]{2,1,0:T(8,128)(2,1)}, u32[]{:S(2)}, u32[]{:S(2)}) collective-permute-start(bf16[4,256,512]{2,1,0:T(8,128)(2,1)} %bitcast.4), channel_id=1, source_target_pairs={{0,1},{1,0},{2,3},{3,2},{4,5},{5,4},{6,7},{7,6},{8,9},{9,8},{10,11... | collective-permute-start | bytes 3145736 | tf_op jit(solution)/shard_map/ppermute | solution.py:260
  76.0 41.9 %collective-permute-start.1 = (bf16[4,256,512]{2,1,0:T(8,128)(2,1)}, bf16[4,256,512]{2,1,0:T(8,128)(2,1)}, u32[]{:S(2)}, u32[]{:S(2)}) collective-permute-start(bf16[4,256,512]{2,1,0:T(8,128)(2,1)} %bitcast.5), channel_id=1, source_target_pairs={{0,33},{1,32},{2,35},{3,34},{4,37},{5,36},{6,39},{7,38},{8,41},{9,... | collective-permute-start | bytes 3145736 | tf_op jit(solution)/shard_map/ppermute | solution.py:260
  118.1 1.5 copy-start
  123.1 9.2 %copy-start.11 = (s32[1024]{0:T(1024)S(1)}, s32[1024]{0:T(1024)}, u32[]{:S(2)}) copy-start(s32[1024]{0:T(1024)} %param.15) | copy-start | bytes 12292
  123.1 15.7 %copy-start.2 = (bf16[16,64,256]{2,1,0:T(8,128)(2,1)S(1)}, bf16[16,64,256]{2,1,0:T(8,128)(2,1)}, u32[]{:S(2)}) copy-start(bf16[16,64,256]{2,1,0:T(8,128)(2,1)} %get-tuple-element.18) | copy-start | bytes 1572868
  123.1 54.5 %all-to-all-start.2 = ((bf16[16,64,896]{2,1,0:T(8,128)(2,1)}), bf16[16,64,896]{2,1,0:T(8,128)(2,1)S(1)}, u32[]{:S(2)}, u32[]{:S(2)}) async-start(bf16[16,64,896]{2,1,0:T(8,128)(2,1)} %place_blocks.1), calls=%async_computation.2 | async-start | bytes 3670016 | tf_op jit(solution)/shard_map/all_to_all | solution.py:341
  133.3 7.7 %collective-permute-start.3 = (bf16[4,256,512]{2,1,0:T(8,128)(2,1)}, bf16[4,256,512]{2,1,0:T(8,128)(2,1)S(1)}, u32[]{:S(2)}, u32[]{:S(2)}) collective-permute-start(bf16[4,256,512]{2,1,0:T(8,128)(2,1)} %collective-permute-done.refs_1_), channel_id=1, source_target_pairs={{0,16},{1,17},{2,18},{3,19},{4,20},{5,21},{6,22},{7,23},{8,24},{9,... | collective-permute-start | bytes 3145736 | tf_op jit(solution)/shard_map/ppermute | solution.py:260
  135.2 5.8 %collective-permute-start.4 = (bf16[4,256,512]{2,1,0:T(8,128)(2,1)}, bf16[4,256,512]{2,1,0:T(8,128)(2,1)}, u32[]{:S(2)}, u32[]{:S(2)}) collective-permute-start(bf16[4,256,512]{2,1,0:T(8,128)(2,1)} %collective-permute-done.1.refs_2_), channel_id=1, source_target_pairs={{0,16},{1,17},{2,18},{3,19},{4,20},{5,21},{6,22},{7,23},{8,24},{9,... | collective-permute-start | bytes 3145736 | tf_op jit(solution)/shard_map/ppermute | solution.py:260
  141.0 1.0 copy-start.4
  148.8 3.3 %copy-start.5 = (bf16[16,64,512]{2,1,0:T(8,128)(2,1)S(1)}, bf16[16,64,512]{2,1,0:T(8,128)(2,1)}, u32[]{:S(2)}) copy-start(bf16[16,64,512]{2,1,0:T(8,128)(2,1)} %pad_maximum_fusion) | copy-start | bytes 3145732
  148.8 3.3 %copy-start.14 = (bf16[16,64,1024]{2,1,0:T(8,128)(2,1)S(1)}, bf16[16,64,1024]{2,1,0:T(8,128)(2,1)}, u32[]{:S(2)}) copy-start(bf16[16,64,1024]{2,1,0:T(8,128)(2,1)} %get-tuple-element.24) | copy-start | bytes 6291460
  152.1 2.3 %copy-start.12 = (bf16[16,64,1024]{2,1,0:T(8,128)(2,1)S(1)}, bf16[16,64,1024]{2,1,0:T(8,128)(2,1)}, u32[]{:S(2)}) copy-start(bf16[16,64,1024]{2,1,0:T(8,128)(2,1)} %get-tuple-element.23) | copy-start | bytes 6291460
  177.6 5.3 %copy-start.13 = (bf16[16,64,1024]{2,1,0:T(8,128)(2,1)S(1)}, bf16[16,64,1024]{2,1,0:T(8,128)(2,1)}, u32[]{:S(2)}) copy-start(bf16[16,64,1024]{2,1,0:T(8,128)(2,1)} %get-tuple-element.23) | copy-start | bytes 6291460
  186.2 10.3 %copy-start.1 = (bf16[16,64,1024]{2,1,0:T(8,128)(2,1)S(1)}, bf16[16,64,1024]{2,1,0:T(8,128)(2,1)}, u32[]{:S(2)}) copy-start(bf16[16,64,1024]{2,1,0:T(8,128)(2,1)} %get-tuple-element.28) | copy-start | bytes 6291460
  186.2 10.3 %copy-start.8 = (f32[1024]{0:T(1024)S(1)}, f32[1024]{0:T(1024)}, u32[]{:S(2)}) copy-start(f32[1024]{0:T(1024)} %param.14) | copy-start | bytes 12292
Sparse Core Ops, SparseCore 0:
  19.9 47.9 all-gather.2
